TPU v7x, 512 devices: a whole 4x8x8 slice. The times are simulated.
512 devices in a mesh: wide: 32 (over x, y), narrow: 16 (over z, core).
Axes of the slice: x: 4, y: 8, z: 8, core: 2. Of those that a mesh axis runs over, the one named last changes fastest.
Arguments:
- inverse: float32 [16384, 16384], P('wide', 'narrow'), may hold values from -0.2 to 1.3, as said below
- activations: bfloat16 [4096, 16384], P('narrow', 'wide'), may hold values from -4 to 4
- forget: int32 [512], replicated, may hold values from 0 to 4095, as said below
Outputs:
- downdated: float32 [16384, 16384], P('wide', 'narrow')
Inputs may be any that keep to these rules, and one draw needn't show every extreme that they name: `inverse`: symmetric positive definite; the factor stays positive definite after every downdate. `forget`: distinct row numbers; rows are stored in order of arrival, and the newest one, 4095, whose request starts the downdate, is always among them.
All inputs are finite; a program needn't handle non-finite values.
Results may differ from a plain program's by a relative error of at most 0.0003.
Values may be sent and summed in bfloat16 or wider, within the bound.
No kernel may reach another device: no remote copies, remote signals or barrier semaphores. Data moves between devices by JAX's collectives and lax.ppermute only.
A program may use at most 64 MiB of HBM per device.

v0:
```python
import math

import jax
import jax.numpy as jnp
from jax import lax
from jax.sharding import PartitionSpec as P

M = 16384
GROUP = 256
GROUPS = 2
ROWS = 512


def broadcast(value, axis, root):
    mine = lax.axis_index(axis) == root
    return lax.psum(jnp.where(mine, value, jnp.zeros_like(value)), axis)


def downdate(current, block, beta):
    row_index = lax.axis_index("wide")
    stride = lax.axis_size("wide") // lax.axis_size("narrow")
    row_width = current.shape[0]
    partial_value = jnp.dot(
        block, current, precision=lax.Precision.HIGHEST, preferred_element_type=jnp.float32
    )
    images = lax.psum(partial_value, "wide")
    portion = lax.dynamic_slice_in_dim(images, row_index % stride * row_width, row_width, 1)
    own_images = broadcast(portion, "narrow", row_index // stride)
    local_cap = jnp.dot(
        block, own_images.T, precision=lax.Precision.HIGHEST, preferred_element_type=jnp.float32
    )
    capacity = lax.psum(local_cap, "wide")
    system = jnp.eye(block.shape[0], dtype=jnp.float32) / beta - capacity
    factor = jnp.linalg.cholesky(system)
    solved = jax.scipy.linalg.cho_solve((factor, True), own_images)
    return current + jnp.dot(
        solved.T, images, precision=lax.Precision.HIGHEST, preferred_element_type=jnp.float32
    )


def on_device(inverse, activations, forget):
    col_index = lax.axis_index("narrow")
    stored_here = activations.shape[0]
    local_rows = forget - col_index * stored_here
    onehot = (local_rows[:, None] == jnp.arange(stored_here, dtype=jnp.int32)[None, :]).astype(
        jnp.bfloat16
    )
    picked = jnp.dot(onehot, activations, preferred_element_type=jnp.float32).astype(jnp.bfloat16)
    fetched = lax.psum(picked, "narrow").astype(jnp.float32)
    beta = 1.0 / (2.0 * (M + 4.0 * math.sqrt(ROWS * M)))
    current = inverse
    for block_num in range(GROUPS):
        block = fetched[block_num * GROUP : (block_num + 1) * GROUP]
        current = downdate(current, block, beta)
    return current


def solution(mesh):
    placed = (P("wide", "narrow"), P("narrow", "wide"), P())
    return jax.shard_map(
        on_device, mesh=mesh, in_specs=placed, out_specs=P("wide", "narrow"), check_vma=False
    )
```

profile of v0, /device:TPU:1, one launch (start us, length us, event | category | flops | bytes accessed | tf_op | source)
XLA Modules:
  0.0 1158.1 jit_solution(7808553782005469628)
XLA Ops:
  6.5 0.7 broadcast_subtract_fusion
  7.5 1.1 convolution_convert_fusion
  8.7 123.4 %all-reduce.9.cloned.1.call-done = bf16[512,512]{1,0:T(8,128)(2,1)} async-done(((bf16[512,512]{1,0:T(8,128)(2,1)}), bf16[512,512]{1,0:T(8,128)(2,1)}) %all-reduce.9.cloned.1.call-update) | async-done | bytes 524304 | tf_op jit(solution)/shard_map/psum | solution.py:49
  132.1 3.8 fusion.19
  136.1 156.3 %all-reduce.11.cloned.1.call-done = f32[256,1024]{1,0:T(8,128)} async-done(((f32[256,1024]{1,0:T(8,128)}), f32[256,1024]{1,0:T(8,128)}) %all-reduce.11.cloned.1.call-update) | async-done | bytes 1048592 | tf_op jit(solution)/shard_map/psum | solution.py:26
  292.4 1.9 dynamic-slice_select_fusion.1
  294.4 119.6 %all-reduce.13.cloned.1.call-done = f32[256,512]{1,0:T(8,128)} async-done(((f32[256,512]{1,0:T(8,128)}), f32[256,512]{1,0:T(8,128)}) %all-reduce.13.cloned.1.call-update) | async-done | bytes 524304 | tf_op jit(solution)/shard_map/psum | solution.py:16
  413.9 2.1 fusion.17
  416.5 152.8 %all-reduce.15.cloned.1.call-done = f32[256,256]{0,1:T(8,128)} async-done(((f32[256,256]{0,1:T(8,128)}), f32[256,256]{0,1:T(8,128)}) %all-reduce.15.cloned.1.call-update) | async-done | bytes 262160 | tf_op jit(solution)/shard_map/psum | solution.py:32
  569.3 1.0 select_subtract_fusion.1
  570.4 1.0 fusion.11
  571.5 11.7 %cholesky.130 = f32[128,128]{1,0:T(8,128)S(1)} custom-call(f32[128,128]{1,0:T(8,128)S(1)} %cholesky.194), custom_call_target="Cholesky" | custom-call | tf_op jit(solution)/shard_map/jit(cholesky)/cholesky | solution.py:34
  583.2 9.8 custom-call.15
  593.5 11.7 %cholesky.147 = f32[128,128]{1,0:T(8,128)S(1)} custom-call(f32[128,128]{1,0:T(8,128)S(1)} %convolution_subtract_fusion.5), custom_call_target="Cholesky" | custom-call | tf_op jit(solution)/shard_map/jit(cholesky)/cholesky | solution.py:34
  605.3 0.7 compare_reduce_fusion.2
  607.3 4.5 while.4
  607.9 0.6 fusion.64
  608.5 1.4 bitcast_dynamic-update-slice_fusion.4
  609.9 0.6 fusion.64
  610.4 1.4 bitcast_dynamic-update-slice_fusion.4
  611.8 19.7 %custom-call.16 = f32[2,128,128]{1,2,0:T(8,128)S(1)} custom-call(f32[2,128,128]{2,1,0:T(8,128)S(1)} %get-tuple-element.21), custom_call_target="InvertDiagBlocksLowerTriangular" | custom-call | tf_op jit(solution)/shard_map/jit(_cho_solve)/triangular_solve | solution.py:35
  633.1 0.4 convolution_subtract_fusion.2
  633.9 3.5 convolution_add_fusion.1
  637.5 2.2 fusion.15
  639.7 158.3 %all-reduce.17.cloned.1.call-done = f32[256,1024]{1,0:T(8,128)} async-done(((f32[256,1024]{1,0:T(8,128)}), f32[256,1024]{1,0:T(8,128)}) %all-reduce.17.cloned.1.call-update) | async-done | bytes 1048592 | tf_op jit(solution)/shard_map/psum | solution.py:26
  798.0 1.9 dynamic-slice_select_fusion
  800.1 119.3 %all-reduce.19.cloned.1.call-done = f32[256,512]{1,0:T(8,128)} async-done(((f32[256,512]{1,0:T(8,128)}), f32[256,512]{1,0:T(8,128)}) %all-reduce.19.cloned.1.call-update) | async-done | bytes 524304 | tf_op jit(solution)/shard_map/psum | solution.py:16
  919.4 2.1 fusion.13
  921.6 153.3 %all-reduce.21.cloned.1.call-done = f32[256,256]{0,1:T(8,128)} async-done(((f32[256,256]{0,1:T(8,128)}), f32[256,256]{0,1:T(8,128)}) %all-reduce.21.cloned.1.call-update) | async-done | bytes 262160 | tf_op jit(solution)/shard_map/psum | solution.py:32
  1074.9 1.0 select_subtract_fusion
  1076.0 1.0 fusion.10
  1077.0 11.7 %cholesky.164 = f32[128,128]{1,0:T(8,128)S(1)} custom-call(f32[128,128]{1,0:T(8,128)S(1)} %cholesky.197), custom_call_target="Cholesky" | custom-call | tf_op jit(solution)/shard_map/jit(cholesky)/cholesky | solution.py:34
  1088.8 9.8 custom-call.17
  1099.1 11.7 %cholesky.181 = f32[128,128]{1,0:T(8,128)S(1)} custom-call(f32[128,128]{1,0:T(8,128)S(1)} %convolution_subtract_fusion.4), custom_call_target="Cholesky" | custom-call | tf_op jit(solution)/shard_map/jit(cholesky)/cholesky | solution.py:34
  1110.9 0.7 compare_reduce_fusion
  1111.5 0.6 compare_reduce_fusion.1
  1113.4 0.7 select_select_fusion
  1114.2 0.7 broadcast.115
  1114.8 7.2 while.5
  1115.0 0.6 fusion.65
  1115.6 2.9 bitcast_dynamic-update-slice_fusion.5
  1118.6 0.6 fusion.65
  1119.2 2.9 bitcast_dynamic-update-slice_fusion.5
  1122.0 20.6 %custom-call.18 = f32[2,128,128]{1,2,0:T(8,128)S(1)} custom-call(f32[2,128,128]{2,1,0:T(8,128)} %get-tuple-element.22), custom_call_target="InvertDiagBlocksLowerTriangular" | custom-call | tf_op jit(solution)/shard_map/jit(_cho_solve)/triangular_solve | solution.py:35
  1142.6 1.4 fusion.6
  1144.0 1.4 convolution_subtract_fusion.1
  1146.2 1.3 convolution_subtract_fusion
  1147.8 3.2 convolution_add_fusion
  (58 shorter events, 5.7 us)
Async XLA Ops:
  6.5 1.0 copy-start
  6.5 125.6 %all-reduce.9.cloned.1.call-start = ((), (), s32[]{:S(2)}) async-start(), calls=%async_computation | async-start | bytes 1048576 | tf_op jit(solution)/shard_map/psum | solution.py:49
  8.7 283.7 %all-reduce.11.cloned.1.call-start = ((), (), s32[]{:S(2)}) async-start(), calls=%async_computation.1 | async-start | bytes 2097152 | tf_op jit(solution)/shard_map/psum | solution.py:26
  136.0 278.0 %copy-start.4 = (bf16[512,512]{1,0:T(8,128)(2,1)S(1)}, bf16[512,512]{1,0:T(8,128)(2,1)}, u32[]{:S(2)}) copy-start(bf16[512,512]{1,0:T(8,128)(2,1)} %all-reduce.9.cloned.1.call-done) | copy-start | bytes 1572868
  136.0 278.0 %all-reduce.13.cloned.1.call-start = ((), (), s32[]{:S(2)}) async-start(), calls=%async_computation.2 | async-start | bytes 1048576 | tf_op jit(solution)/shard_map/psum | solution.py:16
  294.3 275.0 %all-reduce.15.cloned.1.call-start = ((), (), s32[]{:S(2)}) async-start(), calls=%async_computation.3 | async-start | bytes 524288 | tf_op jit(solution)/shard_map/psum | solution.py:32
  416.1 381.9 %all-reduce.17.cloned.1.call-start = ((), (), s32[]{:S(2)}) async-start(), calls=%async_computation.4 | async-start | bytes 2097152 | tf_op jit(solution)/shard_map/psum | solution.py:26
  570.3 61.2 %copy-start.3 = (f32[256,512]{1,0:T(8,128)S(1)}, f32[256,512]{1,0:T(8,128)}, u32[]{:S(2)}) copy-start(f32[256,512]{1,0:T(8,128)} %all-reduce.13.cloned.1.call-done) | copy-start | bytes 1572868
  611.8 22.1 %copy-start.1 = (f32[256,1024]{1,0:T(8,128)S(1)}, f32[256,1024]{1,0:T(8,128)}, u32[]{:S(2)}) copy-start(f32[256,1024]{1,0:T(8,128)} %all-reduce.11.cloned.1.call-done) | copy-start | bytes 3145732
  633.9 3.5 copy-start.5
  639.7 279.8 %copy-start.6 = (bf16[512,512]{1,0:T(8,128)(2,1)S(1)}, bf16[512,512]{1,0:T(8,128)(2,1)}, u32[]{:S(2)}) copy-start(bf16[512,512]{1,0:T(8,128)(2,1)} %all-reduce.9.cloned.1.call-done) | copy-start | bytes 1572868
  639.7 279.7 %all-reduce.19.cloned.1.call-start = ((), (), s32[]{:S(2)}) async-start(), calls=%async_computation.5 | async-start | bytes 1048576 | tf_op jit(solution)/shard_map/psum | solution.py:16
  799.9 275.0 %all-reduce.21.cloned.1.call-start = ((), (), s32[]{:S(2)}) async-start(), calls=%async_computation.6 | async-start | bytes 524288 | tf_op jit(solution)/shard_map/psum | solution.py:32
  1122.0 25.8 %copy-start.2 = (f32[256,1024]{1,0:T(8,128)S(1)}, f32[256,1024]{1,0:T(8,128)}, u32[]{:S(2)}) copy-start(f32[256,1024]{1,0:T(8,128)} %all-reduce.17.cloned.1.call-done) | copy-start | bytes 3145732
Sparse Core Ops, SparseCore 0:
  9.7 122.4 all-reduce.8
  136.1 156.2 all-reduce.10
  294.7 119.1 all-reduce.12
  417.2 152.0 all-reduce.14
  639.8 158.1 all-reduce.16
  800.2 119.1 all-reduce.18
  922.9 152.0 all-reduce.20
where the time goes:
time: 1160 us
  waiting for transfers between devices  983 us (85%)
  other arithmetic  118 us (10%)
  matrix products  26.6 us (2%)
  between operations  16.6 us (1%)
  local copies, waits for them, and re-layouts  12.2 us (1%)
    psum x2, waiting for transfers between devices, downdate(): images = lax.psum(partial_value, 'wide')  315 us
    psum x2, waiting for transfers between devices, downdate(): capacity = lax.psum(local_cap, 'wide')  306 us
    psum x2, waiting for transfers between devices, broadcast(): return lax.psum(jnp.where(mine, value, jnp.zeros_like(value)), axis)  239 us
    psum x1, waiting for transfers between devices, on_device(): fetched = lax.psum(picked, 'narrow').astype(jnp.float32)  123 us
    another operation x13, other arithmetic, downdate(): factor = jnp.linalg.cholesky(system)  68.6 us
    another operation x5, other arithmetic, downdate(): solved = jax.scipy.linalg.cho_solve((factor, True), own_images)  41 us
  transfers between devices with their start and end apart: 7, of which 7 were waited for; matrix products, arithmetic and copies ran while one was open for 0% of the time, Pallas kernels for 0%

commit v1 on v0

v1 whole, which is shorter than its diff:
```python
import math

import jax
import jax.numpy as jnp
import numpy as np
from jax import lax
from jax.sharding import Mesh
from jax.sharding import PartitionSpec as P

M = 16384
ROWS = 512
BETA = 1.0 / (2.0 * (M + 4.0 * math.sqrt(ROWS * M)))
AXES = ("x", "y", "z", "core")
NX, NY, NZ, NC = 4, 8, 8, 2
F32 = jnp.float32
BF16 = jnp.bfloat16
SMALL = 2.0**-14
MAX_FACTORS = 48


def spread(x, axis, parts):
    x = x.reshape((parts, x.shape[0] // parts) + x.shape[1:])
    return lax.all_to_all(x, axis, 0, 0, tiled=True)


def scatter_sum(x, axis, parts):
    return jnp.sum(spread(x, axis, parts).astype(F32), axis=0)


def gather(x, axis, parts):
    got = lax.all_to_all(jnp.broadcast_to(x[None], (parts,) + x.shape), axis, 0, 0, tiled=True)
    return got.reshape((parts * x.shape[0],) + x.shape[1:])


def swap(x):
    return lax.ppermute(x, "core", [(0, 1), (1, 0)])


def fold_cores(x):
    core = lax.axis_index("core")
    half = x.shape[0] // 2
    there = lax.dynamic_slice_in_dim(x, (1 - core) * half, half, 0)
    here = lax.dynamic_slice_in_dim(x, core * half, half, 0)
    return here + swap(there)


def join_cores(x):
    other = swap(x)
    first = lax.axis_index("core") == 0
    return jnp.concatenate([jnp.where(first, x, other), jnp.where(first, other, x)], axis=0)


def exact_pair(x):
    high = lax.reduce_precision(x, 8, 7)
    return high.astype(BF16), (x - high).astype(BF16)


def column_owner():
    pairs = []
    for x in range(NX):
        for y in range(NY):
            for z in range(NZ):
                for core in range(NC):
                    here = ((x * NY + y) * NZ + z) * NC + core
                    to_x, to_y = 2 * (y % 2) + core, z
                    to_z, to_core = 2 * x + y // 4, (y // 2) % 2
                    pairs.append((here, ((to_x * NY + to_y) * NZ + to_z) * NC + to_core))
    return pairs


def solve_rows(start, square):
    def dot(a, b):
        return jnp.dot(a, b, precision=lax.Precision.HIGHEST, preferred_element_type=F32)

    def more(state):
        _, power, last, count = state
        return jnp.logical_and(last > SMALL, count < MAX_FACTORS)

    def step(state):
        total, power, _, count = state
        power = dot(power, power)
        return total + dot(total, power), power, jnp.max(jnp.sum(jnp.abs(power), axis=0)), count + 1

    state = (start + dot(start, square), square, jnp.float32(1.0), jnp.int32(0))
    return lax.while_loop(more, step, state)[0]


def on_device(inverse, activations, forget):
    x, y = lax.axis_index("x"), lax.axis_index("y")
    z, core = lax.axis_index("z"), lax.axis_index("core")
    wide, narrow = x * NY + y, z * NC + core
    height, width = inverse.shape
    stored_here = activations.shape[0]
    to_columns = column_owner()
    to_rows = [(b, a) for a, b in to_columns]

    local = forget - narrow * stored_here
    onehot = (jnp.arange(stored_here, dtype=jnp.int32)[:, None] == local[None, :]).astype(BF16)
    picked = lax.dot_general(
        activations, onehot, (((0,), (0,)), ((), ())), preferred_element_type=F32
    ).astype(BF16)
    piece = scatter_sum(fold_cores(picked), "z", NZ).astype(BF16)
    piece_by_columns = lax.ppermute(piece, AXES, to_columns)
    rows_here = join_cores(gather(piece, "z", NZ))

    row_number = wide * height + lax.broadcasted_iota(jnp.int32, inverse.shape, 0)
    col_number = narrow * width + lax.broadcasted_iota(jnp.int32, inverse.shape, 1)
    less_one = inverse - jnp.where(row_number == col_number, 1.0, 0.0).astype(F32)
    part = sum(
        lax.dot_general(term, rows_here, (((0,), (0,)), ((), ())), preferred_element_type=F32)
        for term in exact_pair(less_one)
    )
    summed = scatter_sum(part.astype(BF16), "x", NX)
    change = scatter_sum(summed.astype(BF16), "y", NY)
    images_piece = change + piece_by_columns.astype(F32)

    share = lax.dot_general(
        piece_by_columns.astype(F32),
        images_piece * BETA,
        (((0,), (0,)), ((), ())),
        precision=lax.Precision.HIGHEST,
        preferred_element_type=F32,
    )
    share = scatter_sum(fold_cores(share).astype(BF16), "z", NZ)
    share = scatter_sum(share, "y", NY)
    share = jnp.sum(gather(share[None], "x", NX), axis=0)
    scaled = join_cores(gather(gather(share, "y", NY), "z", NZ))

    change_here = join_cores(gather(lax.ppermute(change.astype(BF16), AXES, to_rows), "z", NZ))
    images_rows = rows_here.astype(F32) + change_here.astype(F32)
    images_cols = gather(gather(images_piece.astype(BF16), "y", NY), "x", NX)

    solved = solve_rows(images_rows * BETA, scaled)
    update = sum(
        lax.dot_general(term, images_cols, (((1,), (1,)), ((), ())), preferred_element_type=F32)
        for term in exact_pair(solved)
    )
    return inverse + update


def solution(mesh):
    devices = np.asarray(mesh.devices).reshape(NX, NY, NZ, NC)
    placed = (P(("x", "y"), ("z", "core")), P(("z", "core"), ("x", "y")), P())
    return jax.shard_map(
        on_device,
        mesh=Mesh(devices, AXES),
        in_specs=placed,
        out_specs=P(("x", "y"), ("z", "core")),
        check_vma=False,
    )
```

time: 1160 us -> 236 us (0.20)
  the two profiles are of different devices: /device:TPU:1 before, /device:TPU:2 now
where the time goes in v1:
time: 236 us; the launch traced here: 235 us
  blocking collectives  114 us (48%)
  starting transfers between devices  46.8 us (20%)
  waiting for transfers between devices  35.8 us (15%)
  matrix products  23.3 us (10%)
  local copies, waits for them, and re-layouts  7.31 us (3%)
  other arithmetic  4.94 us (2%)
  loops' own time  2.66 us (1%)
    all_to_all x4, blocking collectives, spread(): return lax.all_to_all(x, axis, 0, 0, tiled=True)  74.9 us
    all_to_all x3, blocking collectives, gather(): lax.all_to_all(jnp.broadcast_to(x[None], (parts,) + x.shape), axis, 0, 0,...  39.3 us
    all_to_all x4, starting transfers between devices, gather(): lax.all_to_all(jnp.broadcast_to(x[None], (parts,) + x.shape), axis, 0, 0,...  24.5 us
    dot_general x9, matrix products, dot(): jnp.dot(a, b, precision=lax.Precision.HIGHEST, preferred_element_type=F32)  17.8 us
    all_to_all x4, waiting for transfers between devices, gather(): lax.all_to_all(jnp.broadcast_to(x[None], (parts,) + x.shape), axis, 0, 0,...  16.7 us
    ppermute x5, starting transfers between devices, swap(): return lax.ppermute(x, 'core', [(0, 1), (1, 0)])  10.2 us
    all_to_all x1, waiting for transfers between devices, spread(): return lax.all_to_all(x, axis, 0, 0, tiled=True)  8.04 us
    all_to_all x1, starting transfers between devices, spread(): return lax.all_to_all(x, axis, 0, 0, tiled=True)  7.11 us
  transfers between devices with their start and end apart: 12, of which 8 were waited for; matrix products, arithmetic and copies ran while one was open for 10% of the time, Pallas kernels for 0%

profile of v1, /device:TPU:2, one launch (start us, length us, event | category | flops | bytes accessed | tf_op | source)
XLA Modules:
  0.0 235.3 jit_solution(17646031275692544589)
XLA Ops:
  0.0 0.7 broadcast_subtract_fusion
  1.4 2.1 collective-permute-start
  3.4 1.5 collective-permute-done
  5.0 22.3 %all_to_all.60 = bf16[8,32,512]{2,1,0:T(8,128)(2,1)S(1)} all-to-all(bf16[8,32,512]{2,1,0:T(8,128)(2,1)S(1)} %bitcast.49), channel_id=1, replica_groups=mesh['x'=4,'y'=8,'z'=8,'core'=2] {'z'}, dimensions={0} | all-to-all | bytes 524288 | tf_op jit(solution)/shard_map/all_to_all | solution.py:23
  27.4 13.5 %all_to_all.61 = bf16[8,32,512]{2,1,0:T(8,128)(2,1)S(1)} all-to-all(bf16[8,32,512]{2,1,0:T(8,128)(2,1)S(1)} %broadcast_in_dim.26), channel_id=1, replica_groups=mesh['x'=4,'y'=8,'z'=8,'core'=2] {'z'}, dimensions={0} | all-to-all | bytes 524288 | tf_op jit(solution)/shard_map/all_to_all | solution.py:31
  40.9 1.9 collective-permute-start.1
  42.9 1.5 collective-permute-done.1
  44.4 0.8 fusion.3
  45.3 0.8 add_convert_fusion
  46.1 18.6 %all_to_all.62 = bf16[4,256,512]{2,1,0:T(8,128)(2,1)S(1)} all-to-all(bf16[4,256,512]{2,1,0:T(8,128)(2,1)S(1)} %bitcast.46), channel_id=1, replica_groups=mesh['x'=4,'y'=8,'z'=8,'core'=2] {'x'}, dimensions={0} | all-to-all | bytes 2097152 | tf_op jit(solution)/shard_map/all_to_all | solution.py:23
  64.7 0.9 reduce_sum.70
  65.6 7.1 %all-to-all-start.3 = ((bf16[8,32,512]{2,1,0:T(8,128)(2,1)}), bf16[8,32,512]{2,1,0:T(8,128)(2,1)S(1)}, u32[]{:S(2)}, u32[]{:S(2)}) async-start(bf16[8,32,512]{2,1,0:T(8,128)(2,1)} %bitcast.6), calls=%async_computation.3 | async-start | bytes 524288 | tf_op jit(solution)/shard_map/all_to_all | solution.py:23
  72.7 3.1 %collective-permute-start.4 = (bf16[32,512]{1,0:T(8,128)(2,1)S(1)}, bf16[32,512]{1,0:T(8,128)(2,1)S(1)}, u32[]{:S(2)}, u32[]{:S(2)}) collective-permute-start(bf16[32,512]{1,0:T(8,128)(2,1)S(1)} %reduce_sum.69), channel_id=1, source_target_pairs={{0,0},{1,128},{2,16},{3,144},{4,32},{5,160},{6,48},{7,176},{8,64},... | collective-permute-start | bytes 98312 | tf_op jit(solution)/shard_map/ppermute | solution.py:103
  75.7 8.0 %all-to-all-done.3 = bf16[8,32,512]{2,1,0:T(8,128)(2,1)S(1)} async-done(((bf16[8,32,512]{2,1,0:T(8,128)(2,1)}), bf16[8,32,512]{2,1,0:T(8,128)(2,1)S(1)}, u32[]{:S(2)}, u32[]{:S(2)}) %all-to-all-start.3) | async-done | bytes 262176 | tf_op jit(solution)/shard_map/all_to_all | solution.py:23
  84.5 1.9 collective-permute-start.5
  86.4 1.9 collective-permute-done.5
  88.4 16.9 %all_to_all.63 = bf16[8,32,512]{2,1,0:T(8,128)(2,1)S(1)} all-to-all(bf16[8,32,512]{2,1,0:T(8,128)(2,1)S(1)} %bitcast.45), channel_id=1, replica_groups=mesh['x'=4,'y'=8,'z'=8,'core'=2] {'z'}, dimensions={0} | all-to-all | bytes 524288 | tf_op jit(solution)/shard_map/all_to_all | solution.py:23
  105.4 17.1 %all_to_all.64 = f32[8,4,512]{2,1,0:T(4,128)S(1)} all-to-all(f32[8,4,512]{2,1,0:T(4,128)S(1)} %reshape.44), channel_id=1, replica_groups=mesh['x'=4,'y'=8,'z'=8,'core'=2] {'y'}, dimensions={0} | all-to-all | bytes 131072 | tf_op jit(solution)/shard_map/all_to_all | solution.py:23
  122.6 9.2 %all_to_all.65 = f32[4,1,4,512]{3,2,1,0:T(4,128)S(1)} all-to-all(f32[4,1,4,512]{3,2,1,0:T(4,128)S(1)} %broadcast_in_dim.30), channel_id=1, replica_groups=mesh['x'=4,'y'=8,'z'=8,'core'=2] {'x'}, dimensions={0} | all-to-all | bytes 65536 | tf_op jit(solution)/shard_map/all_to_all | solution.py:31
  132.5 3.4 %all-to-all-start.8 = ((f32[8,4,512]{2,1,0:T(4,128)}), f32[8,4,512]{2,1,0:T(4,128)S(1)}, u32[]{:S(2)}, u32[]{:S(2)}) async-start(f32[8,4,512]{2,1,0:T(4,128)} %broadcast_in_dim.58), calls=%async_computation.8 | async-start | bytes 131072 | tf_op jit(solution)/shard_map/all_to_all | solution.py:31
  135.8 1.9 collective-permute-start.2
  137.8 6.3 %collective-permute-done.2 = bf16[32,512]{1,0:T(8,128)(2,1)S(1)} collective-permute-done((bf16[32,512]{1,0:T(8,128)(2,1)S(1)}, bf16[32,512]{1,0:T(8,128)(2,1)S(1)}, u32[]{:S(2)}, u32[]{:S(2)}) %collective-permute-start.2) | collective-permute-done | bytes 32800 | tf_op jit(solution)/shard_map/ppermute | solution.py:129
  144.1 0.7 broadcast_in_dim.29
  144.8 7.8 %all-to-all-start.4 = ((bf16[8,32,512]{2,1,0:T(8,128)(2,1)}), bf16[8,32,512]{2,1,0:T(8,128)(2,1)S(1)}, u32[]{:S(2)}, u32[]{:S(2)}) async-start(bf16[8,32,512]{2,1,0:T(8,128)(2,1)} %broadcast_in_dim.29), calls=%async_computation.4 | async-start | bytes 524288 | tf_op jit(solution)/shard_map/all_to_all | solution.py:31
  152.7 10.5 %all-to-all-done.4 = bf16[8,32,512]{2,1,0:T(8,128)(2,1)S(1)} async-done(((bf16[8,32,512]{2,1,0:T(8,128)(2,1)}), bf16[8,32,512]{2,1,0:T(8,128)(2,1)S(1)}, u32[]{:S(2)}, u32[]{:S(2)}) %all-to-all-start.4) | async-done | bytes 262176 | tf_op jit(solution)/shard_map/all_to_all | solution.py:31
  163.2 16.5 %all_to_all.66 = f32[8,32,512]{2,1,0:T(8,128)S(1)} all-to-all(f32[8,32,512]{2,1,0:T(8,128)S(1)} %broadcast_in_dim.60), channel_id=1, replica_groups=mesh['x'=4,'y'=8,'z'=8,'core'=2] {'z'}, dimensions={0} | all-to-all | bytes 1048576 | tf_op jit(solution)/shard_map/all_to_all | solution.py:31
  179.7 0.7 broadcast_in_dim.61
  180.5 6.8 %all-to-all-start.10 = ((bf16[8,32,512]{2,1,0:T(8,128)(2,1)}), bf16[8,32,512]{2,1,0:T(8,128)(2,1)S(1)}, u32[]{:S(2)}, u32[]{:S(2)}) async-start(bf16[8,32,512]{2,1,0:T(8,128)(2,1)} %broadcast_in_dim.61), calls=%async_computation.10 | async-start | bytes 524288 | tf_op jit(solution)/shard_map/all_to_all | solution.py:31
  187.3 1.9 collective-permute-start.6
  189.2 2.4 %collective-permute-start.3 = (bf16[256,512]{1,0:T(8,128)(2,1)S(1)}, bf16[256,512]{1,0:T(8,128)(2,1)S(1)}, u32[]{:S(2)}, u32[]{:S(2)}) collective-permute-start(bf16[256,512]{1,0:T(8,128)(2,1)S(1)} %bitcast.47), channel_id=1, source_target_pairs={{0,1},{1,0},{2,3},{3,2},{4,5},{5,4},{6,7},{7,6},{8,9},{9,8},{10,11... | collective-permute-start | bytes 786440 | tf_op jit(solution)/shard_map/ppermute | solution.py:36
  191.6 6.2 %all-to-all-done.10 = bf16[8,32,512]{2,1,0:T(8,128)(2,1)S(1)} async-done(((bf16[8,32,512]{2,1,0:T(8,128)(2,1)}), bf16[8,32,512]{2,1,0:T(8,128)(2,1)S(1)}, u32[]{:S(2)}, u32[]{:S(2)}) %all-to-all-start.10) | async-done | bytes 262176 | tf_op jit(solution)/shard_map/all_to_all | solution.py:31
  197.8 1.1 broadcast_in_dim.63
  198.8 6.5 %all-to-all-start.11 = ((bf16[4,256,512]{2,1,0:T(8,128)(2,1)}), bf16[4,256,512]{2,1,0:T(8,128)(2,1)S(1)}, u32[]{:S(2)}, u32[]{:S(2)}) async-start(bf16[4,256,512]{2,1,0:T(8,128)(2,1)} %broadcast_in_dim.63), calls=%async_computation.11 | async-start | bytes 2097152 | tf_op jit(solution)/shard_map/all_to_all | solution.py:31
  205.6 0.7 copy-done.4
  206.4 2.9 %convolution_add_fusion = f32[512,512]{1,0:T(8,128)} fusion(bf16[256,512]{1,0:T(8,128)(2,1)S(1)} %get-tuple-element.53, bf16[256,512]{1,0:T(8,128)(2,1)S(1)} %get-tuple-element.52, bf16[256,512]{1,0:T(8,128)(2,1)S(1)} %copy-done.6, bf16[256,512]{1,0:T(8,128)(2,1)S(1)} %copy-done.4, f32[256,512]{1,0:T(8,128)S(1)} %get-tuple-element.51, ...), kind=kOutput, calls=%fused_computation.11 | convolution fusion | flops 1613758464 | bytes 3145728 | tf_op jit(solution)/shard_map/dot_general | solution.py:73
  209.4 1.6 copy.7
  210.9 20.7 %while.14 = (f32[512,512]{0,1:T(8,128)S(1)}, f32[512,512]{1,0:T(8,128)S(1)}, f32[]{:T(128)}, s32[]{:T(128)}, f32[]{:T(128)}, /*index=5*/s32[]{:T(128)}) while((f32[512,512]{0,1:T(8,128)S(1)}, f32[512,512]{1,0:T(8,128)S(1)}, f32[]{:T(128)}, s32[]{:T(128)}, f32[]{:T(128)}, /*index=5*/s32[]{:T(128)}) %tuple.28), condition=%wide.region_9.10_spmd, body=%wide.region_6.9_spmd.sunk | while | flops 3222011904 | bytes 9441369 | solution.py:85
  211.0 1.9 abs_reduce_fusion.2
  213.0 1.8 fusion.55
  216.2 1.9 abs_reduce_fusion.2
  218.1 1.8 fusion.55
  221.4 1.9 abs_reduce_fusion.2
  223.3 1.8 fusion.55
  226.5 1.9 abs_reduce_fusion.2
  228.5 1.8 fusion.55
  231.7 0.8 fusion.18
  232.4 0.8 copy-done.2
  233.2 2.1 add_add_fusion
  (53 shorter events, 6.1 us)
Async XLA Ops:
  0.0 1.0 copy-start
  1.3 43.1 %copy-start.1 = (f32[512,1024]{1,0:T(8,128)S(1)}, f32[512,1024]{1,0:T(8,128)}, u32[]{:S(2)}) copy-start(f32[512,1024]{1,0:T(8,128)} %param.5) | copy-start | bytes 6291460
  1.4 3.6 %collective-permute-start = (bf16[256,512]{1,0:T(8,128)(2,1)S(1)}, bf16[256,512]{1,0:T(8,128)(2,1)S(1)}, u32[]{:S(2)}, u32[]{:S(2)}) collective-permute-start(bf16[256,512]{1,0:T(8,128)(2,1)S(1)} %dynamic-slice_bitcast_fusion), channel_id=1, source_target_pairs={{0,1},{1,0},{2,3},{3,2},{4,5},{5,4},{6,7},{7,6},{8,9},{9,8},{10,11... | collective-permute-start | bytes 786440 | tf_op jit(solution)/shard_map/ppermute | solution.py:36
  40.9 3.4 %collective-permute-start.1 = (bf16[256,512]{1,0:T(8,128)(2,1)S(1)}, bf16[256,512]{1,0:T(8,128)(2,1)S(1)}, u32[]{:S(2)}, u32[]{:S(2)}) collective-permute-start(bf16[256,512]{1,0:T(8,128)(2,1)S(1)} %bitcast.48), channel_id=1, source_target_pairs={{0,1},{1,0},{2,3},{3,2},{4,5},{5,4},{6,7},{7,6},{8,9},{9,8},{10,11... | collective-permute-start | bytes 786440 | tf_op jit(solution)/shard_map/ppermute | solution.py:36
  44.4 0.9 copy-start.3
  44.4 0.9 copy-start.5
  65.6 18.2 %all-to-all-start.3 = ((bf16[8,32,512]{2,1,0:T(8,128)(2,1)}), bf16[8,32,512]{2,1,0:T(8,128)(2,1)S(1)}, u32[]{:S(2)}, u32[]{:S(2)}) async-start(bf16[8,32,512]{2,1,0:T(8,128)(2,1)} %bitcast.6), calls=%async_computation.3 | async-start | bytes 524288 | tf_op jit(solution)/shard_map/all_to_all | solution.py:23
  72.7 11.1 %collective-permute-start.4 = (bf16[32,512]{1,0:T(8,128)(2,1)S(1)}, bf16[32,512]{1,0:T(8,128)(2,1)S(1)}, u32[]{:S(2)}, u32[]{:S(2)}) collective-permute-start(bf16[32,512]{1,0:T(8,128)(2,1)S(1)} %reduce_sum.69), channel_id=1, source_target_pairs={{0,0},{1,128},{2,16},{3,144},{4,32},{5,160},{6,48},{7,176},{8,64},... | collective-permute-start | bytes 98312 | tf_op jit(solution)/shard_map/ppermute | solution.py:103
  84.5 3.8 %collective-permute-start.5 = (f32[256,512]{1,0:T(8,128)S(1)}, f32[256,512]{1,0:T(8,128)S(1)}, u32[]{:S(2)}, u32[]{:S(2)}) collective-permute-start(f32[256,512]{1,0:T(8,128)S(1)} %constant_dynamic-slice_fusion), channel_id=1, source_target_pairs={{0,1},{1,0},{2,3},{3,2},{4,5},{5,4},{6,7},{7,6},{8,9},{9,8},{10,11... | collective-permute-start | bytes 1572872 | tf_op jit(solution)/shard_map/ppermute | solution.py:36
  132.5 11.7 %all-to-all-start.8 = ((f32[8,4,512]{2,1,0:T(4,128)}), f32[8,4,512]{2,1,0:T(4,128)S(1)}, u32[]{:S(2)}, u32[]{:S(2)}) async-start(f32[8,4,512]{2,1,0:T(4,128)} %broadcast_in_dim.58), calls=%async_computation.8 | async-start | bytes 131072 | tf_op jit(solution)/shard_map/all_to_all | solution.py:31
  135.8 8.2 %collective-permute-start.2 = (bf16[32,512]{1,0:T(8,128)(2,1)S(1)}, bf16[32,512]{1,0:T(8,128)(2,1)S(1)}, u32[]{:S(2)}, u32[]{:S(2)}) collective-permute-start(bf16[32,512]{1,0:T(8,128)(2,1)S(1)} %get-tuple-element.56), channel_id=1, source_target_pairs={{0,0},{128,1},{16,2},{144,3},{32,4},{160,5},{48,6},{176,7},{64,8},... | collective-permute-start | bytes 98312 | tf_op jit(solution)/shard_map/ppermute | solution.py:129
  144.8 18.3 %all-to-all-start.4 = ((bf16[8,32,512]{2,1,0:T(8,128)(2,1)}), bf16[8,32,512]{2,1,0:T(8,128)(2,1)S(1)}, u32[]{:S(2)}, u32[]{:S(2)}) async-start(bf16[8,32,512]{2,1,0:T(8,128)(2,1)} %broadcast_in_dim.29), calls=%async_computation.4 | async-start | bytes 524288 | tf_op jit(solution)/shard_map/all_to_all | solution.py:31
  180.5 17.3 %all-to-all-start.10 = ((bf16[8,32,512]{2,1,0:T(8,128)(2,1)}), bf16[8,32,512]{2,1,0:T(8,128)(2,1)S(1)}, u32[]{:S(2)}, u32[]{:S(2)}) async-start(bf16[8,32,512]{2,1,0:T(8,128)(2,1)} %broadcast_in_dim.61), calls=%async_computation.10 | async-start | bytes 524288 | tf_op jit(solution)/shard_map/all_to_all | solution.py:31
  187.3 18.1 %collective-permute-start.6 = (f32[256,512]{1,0:T(8,128)S(1)}, f32[256,512]{1,0:T(8,128)S(1)}, u32[]{:S(2)}, u32[]{:S(2)}) collective-permute-start(f32[256,512]{1,0:T(8,128)S(1)} %bitcast.43), channel_id=1, source_target_pairs={{0,1},{1,0},{2,3},{3,2},{4,5},{5,4},{6,7},{7,6},{8,9},{9,8},{10,11... | collective-permute-start | bytes 1572872 | tf_op jit(solution)/shard_map/ppermute | solution.py:36
  189.2 16.1 %collective-permute-start.3 = (bf16[256,512]{1,0:T(8,128)(2,1)S(1)}, bf16[256,512]{1,0:T(8,128)(2,1)S(1)}, u32[]{:S(2)}, u32[]{:S(2)}) collective-permute-start(bf16[256,512]{1,0:T(8,128)(2,1)S(1)} %bitcast.47), channel_id=1, source_target_pairs={{0,1},{1,0},{2,3},{3,2},{4,5},{5,4},{6,7},{7,6},{8,9},{9,8},{10,11... | collective-permute-start | bytes 786440 | tf_op jit(solution)/shard_map/ppermute | solution.py:36
  198.8 32.8 %all-to-all-start.11 = ((bf16[4,256,512]{2,1,0:T(8,128)(2,1)}), bf16[4,256,512]{2,1,0:T(8,128)(2,1)S(1)}, u32[]{:S(2)}, u32[]{:S(2)}) async-start(bf16[4,256,512]{2,1,0:T(8,128)(2,1)} %broadcast_in_dim.63), calls=%async_computation.11 | async-start | bytes 2097152 | tf_op jit(solution)/shard_map/all_to_all | solution.py:31
  205.4 1.0 copy-start.4
  205.4 1.0 copy-start.6
  231.6 1.6 copy-start.2

commit v2 on v1

--- a/solution.py
+++ b/solution.py
@@ -4,6 +4,7 @@
 import jax.numpy as jnp
 import numpy as np
 from jax import lax
+from jax.experimental.layout import Layout, with_layout_constraint
 from jax.sharding import Mesh
 from jax.sharding import PartitionSpec as P
 
@@ -14,7 +15,7 @@
 NX, NY, NZ, NC = 4, 8, 8, 2
 F32 = jnp.float32
 BF16 = jnp.bfloat16
-SMALL = 2.0**-14
+SMALL = 2.0**-1.5
 MAX_FACTORS = 48
 
 
@@ -69,20 +70,30 @@
 
 
 def solve_rows(start, square):
-    def dot(a, b):
-        return jnp.dot(a, b, precision=lax.Precision.HIGHEST, preferred_element_type=F32)
+    def dot(a, b, precision=lax.Precision.HIGHEST):
+        return jnp.dot(a, b, precision=precision, preferred_element_type=F32)
+
+    def norm(power):
+        return jnp.max(jnp.sum(jnp.abs(power), axis=0))
 
     def more(state):
-        _, power, last, count = state
-        return jnp.logical_and(last > SMALL, count < MAX_FACTORS)
+        return jnp.logical_and(state[2] > SMALL, state[3] < MAX_FACTORS)
 
     def step(state):
         total, power, _, count = state
         power = dot(power, power)
-        return total + dot(total, power), power, jnp.max(jnp.sum(jnp.abs(power), axis=0)), count + 1
+        total = with_layout_constraint(total + dot(total, power), Layout((0, 1)))
+        return total, power, norm(power), count + 1
 
-    state = (start + dot(start, square), square, jnp.float32(1.0), jnp.int32(0))
-    return lax.while_loop(more, step, state)[0]
+    total, power = start + dot(start, square), square
+    for _ in range(2):
+        power = dot(power, power)
+        total = total + dot(total, power)
+    total, power, _, _ = lax.while_loop(more, step, (total, power, norm(power), jnp.int32(0)))
+    for precision in (lax.Precision.HIGH, lax.Precision.HIGH, lax.Precision.DEFAULT):
+        power = dot(power, power, precision)
+        total = total + dot(total, power, precision)
+    return total
 
 
 def on_device(inverse, activations, forget):
@@ -112,23 +123,32 @@
     )
     summed = scatter_sum(part.astype(BF16), "x", NX)
     change = scatter_sum(summed.astype(BF16), "y", NY)
-    images_piece = change + piece_by_columns.astype(F32)
+    change = change.astype(BF16)
+    both = jnp.concatenate([piece_by_columns, change], axis=0)
+    both = gather(both, "y", NY).reshape(NY, 2, -1, both.shape[1])
+    rows_cols = both[:, 0].reshape(-1, both.shape[3])
+    change_cols = both[:, 1].reshape(-1, both.shape[3])
 
-    share = lax.dot_general(
-        piece_by_columns.astype(F32),
-        images_piece * BETA,
-        (((0,), (0,)), ((), ())),
-        precision=lax.Precision.HIGHEST,
-        preferred_element_type=F32,
+    share = sum(
+        lax.dot_general(rows_cols, term, (((0,), (0,)), ((), ())), preferred_element_type=F32)
+        for term in (rows_cols, change_cols)
     )
-    share = scatter_sum(fold_cores(share).astype(BF16), "z", NZ)
-    share = scatter_sum(share, "y", NY)
+    share = scatter_sum(fold_cores(share * BETA).astype(BF16), "z", NZ)
     share = jnp.sum(gather(share[None], "x", NX), axis=0)
-    scaled = join_cores(gather(gather(share, "y", NY), "z", NZ))
 
-    change_here = join_cores(gather(lax.ppermute(change.astype(BF16), AXES, to_rows), "z", NZ))
-    images_rows = rows_here.astype(F32) + change_here.astype(F32)
-    images_cols = gather(gather(images_piece.astype(BF16), "y", NY), "x", NX)
+    change_there = lax.ppermute(change, AXES, to_rows)
+    gathered = gather(jnp.concatenate(exact_pair(share) + (change_there,), axis=0), "z", NZ)
+    mine, other = gathered, swap(gathered)
+    first = core == 0
+    halves = [jnp.where(first, mine, other), jnp.where(first, other, mine)]
+    halves = [h.reshape(NZ, -1, h.shape[1]).astype(F32) for h in halves]
+    n = share.shape[0]
+    scaled = [(h[:, :n] + h[:, n : 2 * n]).reshape(-1, h.shape[2]) for h in halves]
+    scaled = jnp.concatenate(scaled, axis=0)
+    change_here = [h[:, 2 * n :].reshape(-1, h.shape[2]) for h in halves]
+    change_here = jnp.concatenate(change_here, axis=0)
+    images_rows = rows_here.astype(F32) + change_here
+    images_cols = gather((rows_cols.astype(F32) + change_cols.astype(F32)).astype(BF16), "x", NX)
 
     solved = solve_rows(images_rows * BETA, scaled)
     update = sum(

time: 236 us -> 204 us (0.86)
  the two profiles are of different devices: /device:TPU:2 before, /device:TPU:1 now
where the time goes in v2:
time: 204 us; the launch traced here: 203 us
  blocking collectives  112 us (55%)
  starting transfers between devices  49.8 us (24%)
  matrix products  22.3 us (11%)
  waiting for transfers between devices  12.3 us (6%)
  other arithmetic  3.45 us (2%)
  local copies, waits for them, and re-layouts  2.33 us (1%)
    all_to_all x3, blocking collectives, gather(): lax.all_to_all(jnp.broadcast_to(x[None], (parts,) + x.shape), axis, 0, 0,...  63.2 us
    all_to_all x3, blocking collectives, spread(): return lax.all_to_all(x, axis, 0, 0, tiled=True)  48.3 us
    ppermute x4, starting transfers between devices, swap(): return lax.ppermute(x, 'core', [(0, 1), (1, 0)])  27.5 us
    dot_general x10, matrix products, dot(): return jnp.dot(a, b, precision=precision, preferred_element_type=F32)  14.2 us
    all_to_all x2, starting transfers between devices, gather(): lax.all_to_all(jnp.broadcast_to(x[None], (parts,) + x.shape), axis, 0, 0,...  8.61 us
    all_to_all x1, starting transfers between devices, spread(): return lax.all_to_all(x, axis, 0, 0, tiled=True)  6.83 us
    dot_general x2, matrix products, on_device(): lax.dot_general(term, images_cols, (((1,), (1,)), ((), ())), preferred_el...  5.42 us
    all_to_all x1, waiting for transfers between devices, spread(): return lax.all_to_all(x, axis, 0, 0, tiled=True)  5.07 us
  transfers between devices with their start and end apart: 9, of which 6 were waited for; matrix products, arithmetic and copies ran while one was open for 8% of the time, Pallas kernels for 0%

profile of v2, /device:TPU:1, one launch (start us, length us, event | category | flops | bytes accessed | tf_op | source)
XLA Modules:
  0.0 203.0 jit_solution(7805572849973301312)
XLA Ops:
  0.0 0.7 broadcast_subtract_fusion
  0.7 0.2 copy-done
  1.0 0.4 convolution_convert_fusion
  1.4 8.9 %collective-permute-start = (bf16[256,512]{1,0:T(8,128)(2,1)S(1)}, bf16[256,512]{1,0:T(8,128)(2,1)S(1)}, u32[]{:S(2)}, u32[]{:S(2)}) collective-permute-start(bf16[256,512]{1,0:T(8,128)(2,1)S(1)} %dynamic-slice_bitcast_fusion), channel_id=1, source_target_pairs={{0,1},{1,0},{2,3},{3,2},{4,5},{5,4},{6,7},{7,6},{8,9},{9,8},{10,11... | collective-permute-start | bytes 786440 | tf_op jit(solution)/shard_map/ppermute | solution.py:37
  10.3 1.1 collective-permute-done
  11.5 15.6 %all_to_all.45 = bf16[8,32,512]{2,1,0:T(8,128)(2,1)S(1)} all-to-all(bf16[8,32,512]{2,1,0:T(8,128)(2,1)S(1)} %bitcast.101), channel_id=1, replica_groups=mesh['x'=4,'y'=8,'z'=8,'core'=2] {'z'}, dimensions={0} | all-to-all | bytes 524288 | tf_op jit(solution)/shard_map/all_to_all | solution.py:24
  27.2 12.2 %all_to_all.46 = bf16[8,32,512]{2,1,0:T(8,128)(2,1)S(1)} all-to-all(bf16[8,32,512]{2,1,0:T(8,128)(2,1)S(1)} %broadcast_in_dim.18), channel_id=1, replica_groups=mesh['x'=4,'y'=8,'z'=8,'core'=2] {'z'}, dimensions={0} | all-to-all | bytes 524288 | tf_op jit(solution)/shard_map/all_to_all | solution.py:32
  39.3 4.9 %collective-permute-start.1 = (bf16[256,512]{1,0:T(8,128)(2,1)S(1)}, bf16[256,512]{1,0:T(8,128)(2,1)S(1)}, u32[]{:S(2)}, u32[]{:S(2)}) collective-permute-start(bf16[256,512]{1,0:T(8,128)(2,1)S(1)} %bitcast.100), channel_id=1, source_target_pairs={{0,1},{1,0},{2,3},{3,2},{4,5},{5,4},{6,7},{7,6},{8,9},{9,8},{10,11... | collective-permute-start | bytes 786440 | tf_op jit(solution)/shard_map/ppermute | solution.py:37
  44.3 1.1 collective-permute-done.1
  45.5 0.8 fusion.7
  46.3 0.8 add_convert_fusion
  47.2 18.1 %all_to_all.47 = bf16[4,256,512]{2,1,0:T(8,128)(2,1)S(1)} all-to-all(bf16[4,256,512]{2,1,0:T(8,128)(2,1)S(1)} %bitcast.99), channel_id=1, replica_groups=mesh['x'=4,'y'=8,'z'=8,'core'=2] {'x'}, dimensions={0} | all-to-all | bytes 2097152 | tf_op jit(solution)/shard_map/all_to_all | solution.py:24
  65.2 0.9 reduce_sum.73
  66.1 6.8 %all-to-all-start.3 = ((bf16[8,32,512]{2,1,0:T(8,128)(2,1)}), bf16[8,32,512]{2,1,0:T(8,128)(2,1)S(1)}, u32[]{:S(2)}, u32[]{:S(2)}) async-start(bf16[8,32,512]{2,1,0:T(8,128)(2,1)} %bitcast.6), calls=%async_computation.3 | async-start | bytes 524288 | tf_op jit(solution)/shard_map/all_to_all | solution.py:24
  73.0 4.2 %collective-permute-start.2 = (bf16[32,512]{1,0:T(8,128)(2,1)S(1)}, bf16[32,512]{1,0:T(8,128)(2,1)S(1)}, u32[]{:S(2)}, u32[]{:S(2)}) collective-permute-start(bf16[32,512]{1,0:T(8,128)(2,1)S(1)} %reduce_sum.72), channel_id=1, source_target_pairs={{0,0},{1,128},{2,16},{3,144},{4,32},{5,160},{6,48},{7,176},{8,64},... | collective-permute-start | bytes 98312 | tf_op jit(solution)/shard_map/ppermute | solution.py:114
  77.1 5.1 %all-to-all-done.3 = bf16[8,32,512]{2,1,0:T(8,128)(2,1)S(1)} async-done(((bf16[8,32,512]{2,1,0:T(8,128)(2,1)}), bf16[8,32,512]{2,1,0:T(8,128)(2,1)S(1)}, u32[]{:S(2)}, u32[]{:S(2)}) %all-to-all-start.3) | async-done | bytes 262176 | tf_op jit(solution)/shard_map/all_to_all | solution.py:24
  82.3 21.6 %all_to_all.48 = bf16[8,64,512]{2,1,0:T(8,128)(2,1)S(1)} all-to-all(bf16[8,64,512]{2,1,0:T(8,128)(2,1)S(1)} %broadcast_in_dim.21), channel_id=1, replica_groups=mesh['x'=4,'y'=8,'z'=8,'core'=2] {'y'}, dimensions={0} | all-to-all | bytes 1048576 | tf_op jit(solution)/shard_map/all_to_all | solution.py:32
  103.9 0.3 convolution_bitcast_fusion.1
  104.3 0.3 fusion.5
  104.6 8.0 %collective-permute-start.3 = (f32[256,512]{1,0:T(8,128)S(1)}, f32[256,512]{1,0:T(8,128)S(1)}, u32[]{:S(2)}, u32[]{:S(2)}) collective-permute-start(f32[256,512]{1,0:T(8,128)S(1)} %constant_dynamic-slice_fusion), channel_id=1, source_target_pairs={{0,1},{1,0},{2,3},{3,2},{4,5},{5,4},{6,7},{7,6},{8,9},{9,8},{10,11... | collective-permute-start | bytes 1572872 | tf_op jit(solution)/shard_map/ppermute | solution.py:37
  112.7 1.5 collective-permute-done.3
  114.3 14.7 %all_to_all.49 = bf16[8,32,512]{2,1,0:T(8,128)(2,1)S(1)} all-to-all(bf16[8,32,512]{2,1,0:T(8,128)(2,1)S(1)} %bitcast.98), channel_id=1, replica_groups=mesh['x'=4,'y'=8,'z'=8,'core'=2] {'z'}, dimensions={0} | all-to-all | bytes 524288 | tf_op jit(solution)/shard_map/all_to_all | solution.py:24
  129.0 0.7 broadcast_in_dim.22
  129.7 4.2 %all-to-all-start.6 = ((f32[4,1,32,512]{3,2,1,0:T(8,128)}), f32[4,1,32,512]{3,2,1,0:T(8,128)S(1)}, u32[]{:S(2)}, u32[]{:S(2)}) async-start(f32[4,1,32,512]{3,2,1,0:T(8,128)} %broadcast_in_dim.22), calls=%async_computation.6 | async-start | bytes 524288 | tf_op jit(solution)/shard_map/all_to_all | solution.py:32
  133.9 2.7 %collective-permute-start.4 = (bf16[32,512]{1,0:T(8,128)(2,1)S(1)}, bf16[32,512]{1,0:T(8,128)(2,1)S(1)}, u32[]{:S(2)}, u32[]{:S(2)}) collective-permute-start(bf16[32,512]{1,0:T(8,128)(2,1)S(1)} %reduce_sum.74), channel_id=1, source_target_pairs={{0,0},{128,1},{16,2},{144,3},{32,4},{160,5},{48,6},{176,7},{64,8},... | collective-permute-start | bytes 98312 | tf_op jit(solution)/shard_map/ppermute | solution.py:139
  136.6 3.0 %all-to-all-done.6 = f32[4,1,32,512]{3,2,1,0:T(8,128)S(1)} async-done(((f32[4,1,32,512]{3,2,1,0:T(8,128)}), f32[4,1,32,512]{3,2,1,0:T(8,128)S(1)}, u32[]{:S(2)}, u32[]{:S(2)}) %all-to-all-start.6) | async-done | bytes 262176 | tf_op jit(solution)/shard_map/all_to_all | solution.py:32
  139.7 0.5 collective-permute-done.4
  140.2 29.4 %all_to_all.50 = bf16[8,96,512]{2,1,0:T(8,128)(2,1)S(1)} all-to-all(bf16[8,96,512]{2,1,0:T(8,128)(2,1)S(1)} %broadcast_in_dim.23), channel_id=1, replica_groups=mesh['x'=4,'y'=8,'z'=8,'core'=2] {'z'}, dimensions={0} | all-to-all | bytes 1572864 | tf_op jit(solution)/shard_map/all_to_all | solution.py:32
  169.6 5.6 %collective-permute-start.5 = (bf16[768,512]{1,0:T(8,128)(2,1)S(1)}, bf16[768,512]{1,0:T(8,128)(2,1)S(1)}, u32[]{:S(2)}, u32[]{:S(2)}) collective-permute-start(bf16[768,512]{1,0:T(8,128)(2,1)S(1)} %bitcast.89), channel_id=1, source_target_pairs={{0,1},{1,0},{2,3},{3,2},{4,5},{5,4},{6,7},{7,6},{8,9},{9,8},{10,11... | collective-permute-start | bytes 2359304 | tf_op jit(solution)/shard_map/ppermute | solution.py:37
  175.4 1.1 broadcast_in_dim.24
  176.4 4.4 %all-to-all-start.8 = ((bf16[4,256,512]{2,1,0:T(8,128)(2,1)}), bf16[4,256,512]{2,1,0:T(8,128)(2,1)}, u32[]{:S(2)}, u32[]{:S(2)}) async-start(bf16[4,256,512]{2,1,0:T(8,128)(2,1)} %broadcast_in_dim.24), calls=%async_computation.8 | async-start | bytes 2097152 | tf_op jit(solution)/shard_map/all_to_all | solution.py:32
  180.9 0.2 broadcast_select_fusion.1
  181.1 0.2 convert.5
  181.4 0.2 convert.6
  181.7 1.9 fusion.22
  183.6 1.9 abs_reduce_fusion.1
  185.5 2.0 convolution_add_fusion.5
  187.5 1.9 convolution_add_fusion.4
  189.3 0.6 reduce_max.18
  189.9 1.8 convolution_add_fusion.3
  191.8 0.9 while.14
  192.7 1.0 fusion.44
  193.7 1.0 fusion.45
  194.7 1.0 convolution_add_fusion.2
  195.7 1.0 convolution_add_fusion.1
  196.7 0.8 convolution_add_fusion
  197.5 2.1 %fusion.24 = f32[512,1024]{1,0:T(8,128)S(1)} fusion(bf16[1024,512]{1,0:T(8,128)(2,1)} %bitcast.23, f32[512,512]{1,0:T(8,128)S(1)} %convolution_add_fusion), kind=kOutput, calls=%fused_computation.43 | convolution fusion | flops 537395200 | bytes 4194304 | tf_op jit(solution)/shard_map/dot_general | solution.py:155
  199.7 3.3 %add_add_fusion = f32[512,1024]{1,0:T(8,128)} fusion(f32[512,1024]{1,0:T(8,128)S(1)} %copy-done.2, f32[512,1024]{1,0:T(8,128)S(1)} %fusion.24, bf16[1024,512]{1,0:T(8,128)(2,1)} %bitcast.23, f32[512,512]{1,0:T(8,128)S(1)} %convolution_add_fusion), kind=kOutput, calls=%fused_computation.6 | convolution fusion | flops 538705920 | bytes 8388608 | tf_op jit(solution)/shard_map/dot_general | solution.py:155
  (30 shorter events, 1.0 us)
Async XLA Ops:
  0.0 1.0 copy-start
  1.3 44.2 %copy-start.1 = (f32[512,1024]{1,0:T(8,128)S(1)}, f32[512,1024]{1,0:T(8,128)}, u32[]{:S(2)}) copy-start(f32[512,1024]{1,0:T(8,128)} %param.5) | copy-start | bytes 6291460
  1.4 10.0 %collective-permute-start = (bf16[256,512]{1,0:T(8,128)(2,1)S(1)}, bf16[256,512]{1,0:T(8,128)(2,1)S(1)}, u32[]{:S(2)}, u32[]{:S(2)}) collective-permute-start(bf16[256,512]{1,0:T(8,128)(2,1)S(1)} %dynamic-slice_bitcast_fusion), channel_id=1, source_target_pairs={{0,1},{1,0},{2,3},{3,2},{4,5},{5,4},{6,7},{7,6},{8,9},{9,8},{10,11... | collective-permute-start | bytes 786440 | tf_op jit(solution)/shard_map/ppermute | solution.py:37
  39.3 6.1 %collective-permute-start.1 = (bf16[256,512]{1,0:T(8,128)(2,1)S(1)}, bf16[256,512]{1,0:T(8,128)(2,1)S(1)}, u32[]{:S(2)}, u32[]{:S(2)}) collective-permute-start(bf16[256,512]{1,0:T(8,128)(2,1)S(1)} %bitcast.100), channel_id=1, source_target_pairs={{0,1},{1,0},{2,3},{3,2},{4,5},{5,4},{6,7},{7,6},{8,9},{9,8},{10,11... | collective-permute-start | bytes 786440 | tf_op jit(solution)/shard_map/ppermute | solution.py:37
  66.1 16.1 %all-to-all-start.3 = ((bf16[8,32,512]{2,1,0:T(8,128)(2,1)}), bf16[8,32,512]{2,1,0:T(8,128)(2,1)S(1)}, u32[]{:S(2)}, u32[]{:S(2)}) async-start(bf16[8,32,512]{2,1,0:T(8,128)(2,1)} %bitcast.6), calls=%async_computation.3 | async-start | bytes 524288 | tf_op jit(solution)/shard_map/all_to_all | solution.py:24
  73.0 9.3 %collective-permute-start.2 = (bf16[32,512]{1,0:T(8,128)(2,1)S(1)}, bf16[32,512]{1,0:T(8,128)(2,1)S(1)}, u32[]{:S(2)}, u32[]{:S(2)}) collective-permute-start(bf16[32,512]{1,0:T(8,128)(2,1)S(1)} %reduce_sum.72), channel_id=1, source_target_pairs={{0,0},{1,128},{2,16},{3,144},{4,32},{5,160},{6,48},{7,176},{8,64},... | collective-permute-start | bytes 98312 | tf_op jit(solution)/shard_map/ppermute | solution.py:114
  104.6 9.6 %collective-permute-start.3 = (f32[256,512]{1,0:T(8,128)S(1)}, f32[256,512]{1,0:T(8,128)S(1)}, u32[]{:S(2)}, u32[]{:S(2)}) collective-permute-start(f32[256,512]{1,0:T(8,128)S(1)} %constant_dynamic-slice_fusion), channel_id=1, source_target_pairs={{0,1},{1,0},{2,3},{3,2},{4,5},{5,4},{6,7},{7,6},{8,9},{9,8},{10,11... | collective-permute-start | bytes 1572872 | tf_op jit(solution)/shard_map/ppermute | solution.py:37
  129.7 9.9 %all-to-all-start.6 = ((f32[4,1,32,512]{3,2,1,0:T(8,128)}), f32[4,1,32,512]{3,2,1,0:T(8,128)S(1)}, u32[]{:S(2)}, u32[]{:S(2)}) async-start(f32[4,1,32,512]{3,2,1,0:T(8,128)} %broadcast_in_dim.22), calls=%async_computation.6 | async-start | bytes 524288 | tf_op jit(solution)/shard_map/all_to_all | solution.py:32
  133.9 6.2 %collective-permute-start.4 = (bf16[32,512]{1,0:T(8,128)(2,1)S(1)}, bf16[32,512]{1,0:T(8,128)(2,1)S(1)}, u32[]{:S(2)}, u32[]{:S(2)}) collective-permute-start(bf16[32,512]{1,0:T(8,128)(2,1)S(1)} %reduce_sum.74), channel_id=1, source_target_pairs={{0,0},{128,1},{16,2},{144,3},{32,4},{160,5},{48,6},{176,7},{64,8},... | collective-permute-start | bytes 98312 | tf_op jit(solution)/shard_map/ppermute | solution.py:139
  169.6 11.2 %collective-permute-start.5 = (bf16[768,512]{1,0:T(8,128)(2,1)S(1)}, bf16[768,512]{1,0:T(8,128)(2,1)S(1)}, u32[]{:S(2)}, u32[]{:S(2)}) collective-permute-start(bf16[768,512]{1,0:T(8,128)(2,1)S(1)} %bitcast.89), channel_id=1, source_target_pairs={{0,1},{1,0},{2,3},{3,2},{4,5},{5,4},{6,7},{7,6},{8,9},{9,8},{10,11... | collective-permute-start | bytes 2359304 | tf_op jit(solution)/shard_map/ppermute | solution.py:37
  176.4 21.1 %all-to-all-start.8 = ((bf16[4,256,512]{2,1,0:T(8,128)(2,1)}), bf16[4,256,512]{2,1,0:T(8,128)(2,1)}, u32[]{:S(2)}, u32[]{:S(2)}) async-start(bf16[4,256,512]{2,1,0:T(8,128)(2,1)} %broadcast_in_dim.24), calls=%async_computation.8 | async-start | bytes 2097152 | tf_op jit(solution)/shard_map/all_to_all | solution.py:32
  197.5 2.1 %copy-start.2 = (f32[512,1024]{1,0:T(8,128)S(1)}, f32[512,1024]{1,0:T(8,128)}, u32[]{:S(2)}) copy-start(f32[512,1024]{1,0:T(8,128)} %param.5) | copy-start | bytes 6291460

commit v3 on v2

--- a/solution.py
+++ b/solution.py
@@ -4,9 +4,12 @@
 import jax.numpy as jnp
 import numpy as np
 from jax import lax
+from jax.experimental import pallas as pl
+from jax.experimental.pallas import tpu as pltpu
 from jax.experimental.layout import Layout, with_layout_constraint
 from jax.sharding import Mesh
 from jax.sharding import PartitionSpec as P
+
 
 M = 16384
 ROWS = 512
@@ -17,6 +20,7 @@
 BF16 = jnp.bfloat16
 SMALL = 2.0**-1.5
 MAX_FACTORS = 48
+PAD = 8
 
 
 def spread(x, axis, parts):
@@ -43,12 +47,6 @@
     there = lax.dynamic_slice_in_dim(x, (1 - core) * half, half, 0)
     here = lax.dynamic_slice_in_dim(x, core * half, half, 0)
     return here + swap(there)
-
-
-def join_cores(x):
-    other = swap(x)
-    first = lax.axis_index("core") == 0
-    return jnp.concatenate([jnp.where(first, x, other), jnp.where(first, other, x)], axis=0)
 
 
 def exact_pair(x):
@@ -70,7 +68,7 @@
 
 
 def solve_rows(start, square):
-    def dot(a, b, precision=lax.Precision.HIGHEST):
+    def dot(a, b, precision=lax.Precision.HIGH):
         return jnp.dot(a, b, precision=precision, preferred_element_type=F32)
 
     def norm(power):
@@ -90,10 +88,46 @@
         power = dot(power, power)
         total = total + dot(total, power)
     total, power, _, _ = lax.while_loop(more, step, (total, power, norm(power), jnp.int32(0)))
-    for precision in (lax.Precision.HIGH, lax.Precision.HIGH, lax.Precision.DEFAULT):
+    for precision in (lax.Precision.HIGH, lax.Precision.DEFAULT, lax.Precision.DEFAULT):
         power = dot(power, power, precision)
         total = total + dot(total, power, precision)
     return total
+
+
+def add_product(inverse, solved, images):
+    height, width = inverse.shape
+    rows = solved.shape[1]
+    block = height // 4
+
+    def kernel(inverse_ref, solved_ref, images_ref, out_ref):
+        left = solved_ref[...]
+        high = left.astype(BF16)
+        low = (left - high.astype(F32)).astype(BF16)
+        total = inverse_ref[...]
+        for term in (low, high):
+            total += lax.dot_general(
+                term, images_ref[...], (((1,), (1,)), ((), ())), preferred_element_type=F32
+            )
+        out_ref[...] = total
+
+    return pl.pallas_call(
+        kernel,
+        out_shape=jax.ShapeDtypeStruct(inverse.shape, F32),
+        grid=(height // block,),
+        in_specs=[
+            pl.BlockSpec((block, width), lambda i: (i, 0)),
+            pl.BlockSpec((block, rows), lambda i: (i, 0)),
+            pl.BlockSpec((width, rows), lambda i: (0, 0)),
+        ],
+        out_specs=pl.BlockSpec((block, width), lambda i: (i, 0)),
+        cost_estimate=pl.CostEstimate(
+            flops=4 * height * width * rows,
+            bytes_accessed=8 * height * width + 4 * height * rows + 2 * width * rows,
+            transcendentals=0,
+        ),
+        compiler_params=pltpu.CompilerParams(vmem_limit_bytes=61 << 20),
+        name="add_product",
+    )(inverse, solved, images)
 
 
 def on_device(inverse, activations, forget):
@@ -111,8 +145,9 @@
         activations, onehot, (((0,), (0,)), ((), ())), preferred_element_type=F32
     ).astype(BF16)
     piece = scatter_sum(fold_cores(picked), "z", NZ).astype(BF16)
-    piece_by_columns = lax.ppermute(piece, AXES, to_columns)
-    rows_here = join_cores(gather(piece, "z", NZ))
+    half = gather(piece, "z", NZ)
+    rows_cols = lax.ppermute(half, AXES, to_columns)
+    rows_here = lax.all_gather(half, "core", axis=0, tiled=True)
 
     row_number = wide * height + lax.broadcasted_iota(jnp.int32, inverse.shape, 0)
     col_number = narrow * width + lax.broadcasted_iota(jnp.int32, inverse.shape, 1)
@@ -124,10 +159,7 @@
     summed = scatter_sum(part.astype(BF16), "x", NX)
     change = scatter_sum(summed.astype(BF16), "y", NY)
     change = change.astype(BF16)
-    both = jnp.concatenate([piece_by_columns, change], axis=0)
-    both = gather(both, "y", NY).reshape(NY, 2, -1, both.shape[1])
-    rows_cols = both[:, 0].reshape(-1, both.shape[3])
-    change_cols = both[:, 1].reshape(-1, both.shape[3])
+    change_cols = gather(change, "y", NY)
 
     share = sum(
         lax.dot_general(rows_cols, term, (((0,), (0,)), ((), ())), preferred_element_type=F32)
@@ -136,31 +168,37 @@
     share = scatter_sum(fold_cores(share * BETA).astype(BF16), "z", NZ)
     share = jnp.sum(gather(share[None], "x", NX), axis=0)
 
+    n = share.shape[0]
+    own = (core * NZ + z) * n + lax.broadcasted_iota(jnp.int32, share.shape, 0)
+    on_diagonal = own == lax.broadcasted_iota(jnp.int32, share.shape, 1)
+    high, low = exact_pair(share)
+    low = jnp.sum(jnp.where(on_diagonal, low.astype(F32), 0.0), axis=0, keepdims=True)
+    low = jnp.pad(low, ((0, PAD - 1), (0, 0))).astype(BF16)
     change_there = lax.ppermute(change, AXES, to_rows)
-    gathered = gather(jnp.concatenate(exact_pair(share) + (change_there,), axis=0), "z", NZ)
+    gathered = gather(jnp.concatenate([high, low, change_there], axis=0), "z", NZ)
     mine, other = gathered, swap(gathered)
     first = core == 0
     halves = [jnp.where(first, mine, other), jnp.where(first, other, mine)]
     halves = [h.reshape(NZ, -1, h.shape[1]).astype(F32) for h in halves]
-    n = share.shape[0]
-    scaled = [(h[:, :n] + h[:, n : 2 * n]).reshape(-1, h.shape[2]) for h in halves]
-    scaled = jnp.concatenate(scaled, axis=0)
-    change_here = [h[:, 2 * n :].reshape(-1, h.shape[2]) for h in halves]
+    scaled = jnp.concatenate([h[:, :n].reshape(-1, h.shape[2]) for h in halves], axis=0)
+    low = jnp.sum(halves[0][:, n] + halves[1][:, n], axis=0)
+    diagonal = lax.broadcasted_iota(jnp.int32, scaled.shape, 0) == lax.broadcasted_iota(
+        jnp.int32, scaled.shape, 1
+    )
+    scaled = scaled + jnp.where(diagonal, low[None], 0.0)
+    change_here = [h[:, n + PAD :].reshape(-1, h.shape[2]) for h in halves]
     change_here = jnp.concatenate(change_here, axis=0)
     images_rows = rows_here.astype(F32) + change_here
     images_cols = gather((rows_cols.astype(F32) + change_cols.astype(F32)).astype(BF16), "x", NX)
 
     solved = solve_rows(images_rows * BETA, scaled)
-    update = sum(
-        lax.dot_general(term, images_cols, (((1,), (1,)), ((), ())), preferred_element_type=F32)
-        for term in exact_pair(solved)
-    )
-    return inverse + update
+    return add_product(inverse, solved, images_cols)
 
 
 def solution(mesh):
     devices = np.asarray(mesh.devices).reshape(NX, NY, NZ, NC)
     placed = (P(("x", "y"), ("z", "core")), P(("z", "core"), ("x", "y")), P())
+
     return jax.shard_map(
         on_device,
         mesh=Mesh(devices, AXES),

time: 204 us -> 230 us (1.13)
  waiting for transfers between devices: 12.3 us -> 33.4 us
  matrix products: 22.3 us -> 12.7 us
  blocking collectives: 112 us -> 120 us
  Pallas kernels: 0 us -> 6.09 us
    all_to_all x3 -> x4, blocking collectives: 48.3 us -> 88.2 us  [spread(): return lax.all_to_all(x, axis, 0, 0, tiled=True)]
    all_to_all x3 -> x1, blocking collectives: 63.2 us -> 27.1 us  [gather(): lax.all_to_all(jnp.broadcast_to(x[None], (parts,) + x.shape), axis, 0, 0,...]
    ppermute x1, waiting for transfers between devices: 0.01 us -> 14.8 us  [on_device(): rows_cols = lax.ppermute(half, AXES, to_columns)]
    all_to_all x2 -> x4, waiting for transfers between devices: 3 us -> 14.3 us  [gather(): lax.all_to_all(jnp.broadcast_to(x[None], (parts,) + x.shape), axis, 0, 0,...]
    all_to_all x1 -> x0, starting transfers between devices: 6.83 us -> none  [spread(): return lax.all_to_all(x, axis, 0, 0, tiled=True)]
    pallas_call x0 -> x1, Pallas kernels: none -> 6.09 us  [add_product(): pl.pallas_call(kernel, out_shape=jax.ShapeDtypeStruct(inverse.shape, F32)...]
    all_to_all x2 -> x4, starting transfers between devices: 8.61 us -> 14.5 us  [gather(): lax.all_to_all(jnp.broadcast_to(x[None], (parts,) + x.shape), axis, 0, 0,...]
    dot_general x2 -> x0, matrix products: 5.42 us -> none  [on_device(): lax.dot_general(term, images_cols, (((1,), (1,)), ((), ())), preferred_el...]
  transfers between devices with their start and end apart: 9 -> 9, of which waited for: 6 -> 7; matrix products, arithmetic and copies ran while one was open for 8% -> 5% of each run, Pallas kernels for 0% -> 0%
where the time goes in v3:
time: 230 us; the launch traced here: 228 us
  blocking collectives  120 us (52%)
  starting transfers between devices  47.7 us (21%)
  waiting for transfers between devices  33.4 us (15%)
  matrix products  12.7 us (6%)
  Pallas kernels  6.09 us (3%)
  local copies, waits for them, and re-layouts  3.83 us (2%)
  other arithmetic  3.46 us (2%)
    all_to_all x4, blocking collectives, spread(): return lax.all_to_all(x, axis, 0, 0, tiled=True)  88.2 us
    all_to_all x1, blocking collectives, gather(): lax.all_to_all(jnp.broadcast_to(x[None], (parts,) + x.shape), axis, 0, 0,...  27.1 us
    ppermute x3, starting transfers between devices, swap(): return lax.ppermute(x, 'core', [(0, 1), (1, 0)])  23.7 us
    ppermute x1, waiting for transfers between devices, on_device(): rows_cols = lax.ppermute(half, AXES, to_columns)  14.8 us
    all_to_all x4, starting transfers between devices, gather(): lax.all_to_all(jnp.broadcast_to(x[None], (parts,) + x.shape), axis, 0, 0,...  14.5 us
    all_to_all x4, waiting for transfers between devices, gather(): lax.all_to_all(jnp.broadcast_to(x[None], (parts,) + x.shape), axis, 0, 0,...  14.3 us
    dot_general x10, matrix products, dot(): return jnp.dot(a, b, precision=precision, preferred_element_type=F32)  9.98 us
    pallas_call x1, Pallas kernels, add_product(): pl.pallas_call(kernel, out_shape=jax.ShapeDtypeStruct(inverse.shape, F32)...  6.09 us
  transfers between devices with their start and end apart: 9, of which 7 were waited for; matrix products, arithmetic and copies ran while one was open for 5% of the time, Pallas kernels for 0%

profile of v3, /device:TPU:1, one launch (start us, length us, event | category | flops | bytes accessed | tf_op | source)
XLA Modules:
  0.0 228.4 jit_solution(16787869184434563038)
XLA Ops:
  0.0 0.7 broadcast_subtract_fusion
  0.7 0.2 copy-done
  1.0 0.4 convolution_convert_fusion
  1.4 8.9 %collective-permute-start = (bf16[256,512]{1,0:T(8,128)(2,1)S(1)}, bf16[256,512]{1,0:T(8,128)(2,1)}, u32[]{:S(2)}, u32[]{:S(2)}) collective-permute-start(bf16[256,512]{1,0:T(8,128)(2,1)S(1)} %dynamic-slice_bitcast_fusion), channel_id=1, source_target_pairs={{0,1},{1,0},{2,3},{3,2},{4,5},{5,4},{6,7},{7,6},{8,9},{9,8},{10,11... | collective-permute-start | bytes 786440 | tf_op jit(solution)/shard_map/ppermute | solution.py:41
  10.3 1.3 collective-permute-done
  11.5 1.0 bitcast_add_fusion
  12.6 15.6 %all_to_all.45 = bf16[8,32,512]{2,1,0:T(8,128)(2,1)S(1)} all-to-all(bf16[8,32,512]{2,1,0:T(8,128)(2,1)S(1)} %bitcast.76), channel_id=1, replica_groups=mesh['x'=4,'y'=8,'z'=8,'core'=2] {'z'}, dimensions={0} | all-to-all | bytes 524288 | tf_op jit(solution)/shard_map/all_to_all | solution.py:28
  28.2 0.7 broadcast_in_dim.60
  28.9 3.4 %all-to-all-start.1 = ((bf16[8,32,512]{2,1,0:T(8,128)(2,1)}), bf16[8,32,512]{2,1,0:T(8,128)(2,1)S(1)}, u32[]{:S(2)}, u32[]{:S(2)}) async-start(bf16[8,32,512]{2,1,0:T(8,128)(2,1)} %broadcast_in_dim.60), calls=%async_computation.1 | async-start | bytes 524288 | tf_op jit(solution)/shard_map/all_to_all | solution.py:36
  32.4 9.6 %all-to-all-done.1 = bf16[8,32,512]{2,1,0:T(8,128)(2,1)S(1)} async-done(((bf16[8,32,512]{2,1,0:T(8,128)(2,1)}), bf16[8,32,512]{2,1,0:T(8,128)(2,1)S(1)}, u32[]{:S(2)}, u32[]{:S(2)}) %all-to-all-start.1) | async-done | bytes 262176 | tf_op jit(solution)/shard_map/all_to_all | solution.py:36
  42.0 4.9 %all_gather.3 = bf16[512,512]{1,0:T(8,128)(2,1)S(1)} all-gather(bf16[256,512]{1,0:T(8,128)(2,1)S(1)} %bitcast.71), channel_id=1, replica_groups=mesh['x'=4,'y'=8,'z'=8,'core'=2] {'core'}, dimensions={0}, use_global_device_ids=true | all-gather | bytes 786432 | tf_op jit(solution)/shard_map/all_gather | solution.py:150
  46.9 0.9 fusion.6
  47.8 0.8 add_convert_fusion
  48.6 18.1 %all_to_all.46 = bf16[4,256,512]{2,1,0:T(8,128)(2,1)S(1)} all-to-all(bf16[4,256,512]{2,1,0:T(8,128)(2,1)S(1)} %bitcast.75), channel_id=1, replica_groups=mesh['x'=4,'y'=8,'z'=8,'core'=2] {'x'}, dimensions={0} | all-to-all | bytes 2097152 | tf_op jit(solution)/shard_map/all_to_all | solution.py:28
  66.7 0.2 reduce_sum.91
  66.9 15.8 %all_to_all.47 = bf16[8,32,512]{2,1,0:T(8,128)(2,1)S(1)} all-to-all(bf16[8,32,512]{2,1,0:T(8,128)(2,1)S(1)} %bitcast.74), channel_id=1, replica_groups=mesh['x'=4,'y'=8,'z'=8,'core'=2] {'y'}, dimensions={0} | all-to-all | bytes 524288 | tf_op jit(solution)/shard_map/all_to_all | solution.py:28
  82.8 0.7 broadcast_in_dim.63
  83.5 3.4 %all-to-all-start.4 = ((bf16[8,32,512]{2,1,0:T(8,128)(2,1)}), bf16[8,32,512]{2,1,0:T(8,128)(2,1)S(1)}, u32[]{:S(2)}, u32[]{:S(2)}) async-start(bf16[8,32,512]{2,1,0:T(8,128)(2,1)} %broadcast_in_dim.63), calls=%async_computation.4 | async-start | bytes 524288 | tf_op jit(solution)/shard_map/all_to_all | solution.py:36
  86.9 5.7 %collective-permute-start.1 = (bf16[256,512]{1,0:T(8,128)(2,1)S(1)}, bf16[256,512]{1,0:T(8,128)(2,1)S(1)}, u32[]{:S(2)}, u32[]{:S(2)}) collective-permute-start(bf16[256,512]{1,0:T(8,128)(2,1)S(1)} %bitcast.72), channel_id=1, source_target_pairs={{0,0},{1,128},{2,16},{3,144},{4,32},{5,160},{6,48},{7,176},{8,64},... | collective-permute-start | bytes 786440 | tf_op jit(solution)/shard_map/ppermute | solution.py:149
  92.6 14.8 %collective-permute-done.1 = bf16[256,512]{1,0:T(8,128)(2,1)S(1)} collective-permute-done((bf16[256,512]{1,0:T(8,128)(2,1)S(1)}, bf16[256,512]{1,0:T(8,128)(2,1)S(1)}, u32[]{:S(2)}, u32[]{:S(2)}) %collective-permute-start.1) | collective-permute-done | bytes 262176 | tf_op jit(solution)/shard_map/ppermute | solution.py:149
  107.4 0.3 fusion.44
  107.7 0.3 fusion.4
  108.1 10.3 %collective-permute-start.2 = (f32[256,512]{1,0:T(8,128)S(1)}, f32[256,512]{1,0:T(8,128)S(1)}, u32[]{:S(2)}, u32[]{:S(2)}) collective-permute-start(f32[256,512]{1,0:T(8,128)S(1)} %constant_dynamic-slice_fusion), channel_id=1, source_target_pairs={{0,1},{1,0},{2,3},{3,2},{4,5},{5,4},{6,7},{7,6},{8,9},{9,8},{10,11... | collective-permute-start | bytes 1572872 | tf_op jit(solution)/shard_map/ppermute | solution.py:41
  118.4 1.5 collective-permute-done.2
  120.0 38.7 %all_to_all.48 = bf16[8,32,512]{2,1,0:T(8,128)(2,1)S(1)} all-to-all(bf16[8,32,512]{2,1,0:T(8,128)(2,1)S(1)} %bitcast.73), channel_id=1, replica_groups=mesh['x'=4,'y'=8,'z'=8,'core'=2] {'z'}, dimensions={0} | all-to-all | bytes 524288 | tf_op jit(solution)/shard_map/all_to_all | solution.py:28
  158.8 0.7 broadcast_in_dim.64
  159.5 3.4 %all-to-all-start.6 = ((f32[4,1,32,512]{3,2,1,0:T(8,128)}), f32[4,1,32,512]{3,2,1,0:T(8,128)S(1)}, u32[]{:S(2)}, u32[]{:S(2)}) async-start(f32[4,1,32,512]{3,2,1,0:T(8,128)} %broadcast_in_dim.64), calls=%async_computation.6 | async-start | bytes 524288 | tf_op jit(solution)/shard_map/all_to_all | solution.py:36
  162.9 3.9 %collective-permute-start.3 = (bf16[32,512]{1,0:T(8,128)(2,1)S(1)}, bf16[32,512]{1,0:T(8,128)(2,1)S(1)}, u32[]{:S(2)}, u32[]{:S(2)}) collective-permute-start(bf16[32,512]{1,0:T(8,128)(2,1)S(1)} %reduce_sum.92), channel_id=1, source_target_pairs={{0,0},{128,1},{16,2},{144,3},{32,4},{160,5},{48,6},{176,7},{64,8},... | collective-permute-start | bytes 98312 | tf_op jit(solution)/shard_map/ppermute | solution.py:177
  166.8 1.6 all-to-all-done.6
  168.5 1.5 collective-permute-done.3
  170.1 27.1 %all_to_all.49 = bf16[8,72,512]{2,1,0:T(8,128)(2,1)S(1)} all-to-all(bf16[8,72,512]{2,1,0:T(8,128)(2,1)S(1)} %broadcast_in_dim.67), channel_id=1, replica_groups=mesh['x'=4,'y'=8,'z'=8,'core'=2] {'z'}, dimensions={0} | all-to-all | bytes 1179648 | tf_op jit(solution)/shard_map/all_to_all | solution.py:36
  197.2 4.5 %collective-permute-start.4 = (bf16[576,512]{1,0:T(8,128)(2,1)S(1)}, bf16[576,512]{1,0:T(8,128)(2,1)S(1)}, u32[]{:S(2)}, u32[]{:S(2)}) collective-permute-start(bf16[576,512]{1,0:T(8,128)(2,1)S(1)} %bitcast.69), channel_id=1, source_target_pairs={{0,1},{1,0},{2,3},{3,2},{4,5},{5,4},{6,7},{7,6},{8,9},{9,8},{10,11... | collective-permute-start | bytes 1769480 | tf_op jit(solution)/shard_map/ppermute | solution.py:41
  201.8 1.1 broadcast_in_dim.70
  202.9 4.2 %all-to-all-start.8 = ((bf16[4,256,512]{2,1,0:T(8,128)(2,1)}), bf16[4,256,512]{2,1,0:T(8,128)(2,1)}, u32[]{:S(2)}, u32[]{:S(2)}) async-start(bf16[4,256,512]{2,1,0:T(8,128)(2,1)} %broadcast_in_dim.70), calls=%async_computation.8 | async-start | bytes 2097152 | tf_op jit(solution)/shard_map/all_to_all | solution.py:36
  207.8 1.1 fusion.20
  208.9 1.1 abs_reduce_fusion.1
  210.0 1.1 convolution_add_fusion.5
  211.1 1.0 convolution_add_fusion.4
  212.2 1.0 convolution_add_fusion.3
  213.2 0.6 reduce_max.18
  213.8 0.7 while.14
  214.5 1.0 fusion.45
  215.6 1.0 convolution_add_fusion.2
  216.6 0.4 fusion.46
  217.0 0.4 convolution_add_fusion.1
  217.5 1.8 convolution_add_fusion.solved_ref
  219.3 3.1 %all-to-all-done.8 = bf16[4,256,512]{2,1,0:T(8,128)(2,1)} async-done(((bf16[4,256,512]{2,1,0:T(8,128)(2,1)}), bf16[4,256,512]{2,1,0:T(8,128)(2,1)}, u32[]{:S(2)}, u32[]{:S(2)}) %all-to-all-start.8) | async-done | bytes 1048608 | tf_op jit(solution)/shard_map/all_to_all | solution.py:36
  222.4 6.1 %add_product.1 = f32[512,1024]{1,0:T(8,128)} custom-call(f32[512,1024]{1,0:T(8,128)} %inverse_ref.1, f32[512,512]{1,0:T(8,128)} %convolution_add_fusion.solved_ref, bf16[1024,512]{1,0:T(8,128)(2,1)} %bitcast.18.images_ref), custom_call_target="tpu_custom_call" | custom-call | flops 1073741824 | bytes 6291456 | tf_op jit(solution)/shard_map/add_product/pallas_call | solution.py:113
  (30 shorter events, 1.2 us)
Async XLA Ops:
  0.0 1.0 copy-start
  1.0 45.9 %copy-start.1 = (f32[512,1024]{1,0:T(8,128)S(1)}, f32[512,1024]{1,0:T(8,128)}, u32[]{:S(2)}) copy-start(f32[512,1024]{1,0:T(8,128)} %inverse_ref.1) | copy-start | bytes 6291460
  1.4 10.2 %collective-permute-start = (bf16[256,512]{1,0:T(8,128)(2,1)S(1)}, bf16[256,512]{1,0:T(8,128)(2,1)}, u32[]{:S(2)}, u32[]{:S(2)}) collective-permute-start(bf16[256,512]{1,0:T(8,128)(2,1)S(1)} %dynamic-slice_bitcast_fusion), channel_id=1, source_target_pairs={{0,1},{1,0},{2,3},{3,2},{4,5},{5,4},{6,7},{7,6},{8,9},{9,8},{10,11... | collective-permute-start | bytes 786440 | tf_op jit(solution)/shard_map/ppermute | solution.py:41
  28.9 13.1 %all-to-all-start.1 = ((bf16[8,32,512]{2,1,0:T(8,128)(2,1)}), bf16[8,32,512]{2,1,0:T(8,128)(2,1)S(1)}, u32[]{:S(2)}, u32[]{:S(2)}) async-start(bf16[8,32,512]{2,1,0:T(8,128)(2,1)} %broadcast_in_dim.60), calls=%async_computation.1 | async-start | bytes 524288 | tf_op jit(solution)/shard_map/all_to_all | solution.py:36
  46.9 0.9 copy-start.2
  83.5 23.9 %all-to-all-start.4 = ((bf16[8,32,512]{2,1,0:T(8,128)(2,1)}), bf16[8,32,512]{2,1,0:T(8,128)(2,1)S(1)}, u32[]{:S(2)}, u32[]{:S(2)}) async-start(bf16[8,32,512]{2,1,0:T(8,128)(2,1)} %broadcast_in_dim.63), calls=%async_computation.4 | async-start | bytes 524288 | tf_op jit(solution)/shard_map/all_to_all | solution.py:36
  86.9 20.5 %collective-permute-start.1 = (bf16[256,512]{1,0:T(8,128)(2,1)S(1)}, bf16[256,512]{1,0:T(8,128)(2,1)S(1)}, u32[]{:S(2)}, u32[]{:S(2)}) collective-permute-start(bf16[256,512]{1,0:T(8,128)(2,1)S(1)} %bitcast.72), channel_id=1, source_target_pairs={{0,0},{1,128},{2,16},{3,144},{4,32},{5,160},{6,48},{7,176},{8,64},... | collective-permute-start | bytes 786440 | tf_op jit(solution)/shard_map/ppermute | solution.py:149
  108.1 11.8 %collective-permute-start.2 = (f32[256,512]{1,0:T(8,128)S(1)}, f32[256,512]{1,0:T(8,128)S(1)}, u32[]{:S(2)}, u32[]{:S(2)}) collective-permute-start(f32[256,512]{1,0:T(8,128)S(1)} %constant_dynamic-slice_fusion), channel_id=1, source_target_pairs={{0,1},{1,0},{2,3},{3,2},{4,5},{5,4},{6,7},{7,6},{8,9},{9,8},{10,11... | collective-permute-start | bytes 1572872 | tf_op jit(solution)/shard_map/ppermute | solution.py:41
  159.5 8.9 %all-to-all-start.6 = ((f32[4,1,32,512]{3,2,1,0:T(8,128)}), f32[4,1,32,512]{3,2,1,0:T(8,128)S(1)}, u32[]{:S(2)}, u32[]{:S(2)}) async-start(f32[4,1,32,512]{3,2,1,0:T(8,128)} %broadcast_in_dim.64), calls=%async_computation.6 | async-start | bytes 524288 | tf_op jit(solution)/shard_map/all_to_all | solution.py:36
  162.9 7.1 %collective-permute-start.3 = (bf16[32,512]{1,0:T(8,128)(2,1)S(1)}, bf16[32,512]{1,0:T(8,128)(2,1)S(1)}, u32[]{:S(2)}, u32[]{:S(2)}) collective-permute-start(bf16[32,512]{1,0:T(8,128)(2,1)S(1)} %reduce_sum.92), channel_id=1, source_target_pairs={{0,0},{128,1},{16,2},{144,3},{32,4},{160,5},{48,6},{176,7},{64,8},... | collective-permute-start | bytes 98312 | tf_op jit(solution)/shard_map/ppermute | solution.py:177
  197.2 9.9 %collective-permute-start.4 = (bf16[576,512]{1,0:T(8,128)(2,1)S(1)}, bf16[576,512]{1,0:T(8,128)(2,1)S(1)}, u32[]{:S(2)}, u32[]{:S(2)}) collective-permute-start(bf16[576,512]{1,0:T(8,128)(2,1)S(1)} %bitcast.69), channel_id=1, source_target_pairs={{0,1},{1,0},{2,3},{3,2},{4,5},{5,4},{6,7},{7,6},{8,9},{9,8},{10,11... | collective-permute-start | bytes 1769480 | tf_op jit(solution)/shard_map/ppermute | solution.py:41
  202.9 19.5 %all-to-all-start.8 = ((bf16[4,256,512]{2,1,0:T(8,128)(2,1)}), bf16[4,256,512]{2,1,0:T(8,128)(2,1)}, u32[]{:S(2)}, u32[]{:S(2)}) async-start(bf16[4,256,512]{2,1,0:T(8,128)(2,1)} %broadcast_in_dim.70), calls=%async_computation.8 | async-start | bytes 2097152 | tf_op jit(solution)/shard_map/all_to_all | solution.py:36
  208.9 1.1 copy-start.3

commit v4 on v2

--- a/solution.py
+++ b/solution.py
@@ -17,6 +17,7 @@
 BF16 = jnp.bfloat16
 SMALL = 2.0**-1.5
 MAX_FACTORS = 48
+PAD = 8
 
 
 def spread(x, axis, parts):
@@ -70,7 +71,7 @@
 
 
 def solve_rows(start, square):
-    def dot(a, b, precision=lax.Precision.HIGHEST):
+    def dot(a, b, precision=lax.Precision.HIGH):
         return jnp.dot(a, b, precision=precision, preferred_element_type=F32)
 
     def norm(power):
@@ -90,7 +91,7 @@
         power = dot(power, power)
         total = total + dot(total, power)
     total, power, _, _ = lax.while_loop(more, step, (total, power, norm(power), jnp.int32(0)))
-    for precision in (lax.Precision.HIGH, lax.Precision.HIGH, lax.Precision.DEFAULT):
+    for precision in (lax.Precision.HIGH, lax.Precision.DEFAULT, lax.Precision.DEFAULT):
         power = dot(power, power, precision)
         total = total + dot(total, power, precision)
     return total
@@ -111,8 +112,9 @@
         activations, onehot, (((0,), (0,)), ((), ())), preferred_element_type=F32
     ).astype(BF16)
     piece = scatter_sum(fold_cores(picked), "z", NZ).astype(BF16)
+    half = gather(piece, "z", NZ)
     piece_by_columns = lax.ppermute(piece, AXES, to_columns)
-    rows_here = join_cores(gather(piece, "z", NZ))
+    rows_here = lax.all_gather(half, "core", axis=0, tiled=True)
 
     row_number = wide * height + lax.broadcasted_iota(jnp.int32, inverse.shape, 0)
     col_number = narrow * width + lax.broadcasted_iota(jnp.int32, inverse.shape, 1)
@@ -136,26 +138,37 @@
     share = scatter_sum(fold_cores(share * BETA).astype(BF16), "z", NZ)
     share = jnp.sum(gather(share[None], "x", NX), axis=0)
 
+    n = share.shape[0]
+    own = (core * NZ + z) * n + lax.broadcasted_iota(jnp.int32, share.shape, 0)
+    on_diagonal = own == lax.broadcasted_iota(jnp.int32, share.shape, 1)
+    high, low = exact_pair(share)
+    low = jnp.sum(jnp.where(on_diagonal, low.astype(F32), 0.0), axis=0, keepdims=True)
+    low = jnp.pad(low, ((0, PAD - 1), (0, 0))).astype(BF16)
     change_there = lax.ppermute(change, AXES, to_rows)
-    gathered = gather(jnp.concatenate(exact_pair(share) + (change_there,), axis=0), "z", NZ)
+    gathered = gather(jnp.concatenate([high, low, change_there], axis=0), "z", NZ)
     mine, other = gathered, swap(gathered)
     first = core == 0
     halves = [jnp.where(first, mine, other), jnp.where(first, other, mine)]
     halves = [h.reshape(NZ, -1, h.shape[1]).astype(F32) for h in halves]
-    n = share.shape[0]
-    scaled = [(h[:, :n] + h[:, n : 2 * n]).reshape(-1, h.shape[2]) for h in halves]
-    scaled = jnp.concatenate(scaled, axis=0)
-    change_here = [h[:, 2 * n :].reshape(-1, h.shape[2]) for h in halves]
+    scaled = jnp.concatenate([h[:, :n].reshape(-1, h.shape[2]) for h in halves], axis=0)
+    low = jnp.sum(halves[0][:, n] + halves[1][:, n], axis=0)
+    diagonal = lax.broadcasted_iota(jnp.int32, scaled.shape, 0) == lax.broadcasted_iota(
+        jnp.int32, scaled.shape, 1
+    )
+    scaled = scaled + jnp.where(diagonal, low[None], 0.0)
+    change_here = [h[:, n + PAD :].reshape(-1, h.shape[2]) for h in halves]
     change_here = jnp.concatenate(change_here, axis=0)
     images_rows = rows_here.astype(F32) + change_here
     images_cols = gather((rows_cols.astype(F32) + change_cols.astype(F32)).astype(BF16), "x", NX)
 
     solved = solve_rows(images_rows * BETA, scaled)
-    update = sum(
-        lax.dot_general(term, images_cols, (((1,), (1,)), ((), ())), preferred_element_type=F32)
-        for term in exact_pair(solved)
+    return inverse + lax.dot_general(
+        solved,
+        images_cols.astype(F32),
+        (((1,), (1,)), ((), ())),
+        precision=lax.Precision.HIGH,
+        preferred_element_type=F32,
     )
-    return inverse + update
 
 
 def solution(mesh):

time: 204 us -> 197 us (0.966)
  blocking collectives: 112 us -> 99.7 us
  waiting for transfers between devices: 12.3 us -> 20.8 us
  matrix products: 22.3 us -> 19.5 us
  starting transfers between devices: 49.8 us -> 47.7 us
    all_to_all x3 -> x2, blocking collectives: 63.2 us -> 46.5 us  [gather(): lax.all_to_all(jnp.broadcast_to(x[None], (parts,) + x.shape), axis, 0, 0,...]
    all_to_all x2 -> x3, waiting for transfers between devices: 3 us -> 12.6 us  [gather(): lax.all_to_all(jnp.broadcast_to(x[None], (parts,) + x.shape), axis, 0, 0,...]
    all_gather x0 -> x1, blocking collectives: none -> 4.86 us  [on_device(): rows_here = lax.all_gather(half, 'core', axis=0, tiled=True)]
    ppermute x4 -> x3, starting transfers between devices: 27.5 us -> 22.9 us  [swap(): return lax.ppermute(x, 'core', [(0, 1), (1, 0)])]
    all_to_all x2 -> x3, starting transfers between devices: 8.61 us -> 11.1 us  [gather(): lax.all_to_all(jnp.broadcast_to(x[None], (parts,) + x.shape), axis, 0, 0,...]
    dot_general x2 -> x1, matrix products: 5.42 us -> 3.84 us  [on_device(): lax.dot_general(solved, images_cols.astype(F32), (((1,), (1,)), ((), ()))...]
where the time goes in v4:
time: 197 us; the launch traced here: 196 us
  blocking collectives  99.7 us (51%)
  starting transfers between devices  47.7 us (24%)
  waiting for transfers between devices  20.8 us (11%)
  matrix products  19.5 us (10%)
  local copies, waits for them, and re-layouts  3.95 us (2%)
  other arithmetic  3.17 us (2%)
    all_to_all x3, blocking collectives, spread(): return lax.all_to_all(x, axis, 0, 0, tiled=True)  48.3 us
    all_to_all x2, blocking collectives, gather(): lax.all_to_all(jnp.broadcast_to(x[None], (parts,) + x.shape), axis, 0, 0,...  46.5 us
    ppermute x3, starting transfers between devices, swap(): return lax.ppermute(x, 'core', [(0, 1), (1, 0)])  22.9 us
    dot_general x10, matrix products, dot(): return jnp.dot(a, b, precision=precision, preferred_element_type=F32)  13 us
    all_to_all x3, waiting for transfers between devices, gather(): lax.all_to_all(jnp.broadcast_to(x[None], (parts,) + x.shape), axis, 0, 0,...  12.6 us
    all_to_all x3, starting transfers between devices, gather(): lax.all_to_all(jnp.broadcast_to(x[None], (parts,) + x.shape), axis, 0, 0,...  11.1 us
    all_to_all x1, starting transfers between devices, spread(): return lax.all_to_all(x, axis, 0, 0, tiled=True)  6.82 us
    all_to_all x1, waiting for transfers between devices, spread(): return lax.all_to_all(x, axis, 0, 0, tiled=True)  5.07 us
  transfers between devices with their start and end apart: 9, of which 6 were waited for; matrix products, arithmetic and copies ran while one was open for 8% of the time, Pallas kernels for 0%

profile of v4, /device:TPU:1, one launch (start us, length us, event | category | flops | bytes accessed | tf_op | source)
XLA Modules:
  0.0 195.9 jit_solution(2236093282195487478)
XLA Ops:
  0.0 0.7 broadcast_subtract_fusion
  0.7 0.2 copy-done
  1.0 0.4 convolution_convert_fusion
  1.4 8.9 %collective-permute-start = (bf16[256,512]{1,0:T(8,128)(2,1)S(1)}, bf16[256,512]{1,0:T(8,128)(2,1)S(1)}, u32[]{:S(2)}, u32[]{:S(2)}) collective-permute-start(bf16[256,512]{1,0:T(8,128)(2,1)S(1)} %dynamic-slice_bitcast_fusion), channel_id=1, source_target_pairs={{0,1},{1,0},{2,3},{3,2},{4,5},{5,4},{6,7},{7,6},{8,9},{9,8},{10,11... | collective-permute-start | bytes 786440 | tf_op jit(solution)/shard_map/ppermute | solution.py:38
  10.3 1.1 collective-permute-done
  11.5 15.6 %all_to_all.45 = bf16[8,32,512]{2,1,0:T(8,128)(2,1)S(1)} all-to-all(bf16[8,32,512]{2,1,0:T(8,128)(2,1)S(1)} %bitcast.98), channel_id=1, replica_groups=mesh['x'=4,'y'=8,'z'=8,'core'=2] {'z'}, dimensions={0} | all-to-all | bytes 524288 | tf_op jit(solution)/shard_map/all_to_all | solution.py:25
  27.1 0.7 broadcast_in_dim.60
  27.8 3.4 %all-to-all-start.1 = ((bf16[8,32,512]{2,1,0:T(8,128)(2,1)}), bf16[8,32,512]{2,1,0:T(8,128)(2,1)S(1)}, u32[]{:S(2)}, u32[]{:S(2)}) async-start(bf16[8,32,512]{2,1,0:T(8,128)(2,1)} %broadcast_in_dim.60), calls=%async_computation.1 | async-start | bytes 524288 | tf_op jit(solution)/shard_map/all_to_all | solution.py:33
  31.3 9.6 %all-to-all-done.1 = bf16[8,32,512]{2,1,0:T(8,128)(2,1)S(1)} async-done(((bf16[8,32,512]{2,1,0:T(8,128)(2,1)}), bf16[8,32,512]{2,1,0:T(8,128)(2,1)S(1)}, u32[]{:S(2)}, u32[]{:S(2)}) %all-to-all-start.1) | async-done | bytes 262176 | tf_op jit(solution)/shard_map/all_to_all | solution.py:33
  40.9 4.9 %all_gather.3 = bf16[512,512]{1,0:T(8,128)(2,1)S(1)} all-gather(bf16[256,512]{1,0:T(8,128)(2,1)S(1)} %bitcast.95), channel_id=1, replica_groups=mesh['x'=4,'y'=8,'z'=8,'core'=2] {'core'}, dimensions={0}, use_global_device_ids=true | all-gather | bytes 786432 | tf_op jit(solution)/shard_map/all_gather | solution.py:117
  45.8 0.8 fusion.7
  46.6 0.8 add_convert_fusion
  47.5 18.1 %all_to_all.46 = bf16[4,256,512]{2,1,0:T(8,128)(2,1)S(1)} all-to-all(bf16[4,256,512]{2,1,0:T(8,128)(2,1)S(1)} %bitcast.97), channel_id=1, replica_groups=mesh['x'=4,'y'=8,'z'=8,'core'=2] {'x'}, dimensions={0} | all-to-all | bytes 2097152 | tf_op jit(solution)/shard_map/all_to_all | solution.py:25
  65.5 0.9 reduce_sum.91
  66.4 6.8 %all-to-all-start.3 = ((bf16[8,32,512]{2,1,0:T(8,128)(2,1)}), bf16[8,32,512]{2,1,0:T(8,128)(2,1)S(1)}, u32[]{:S(2)}, u32[]{:S(2)}) async-start(bf16[8,32,512]{2,1,0:T(8,128)(2,1)} %bitcast.6), calls=%async_computation.3 | async-start | bytes 524288 | tf_op jit(solution)/shard_map/all_to_all | solution.py:25
  73.3 4.2 %collective-permute-start.1 = (bf16[32,512]{1,0:T(8,128)(2,1)S(1)}, bf16[32,512]{1,0:T(8,128)(2,1)S(1)}, u32[]{:S(2)}, u32[]{:S(2)}) collective-permute-start(bf16[32,512]{1,0:T(8,128)(2,1)S(1)} %reduce_sum.90), channel_id=1, source_target_pairs={{0,0},{1,128},{2,16},{3,144},{4,32},{5,160},{6,48},{7,176},{8,64},... | collective-permute-start | bytes 98312 | tf_op jit(solution)/shard_map/ppermute | solution.py:116
  77.4 5.1 %all-to-all-done.3 = bf16[8,32,512]{2,1,0:T(8,128)(2,1)S(1)} async-done(((bf16[8,32,512]{2,1,0:T(8,128)(2,1)}), bf16[8,32,512]{2,1,0:T(8,128)(2,1)S(1)}, u32[]{:S(2)}, u32[]{:S(2)}) %all-to-all-start.3) | async-done | bytes 262176 | tf_op jit(solution)/shard_map/all_to_all | solution.py:25
  82.6 21.6 %all_to_all.47 = bf16[8,64,512]{2,1,0:T(8,128)(2,1)S(1)} all-to-all(bf16[8,64,512]{2,1,0:T(8,128)(2,1)S(1)} %broadcast_in_dim.63), channel_id=1, replica_groups=mesh['x'=4,'y'=8,'z'=8,'core'=2] {'y'}, dimensions={0} | all-to-all | bytes 1048576 | tf_op jit(solution)/shard_map/all_to_all | solution.py:33
  104.2 0.3 convolution_bitcast_fusion.1
  104.6 0.3 fusion.5
  104.9 8.0 %collective-permute-start.2 = (f32[256,512]{1,0:T(8,128)S(1)}, f32[256,512]{1,0:T(8,128)S(1)}, u32[]{:S(2)}, u32[]{:S(2)}) collective-permute-start(f32[256,512]{1,0:T(8,128)S(1)} %constant_dynamic-slice_fusion), channel_id=1, source_target_pairs={{0,1},{1,0},{2,3},{3,2},{4,5},{5,4},{6,7},{7,6},{8,9},{9,8},{10,11... | collective-permute-start | bytes 1572872 | tf_op jit(solution)/shard_map/ppermute | solution.py:38
  113.0 1.5 collective-permute-done.2
  114.6 14.7 %all_to_all.48 = bf16[8,32,512]{2,1,0:T(8,128)(2,1)S(1)} all-to-all(bf16[8,32,512]{2,1,0:T(8,128)(2,1)S(1)} %bitcast.96), channel_id=1, replica_groups=mesh['x'=4,'y'=8,'z'=8,'core'=2] {'z'}, dimensions={0} | all-to-all | bytes 524288 | tf_op jit(solution)/shard_map/all_to_all | solution.py:25
  129.3 0.7 broadcast_in_dim.64
  130.0 4.2 %all-to-all-start.6 = ((f32[4,1,32,512]{3,2,1,0:T(8,128)}), f32[4,1,32,512]{3,2,1,0:T(8,128)S(1)}, u32[]{:S(2)}, u32[]{:S(2)}) async-start(f32[4,1,32,512]{3,2,1,0:T(8,128)} %broadcast_in_dim.64), calls=%async_computation.6 | async-start | bytes 524288 | tf_op jit(solution)/shard_map/all_to_all | solution.py:33
  134.2 2.7 %collective-permute-start.3 = (bf16[32,512]{1,0:T(8,128)(2,1)S(1)}, bf16[32,512]{1,0:T(8,128)(2,1)S(1)}, u32[]{:S(2)}, u32[]{:S(2)}) collective-permute-start(bf16[32,512]{1,0:T(8,128)(2,1)S(1)} %reduce_sum.92), channel_id=1, source_target_pairs={{0,0},{128,1},{16,2},{144,3},{32,4},{160,5},{48,6},{176,7},{64,8},... | collective-permute-start | bytes 98312 | tf_op jit(solution)/shard_map/ppermute | solution.py:147
  136.9 3.0 %all-to-all-done.6 = f32[4,1,32,512]{3,2,1,0:T(8,128)S(1)} async-done(((f32[4,1,32,512]{3,2,1,0:T(8,128)}), f32[4,1,32,512]{3,2,1,0:T(8,128)S(1)}, u32[]{:S(2)}, u32[]{:S(2)}) %all-to-all-start.6) | async-done | bytes 262176 | tf_op jit(solution)/shard_map/all_to_all | solution.py:33
  140.0 0.4 collective-permute-done.3
  140.5 24.9 %all_to_all.49 = bf16[8,72,512]{2,1,0:T(8,128)(2,1)S(1)} all-to-all(bf16[8,72,512]{2,1,0:T(8,128)(2,1)S(1)} %broadcast_in_dim.67), channel_id=1, replica_groups=mesh['x'=4,'y'=8,'z'=8,'core'=2] {'z'}, dimensions={0} | all-to-all | bytes 1179648 | tf_op jit(solution)/shard_map/all_to_all | solution.py:33
  165.4 6.0 %collective-permute-start.4 = (bf16[576,512]{1,0:T(8,128)(2,1)S(1)}, bf16[576,512]{1,0:T(8,128)(2,1)S(1)}, u32[]{:S(2)}, u32[]{:S(2)}) collective-permute-start(bf16[576,512]{1,0:T(8,128)(2,1)S(1)} %bitcast.90), channel_id=1, source_target_pairs={{0,1},{1,0},{2,3},{3,2},{4,5},{5,4},{6,7},{7,6},{8,9},{9,8},{10,11... | collective-permute-start | bytes 1769480 | tf_op jit(solution)/shard_map/ppermute | solution.py:38
  171.4 1.1 broadcast_in_dim.70
  172.5 3.5 %all-to-all-start.8 = ((bf16[4,256,512]{2,1,0:T(8,128)(2,1)}), bf16[4,256,512]{2,1,0:T(8,128)(2,1)S(1)}, u32[]{:S(2)}, u32[]{:S(2)}) async-start(bf16[4,256,512]{2,1,0:T(8,128)(2,1)} %broadcast_in_dim.70), calls=%async_computation.8 | async-start | bytes 2097152 | tf_op jit(solution)/shard_map/all_to_all | solution.py:33
  176.3 0.1 convert.12
  176.6 0.1 convert.11
  176.8 1.1 fusion.21
  177.8 1.1 abs_reduce_fusion.1
  178.9 1.1 convolution_add_fusion.6
  180.0 1.0 convolution_add_fusion.5
  181.1 1.0 convolution_add_fusion.4
  182.1 0.6 reduce_max.18
  182.7 0.8 while.14
  183.5 1.0 fusion.51
  184.5 1.0 convolution_add_fusion.3
  185.5 0.4 fusion.52
  186.0 0.8 copy-done.3
  186.8 1.4 convolution_add_fusion.2
  188.2 3.8 %convolution_add_fusion.1 = f32[512,512]{1,0:T(8,128)} fusion(f32[512,512]{1,0:T(8,128)} %convolution_add_fusion.2, bf16[512,512]{1,0:T(8,128)(2,1)} %copy-done.3), kind=kOutput, calls=%fused_computation.9 | convolution fusion | flops 537133056 | bytes 2621440 | tf_op jit(solution)/shard_map/dot_general | solution.py:75
  192.0 3.8 %convolution_add_fusion = f32[512,1024]{1,0:T(8,128)} fusion(f32[512,1024]{1,0:T(8,128)S(1)} %copy-done.2, f32[512,512]{1,0:T(8,128)} %convolution_add_fusion.1, bf16[1024,512]{1,0:T(8,128)(2,1)S(1)} %bitcast.89), kind=kOutput, calls=%fused_computation.8 | convolution fusion | flops 1611137024 | bytes 6291456 | tf_op jit(solution)/shard_map/dot_general | solution.py:165
  (31 shorter events, 1.1 us)
Async XLA Ops:
  0.0 1.0 copy-start
  1.0 44.8 %copy-start.1 = (f32[512,1024]{1,0:T(8,128)S(1)}, f32[512,1024]{1,0:T(8,128)}, u32[]{:S(2)}) copy-start(f32[512,1024]{1,0:T(8,128)} %param.5) | copy-start | bytes 6291460
  1.4 10.0 %collective-permute-start = (bf16[256,512]{1,0:T(8,128)(2,1)S(1)}, bf16[256,512]{1,0:T(8,128)(2,1)S(1)}, u32[]{:S(2)}, u32[]{:S(2)}) collective-permute-start(bf16[256,512]{1,0:T(8,128)(2,1)S(1)} %dynamic-slice_bitcast_fusion), channel_id=1, source_target_pairs={{0,1},{1,0},{2,3},{3,2},{4,5},{5,4},{6,7},{7,6},{8,9},{9,8},{10,11... | collective-permute-start | bytes 786440 | tf_op jit(solution)/shard_map/ppermute | solution.py:38
  27.8 13.1 %all-to-all-start.1 = ((bf16[8,32,512]{2,1,0:T(8,128)(2,1)}), bf16[8,32,512]{2,1,0:T(8,128)(2,1)S(1)}, u32[]{:S(2)}, u32[]{:S(2)}) async-start(bf16[8,32,512]{2,1,0:T(8,128)(2,1)} %broadcast_in_dim.60), calls=%async_computation.1 | async-start | bytes 524288 | tf_op jit(solution)/shard_map/all_to_all | solution.py:33
  66.4 16.1 %all-to-all-start.3 = ((bf16[8,32,512]{2,1,0:T(8,128)(2,1)}), bf16[8,32,512]{2,1,0:T(8,128)(2,1)S(1)}, u32[]{:S(2)}, u32[]{:S(2)}) async-start(bf16[8,32,512]{2,1,0:T(8,128)(2,1)} %bitcast.6), calls=%async_computation.3 | async-start | bytes 524288 | tf_op jit(solution)/shard_map/all_to_all | solution.py:25
  73.3 9.3 %collective-permute-start.1 = (bf16[32,512]{1,0:T(8,128)(2,1)S(1)}, bf16[32,512]{1,0:T(8,128)(2,1)S(1)}, u32[]{:S(2)}, u32[]{:S(2)}) collective-permute-start(bf16[32,512]{1,0:T(8,128)(2,1)S(1)} %reduce_sum.90), channel_id=1, source_target_pairs={{0,0},{1,128},{2,16},{3,144},{4,32},{5,160},{6,48},{7,176},{8,64},... | collective-permute-start | bytes 98312 | tf_op jit(solution)/shard_map/ppermute | solution.py:116
  104.9 9.6 %collective-permute-start.2 = (f32[256,512]{1,0:T(8,128)S(1)}, f32[256,512]{1,0:T(8,128)S(1)}, u32[]{:S(2)}, u32[]{:S(2)}) collective-permute-start(f32[256,512]{1,0:T(8,128)S(1)} %constant_dynamic-slice_fusion), channel_id=1, source_target_pairs={{0,1},{1,0},{2,3},{3,2},{4,5},{5,4},{6,7},{7,6},{8,9},{9,8},{10,11... | collective-permute-start | bytes 1572872 | tf_op jit(solution)/shard_map/ppermute | solution.py:38
  130.0 9.9 %all-to-all-start.6 = ((f32[4,1,32,512]{3,2,1,0:T(8,128)}), f32[4,1,32,512]{3,2,1,0:T(8,128)S(1)}, u32[]{:S(2)}, u32[]{:S(2)}) async-start(f32[4,1,32,512]{3,2,1,0:T(8,128)} %broadcast_in_dim.64), calls=%async_computation.6 | async-start | bytes 524288 | tf_op jit(solution)/shard_map/all_to_all | solution.py:33
  134.2 6.2 %collective-permute-start.3 = (bf16[32,512]{1,0:T(8,128)(2,1)S(1)}, bf16[32,512]{1,0:T(8,128)(2,1)S(1)}, u32[]{:S(2)}, u32[]{:S(2)}) collective-permute-start(bf16[32,512]{1,0:T(8,128)(2,1)S(1)} %reduce_sum.92), channel_id=1, source_target_pairs={{0,0},{128,1},{16,2},{144,3},{32,4},{160,5},{48,6},{176,7},{64,8},... | collective-permute-start | bytes 98312 | tf_op jit(solution)/shard_map/ppermute | solution.py:147
  165.4 10.7 %collective-permute-start.4 = (bf16[576,512]{1,0:T(8,128)(2,1)S(1)}, bf16[576,512]{1,0:T(8,128)(2,1)S(1)}, u32[]{:S(2)}, u32[]{:S(2)}) collective-permute-start(bf16[576,512]{1,0:T(8,128)(2,1)S(1)} %bitcast.90), channel_id=1, source_target_pairs={{0,1},{1,0},{2,3},{3,2},{4,5},{5,4},{6,7},{7,6},{8,9},{9,8},{10,11... | collective-permute-start | bytes 1769480 | tf_op jit(solution)/shard_map/ppermute | solution.py:38
  172.5 19.5 %all-to-all-start.8 = ((bf16[4,256,512]{2,1,0:T(8,128)(2,1)}), bf16[4,256,512]{2,1,0:T(8,128)(2,1)S(1)}, u32[]{:S(2)}, u32[]{:S(2)}) async-start(bf16[4,256,512]{2,1,0:T(8,128)(2,1)} %broadcast_in_dim.70), calls=%async_computation.8 | async-start | bytes 2097152 | tf_op jit(solution)/shard_map/all_to_all | solution.py:33
  186.0 0.8 copy-start.3
  188.2 3.8 %copy-start.2 = (f32[512,1024]{1,0:T(8,128)S(1)}, f32[512,1024]{1,0:T(8,128)}, u32[]{:S(2)}) copy-start(f32[512,1024]{1,0:T(8,128)} %param.5) | copy-start | bytes 6291460

commit v5 on v4

--- a/solution.py
+++ b/solution.py
@@ -15,9 +15,10 @@
 NX, NY, NZ, NC = 4, 8, 8, 2
 F32 = jnp.float32
 BF16 = jnp.bfloat16
-SMALL = 2.0**-1.5
+SMALL = 2.0**-6
 MAX_FACTORS = 48
 PAD = 8
+SLOTS = 96
 
 
 def spread(x, axis, parts):
@@ -87,14 +88,53 @@
         return total, power, norm(power), count + 1
 
     total, power = start + dot(start, square), square
-    for _ in range(2):
+    for _ in range(3):
         power = dot(power, power)
         total = total + dot(total, power)
     total, power, _, _ = lax.while_loop(more, step, (total, power, norm(power), jnp.int32(0)))
-    for precision in (lax.Precision.HIGH, lax.Precision.DEFAULT, lax.Precision.DEFAULT):
-        power = dot(power, power, precision)
-        total = total + dot(total, power, precision)
+    power = dot(power, power, lax.Precision.DEFAULT)
+    total = total + dot(total, power, lax.Precision.DEFAULT)
     return total
+
+
+def forgotten_half(activations, forget):
+    z, core = lax.axis_index("z"), lax.axis_index("core")
+    stored_here, features = activations.shape
+    rows = forget.shape[0]
+    first_here = (z * NC + core) * stored_here
+    chip = forget // (NC * stored_here)
+
+    earlier = lax.broadcasted_iota(jnp.int32, (rows, rows), 0) < lax.broadcasted_iota(
+        jnp.int32, (rows, rows), 1
+    )
+    rank = jnp.sum((earlier & (chip[:, None] == chip[None, :])).astype(jnp.int32), axis=0)
+
+    def onehot(places, numbers):
+        return (jnp.arange(places, dtype=jnp.int32)[:, None] == numbers[None, :]).astype(BF16)
+
+    def by_slots(activations):
+        here = onehot(stored_here, forget - first_here)
+        slot = onehot(SLOTS, jnp.where(chip == z, rank, -1))
+        chosen = lax.dot_general(
+            slot, here, (((1,), (1,)), ((), ())), preferred_element_type=F32
+        ).astype(BF16)
+        picked = jnp.dot(chosen, activations, preferred_element_type=F32).astype(BF16)
+        there = lax.dynamic_slice_in_dim(picked, (1 - core) * (features // NC), features // NC, 1)
+        mine = lax.dynamic_slice_in_dim(picked, core * (features // NC), features // NC, 1)
+        slots = gather(mine + swap(there), "z", NZ)
+        order = onehot(NZ * SLOTS, chip * SLOTS + rank)
+        return lax.dot_general(
+            slots, order, (((0,), (0,)), ((), ())), preferred_element_type=F32
+        ).astype(BF16)
+
+    def by_sums(activations):
+        here = onehot(stored_here, forget - first_here)
+        picked = lax.dot_general(
+            activations, here, (((0,), (0,)), ((), ())), preferred_element_type=F32
+        ).astype(BF16)
+        return gather(scatter_sum(fold_cores(picked), "z", NZ).astype(BF16), "z", NZ)
+
+    return lax.cond(jnp.max(rank) < SLOTS, by_slots, by_sums, activations)
 
 
 def on_device(inverse, activations, forget):
@@ -102,17 +142,11 @@
     z, core = lax.axis_index("z"), lax.axis_index("core")
     wide, narrow = x * NY + y, z * NC + core
     height, width = inverse.shape
-    stored_here = activations.shape[0]
     to_columns = column_owner()
     to_rows = [(b, a) for a, b in to_columns]
 
-    local = forget - narrow * stored_here
-    onehot = (jnp.arange(stored_here, dtype=jnp.int32)[:, None] == local[None, :]).astype(BF16)
-    picked = lax.dot_general(
-        activations, onehot, (((0,), (0,)), ((), ())), preferred_element_type=F32
-    ).astype(BF16)
-    piece = scatter_sum(fold_cores(picked), "z", NZ).astype(BF16)
-    half = gather(piece, "z", NZ)
+    half = forgotten_half(activations, forget)
+    piece = lax.dynamic_slice_in_dim(half, z * (half.shape[0] // NZ), half.shape[0] // NZ, 0)
     piece_by_columns = lax.ppermute(piece, AXES, to_columns)
     rows_here = lax.all_gather(half, "core", axis=0, tiled=True)
 
@@ -123,9 +157,7 @@
         lax.dot_general(term, rows_here, (((0,), (0,)), ((), ())), preferred_element_type=F32)
         for term in exact_pair(less_one)
     )
-    summed = scatter_sum(part.astype(BF16), "x", NX)
-    change = scatter_sum(summed.astype(BF16), "y", NY)
-    change = change.astype(BF16)
+    change = scatter_sum(part.astype(BF16), ("x", "y"), NX * NY).astype(BF16)
     both = jnp.concatenate([piece_by_columns, change], axis=0)
     both = gather(both, "y", NY).reshape(NY, 2, -1, both.shape[1])
     rows_cols = both[:, 0].reshape(-1, both.shape[3])

time: 197 us -> 190 us (0.964)
  blocking collectives: 99.7 us -> 66.3 us
  waiting for transfers between devices: 20.8 us -> 47.2 us
    all_to_all x3 -> x1, blocking collectives: 48.3 us -> 17.7 us  [spread(): return lax.all_to_all(x, axis, 0, 0, tiled=True)]
    all_to_all x1, waiting for transfers between devices: 5.07 us -> 21.1 us  [spread(): return lax.all_to_all(x, axis, 0, 0, tiled=True)]
    all_to_all x3, waiting for transfers between devices: 12.6 us -> 21.1 us  [gather(): lax.all_to_all(jnp.broadcast_to(x[None], (parts,) + x.shape), axis, 0, 0,...]
    ppermute x3, starting transfers between devices: 22.9 us -> 18.7 us  [swap(): return lax.ppermute(x, 'core', [(0, 1), (1, 0)])]
    dot_general x10 -> x8, matrix products: 13 us -> 9.16 us  [dot(): return jnp.dot(a, b, precision=precision, preferred_element_type=F32)]
    all_to_all x1, starting transfers between devices: 6.82 us -> 9.67 us  [spread(): return lax.all_to_all(x, axis, 0, 0, tiled=True)]
  transfers between devices with their start and end apart: 9 -> 9, of which waited for: 6 -> 8; matrix products, arithmetic and copies ran while one was open for 8% -> 6% of each run, Pallas kernels for 0% -> 0%
where the time goes in v5:
time: 190 us; the launch traced here: 189 us
  blocking collectives  66.3 us (35%)
  starting transfers between devices  48.4 us (25%)
  waiting for transfers between devices  47.2 us (25%)
  matrix products  18.8 us (10%)
  other arithmetic  3.92 us (2%)
  local copies, waits for them, and re-layouts  3.01 us (2%)
    all_to_all x2, blocking collectives, gather(): lax.all_to_all(jnp.broadcast_to(x[None], (parts,) + x.shape), axis, 0, 0,...  45.2 us
    all_to_all x3, waiting for transfers between devices, gather(): lax.all_to_all(jnp.broadcast_to(x[None], (parts,) + x.shape), axis, 0, 0,...  21.1 us
    all_to_all x1, waiting for transfers between devices, spread(): return lax.all_to_all(x, axis, 0, 0, tiled=True)  21.1 us
    ppermute x3, starting transfers between devices, swap(): return lax.ppermute(x, 'core', [(0, 1), (1, 0)])  18.7 us
    all_to_all x1, blocking collectives, spread(): return lax.all_to_all(x, axis, 0, 0, tiled=True)  17.7 us
    all_to_all x3, starting transfers between devices, gather(): lax.all_to_all(jnp.broadcast_to(x[None], (parts,) + x.shape), axis, 0, 0,...  12.9 us
    all_to_all x1, starting transfers between devices, spread(): return lax.all_to_all(x, axis, 0, 0, tiled=True)  9.67 us
    dot_general x8, matrix products, dot(): return jnp.dot(a, b, precision=precision, preferred_element_type=F32)  9.16 us
  transfers between devices with their start and end apart: 9, of which 8 were waited for; matrix products, arithmetic and copies ran while one was open for 6% of the time, Pallas kernels for 0%

profile of v5, /device:TPU:1, one launch (start us, length us, event | category | flops | bytes accessed | tf_op | source)
XLA Modules:
  0.0 189.3 jit_solution(11321571794065900472)
XLA Ops:
  0.0 0.7 add_select_fusion
  0.7 0.2 convert_reduce_fusion
  0.9 0.6 reduce_max.27
  2.2 30.9 %conditional.1 = (bf16[256,512]{1,0:T(8,128)(2,1)S(1)}) conditional(s32[]{:T(128)} %convert_element_type.97, (s32[]{:T(128)}, s32[512]{0:T(512)}, bf16[256,512]{1,0:T(8,128)(2,1)}) %tuple.15, (s32[]{:T(128)}, s32[512]{0:T(512)S(1)}, s32[512]{0:T(512)S(1)}, s32[]{:T(128)}, s32[512]{0:T(512)}, /*index=5*/bf16[256,512]{1,0:T(8,128)(2,1)}, ...), branch_computations={%region_2.4_spmd, %region_4.5_spmd} | conditional | flops 252537344 | bytes 4790458 | solution.py:137
  2.2 0.8 multiply_add_fusion
  3.0 1.4 convolution_convert_fusion.1
  4.4 8.7 %collective-permute-start.1 = (bf16[96,256]{1,0:T(8,128)(2,1)S(1)}, bf16[96,256]{1,0:T(8,128)(2,1)S(1)}, u32[]{:S(2)}, u32[]{:S(2)}) collective-permute-start(bf16[96,256]{1,0:T(8,128)(2,1)S(1)} %constant_dynamic-slice_fusion), channel_id=1, source_target_pairs={{0,1},{1,0},{2,3},{3,2},{4,5},{5,4},{6,7},{7,6},{8,9},{9,8},{10,11... | collective-permute-start | bytes 147464 | tf_op jit(solution)/shard_map/cond/branch_1_fun/ppermute | solution.py:39
  13.2 0.9 collective-permute-done.1
  14.1 18.5 %all_to_all.44 = bf16[8,96,256]{2,1,0:T(8,128)(2,1)S(1)} all-to-all(bf16[8,96,256]{2,1,0:T(8,128)(2,1)S(1)} %broadcast_in_dim.43), channel_id=1, replica_groups=mesh['x'=4,'y'=8,'z'=8,'core'=2] {'z'}, dimensions={0} | all-to-all | bytes 786432 | tf_op jit(solution)/shard_map/cond/branch_1_fun/all_to_all | solution.py:34
  32.6 0.5 fusion.2
  33.1 3.4 %all_gather.3 = bf16[512,512]{1,0:T(8,128)(2,1)S(1)} all-gather(bf16[256,512]{1,0:T(8,128)(2,1)S(1)} %get-tuple-element.132), channel_id=1, replica_groups=mesh['x'=4,'y'=8,'z'=8,'core'=2] {'core'}, dimensions={0}, use_global_device_ids=true | all-gather | bytes 786432 | tf_op jit(solution)/shard_map/all_gather | solution.py:151
  36.5 0.8 fusion.15
  37.4 1.8 add_convert_fusion
  39.2 9.7 %all-to-all-start.3 = ((bf16[32,32,512]{2,1,0:T(8,128)(2,1)}), bf16[32,32,512]{2,1,0:T(8,128)(2,1)S(1)}, u32[]{:S(2)}, u32[]{:S(2)}) async-start(bf16[32,32,512]{2,1,0:T(8,128)(2,1)} %bitcast.6), calls=%async_computation.3 | async-start | bytes 2097152 | tf_op jit(solution)/shard_map/all_to_all | solution.py:26
  48.9 4.0 %collective-permute-start.2 = (bf16[32,512]{1,0:T(8,128)(2,1)S(1)}, bf16[32,512]{1,0:T(8,128)(2,1)S(1)}, u32[]{:S(2)}, u32[]{:S(2)}) collective-permute-start(bf16[32,512]{1,0:T(8,128)(2,1)S(1)} %constant_dynamic-slice_fusion.2), channel_id=1, source_target_pairs={{0,0},{1,128},{2,16},{3,144},{4,32},{5,160},{6,48},{7,176},{8,64},... | collective-permute-start | bytes 98312 | tf_op jit(solution)/shard_map/ppermute | solution.py:150
  52.9 21.1 %all-to-all-done.3 = bf16[32,32,512]{2,1,0:T(8,128)(2,1)S(1)} async-done(((bf16[32,32,512]{2,1,0:T(8,128)(2,1)}), bf16[32,32,512]{2,1,0:T(8,128)(2,1)S(1)}, u32[]{:S(2)}, u32[]{:S(2)}) %all-to-all-start.3) | async-done | bytes 1048608 | tf_op jit(solution)/shard_map/all_to_all | solution.py:26
  74.0 0.2 reduce_sum.88
  74.1 1.2 collective-permute-done.2
  75.3 0.8 broadcast_in_dim.57
  76.1 5.7 %all-to-all-start.4 = ((bf16[8,64,512]{2,1,0:T(8,128)(2,1)}), bf16[8,64,512]{2,1,0:T(8,128)(2,1)S(1)}, u32[]{:S(2)}, u32[]{:S(2)}) async-start(bf16[8,64,512]{2,1,0:T(8,128)(2,1)} %broadcast_in_dim.57), calls=%async_computation.4 | async-start | bytes 1048576 | tf_op jit(solution)/shard_map/all_to_all | solution.py:34
  81.9 15.1 %all-to-all-done.4 = bf16[8,64,512]{2,1,0:T(8,128)(2,1)S(1)} async-done(((bf16[8,64,512]{2,1,0:T(8,128)(2,1)}), bf16[8,64,512]{2,1,0:T(8,128)(2,1)S(1)}, u32[]{:S(2)}, u32[]{:S(2)}) %all-to-all-start.4) | async-done | bytes 524320 | tf_op jit(solution)/shard_map/all_to_all | solution.py:34
  97.0 0.3 convolution_bitcast_fusion.1
  97.3 0.3 fusion.13
  97.7 5.3 %collective-permute-start.3 = (f32[256,512]{1,0:T(8,128)S(1)}, f32[256,512]{1,0:T(8,128)S(1)}, u32[]{:S(2)}, u32[]{:S(2)}) collective-permute-start(f32[256,512]{1,0:T(8,128)S(1)} %constant_dynamic-slice_fusion.1), channel_id=1, source_target_pairs={{0,1},{1,0},{2,3},{3,2},{4,5},{5,4},{6,7},{7,6},{8,9},{9,8},{10,11... | collective-permute-start | bytes 1572872 | tf_op jit(solution)/shard_map/ppermute | solution.py:39
  102.9 1.5 collective-permute-done.3
  104.5 17.7 %all_to_all.45 = bf16[8,32,512]{2,1,0:T(8,128)(2,1)S(1)} all-to-all(bf16[8,32,512]{2,1,0:T(8,128)(2,1)S(1)} %bitcast.94), channel_id=1, replica_groups=mesh['x'=4,'y'=8,'z'=8,'core'=2] {'z'}, dimensions={0} | all-to-all | bytes 524288 | tf_op jit(solution)/shard_map/all_to_all | solution.py:26
  122.3 0.7 broadcast_in_dim.58
  123.0 3.4 %all-to-all-start.6 = ((f32[4,1,32,512]{3,2,1,0:T(8,128)}), f32[4,1,32,512]{3,2,1,0:T(8,128)S(1)}, u32[]{:S(2)}, u32[]{:S(2)}) async-start(f32[4,1,32,512]{3,2,1,0:T(8,128)} %broadcast_in_dim.58), calls=%async_computation.6 | async-start | bytes 524288 | tf_op jit(solution)/shard_map/all_to_all | solution.py:34
  126.4 3.2 %collective-permute-start.4 = (bf16[32,512]{1,0:T(8,128)(2,1)S(1)}, bf16[32,512]{1,0:T(8,128)(2,1)S(1)}, u32[]{:S(2)}, u32[]{:S(2)}) collective-permute-start(bf16[32,512]{1,0:T(8,128)(2,1)S(1)} %reduce_sum.88), channel_id=1, source_target_pairs={{0,0},{128,1},{16,2},{144,3},{32,4},{160,5},{48,6},{176,7},{64,8},... | collective-permute-start | bytes 98312 | tf_op jit(solution)/shard_map/ppermute | solution.py:179
  129.6 2.3 %all-to-all-done.6 = f32[4,1,32,512]{3,2,1,0:T(8,128)S(1)} async-done(((f32[4,1,32,512]{3,2,1,0:T(8,128)}), f32[4,1,32,512]{3,2,1,0:T(8,128)S(1)}, u32[]{:S(2)}, u32[]{:S(2)}) %all-to-all-start.6) | async-done | bytes 262176 | tf_op jit(solution)/shard_map/all_to_all | solution.py:34
  132.0 1.5 collective-permute-done.4
  133.6 26.7 %all_to_all.46 = bf16[8,72,512]{2,1,0:T(8,128)(2,1)S(1)} all-to-all(bf16[8,72,512]{2,1,0:T(8,128)(2,1)S(1)} %broadcast_in_dim.65), channel_id=1, replica_groups=mesh['x'=4,'y'=8,'z'=8,'core'=2] {'z'}, dimensions={0} | all-to-all | bytes 1179648 | tf_op jit(solution)/shard_map/all_to_all | solution.py:34
  160.3 4.7 %collective-permute-start.5 = (bf16[576,512]{1,0:T(8,128)(2,1)S(1)}, bf16[576,512]{1,0:T(8,128)(2,1)S(1)}, u32[]{:S(2)}, u32[]{:S(2)}) collective-permute-start(bf16[576,512]{1,0:T(8,128)(2,1)S(1)} %bitcast.88), channel_id=1, source_target_pairs={{0,1},{1,0},{2,3},{3,2},{4,5},{5,4},{6,7},{7,6},{8,9},{9,8},{10,11... | collective-permute-start | bytes 1769480 | tf_op jit(solution)/shard_map/ppermute | solution.py:39
  165.1 1.1 broadcast_in_dim.87
  166.1 3.7 %all-to-all-start.8 = ((bf16[4,256,512]{2,1,0:T(8,128)(2,1)}), bf16[4,256,512]{2,1,0:T(8,128)(2,1)S(1)}, u32[]{:S(2)}, u32[]{:S(2)}) async-start(bf16[4,256,512]{2,1,0:T(8,128)(2,1)} %broadcast_in_dim.87), calls=%async_computation.8 | async-start | bytes 2097152 | tf_op jit(solution)/shard_map/all_to_all | solution.py:34
  170.2 0.1 convert.11
  170.5 1.0 fusion.30
  171.6 1.0 fusion.61
  172.6 1.1 convolution_add_fusion.5
  173.8 1.0 convolution_add_fusion.4
  174.8 1.1 abs_reduce_fusion.1
  175.9 1.1 convolution_add_fusion.3
  177.0 1.0 convolution_add_fusion.2
  178.0 0.6 reduce_max.28
  178.6 0.6 while.14
  179.3 1.8 convolution_add_fusion.1
  181.0 3.7 %all-to-all-done.8 = bf16[4,256,512]{2,1,0:T(8,128)(2,1)S(1)} async-done(((bf16[4,256,512]{2,1,0:T(8,128)(2,1)}), bf16[4,256,512]{2,1,0:T(8,128)(2,1)S(1)}, u32[]{:S(2)}, u32[]{:S(2)}) %all-to-all-start.8) | async-done | bytes 1048608 | tf_op jit(solution)/shard_map/all_to_all | solution.py:34
  184.8 4.5 %convolution_add_fusion = f32[512,1024]{1,0:T(8,128)} fusion(f32[512,1024]{1,0:T(8,128)} %param.7, f32[512,512]{1,0:T(8,128)} %convolution_add_fusion.1, bf16[1024,512]{1,0:T(8,128)(2,1)S(1)} %bitcast.87), kind=kOutput, calls=%fused_computation.29 | convolution fusion | flops 1611137024 | bytes 6291456 | tf_op jit(solution)/shard_map/dot_general | solution.py:197
  (25 shorter events, 1.0 us)
Async XLA Ops:
  2.2 34.4 %copy-start = (f32[512,1024]{1,0:T(8,128)S(1)}, f32[512,1024]{1,0:T(8,128)}, u32[]{:S(2)}) copy-start(f32[512,1024]{1,0:T(8,128)} %param.7) | copy-start | bytes 6291460
  4.4 9.6 %collective-permute-start.1 = (bf16[96,256]{1,0:T(8,128)(2,1)S(1)}, bf16[96,256]{1,0:T(8,128)(2,1)S(1)}, u32[]{:S(2)}, u32[]{:S(2)}) collective-permute-start(bf16[96,256]{1,0:T(8,128)(2,1)S(1)} %constant_dynamic-slice_fusion), channel_id=1, source_target_pairs={{0,1},{1,0},{2,3},{3,2},{4,5},{5,4},{6,7},{7,6},{8,9},{9,8},{10,11... | collective-permute-start | bytes 147464 | tf_op jit(solution)/shard_map/cond/branch_1_fun/ppermute | solution.py:39
  39.2 34.8 %all-to-all-start.3 = ((bf16[32,32,512]{2,1,0:T(8,128)(2,1)}), bf16[32,32,512]{2,1,0:T(8,128)(2,1)S(1)}, u32[]{:S(2)}, u32[]{:S(2)}) async-start(bf16[32,32,512]{2,1,0:T(8,128)(2,1)} %bitcast.6), calls=%async_computation.3 | async-start | bytes 2097152 | tf_op jit(solution)/shard_map/all_to_all | solution.py:26
  48.9 26.4 %collective-permute-start.2 = (bf16[32,512]{1,0:T(8,128)(2,1)S(1)}, bf16[32,512]{1,0:T(8,128)(2,1)S(1)}, u32[]{:S(2)}, u32[]{:S(2)}) collective-permute-start(bf16[32,512]{1,0:T(8,128)(2,1)S(1)} %constant_dynamic-slice_fusion.2), channel_id=1, source_target_pairs={{0,0},{1,128},{2,16},{3,144},{4,32},{5,160},{6,48},{7,176},{8,64},... | collective-permute-start | bytes 98312 | tf_op jit(solution)/shard_map/ppermute | solution.py:150
  76.1 20.8 %all-to-all-start.4 = ((bf16[8,64,512]{2,1,0:T(8,128)(2,1)}), bf16[8,64,512]{2,1,0:T(8,128)(2,1)S(1)}, u32[]{:S(2)}, u32[]{:S(2)}) async-start(bf16[8,64,512]{2,1,0:T(8,128)(2,1)} %broadcast_in_dim.57), calls=%async_computation.4 | async-start | bytes 1048576 | tf_op jit(solution)/shard_map/all_to_all | solution.py:34
  97.7 6.8 %collective-permute-start.3 = (f32[256,512]{1,0:T(8,128)S(1)}, f32[256,512]{1,0:T(8,128)S(1)}, u32[]{:S(2)}, u32[]{:S(2)}) collective-permute-start(f32[256,512]{1,0:T(8,128)S(1)} %constant_dynamic-slice_fusion.1), channel_id=1, source_target_pairs={{0,1},{1,0},{2,3},{3,2},{4,5},{5,4},{6,7},{7,6},{8,9},{9,8},{10,11... | collective-permute-start | bytes 1572872 | tf_op jit(solution)/shard_map/ppermute | solution.py:39
  123.0 8.9 %all-to-all-start.6 = ((f32[4,1,32,512]{3,2,1,0:T(8,128)}), f32[4,1,32,512]{3,2,1,0:T(8,128)S(1)}, u32[]{:S(2)}, u32[]{:S(2)}) async-start(f32[4,1,32,512]{3,2,1,0:T(8,128)} %broadcast_in_dim.58), calls=%async_computation.6 | async-start | bytes 524288 | tf_op jit(solution)/shard_map/all_to_all | solution.py:34
  126.4 7.1 %collective-permute-start.4 = (bf16[32,512]{1,0:T(8,128)(2,1)S(1)}, bf16[32,512]{1,0:T(8,128)(2,1)S(1)}, u32[]{:S(2)}, u32[]{:S(2)}) collective-permute-start(bf16[32,512]{1,0:T(8,128)(2,1)S(1)} %reduce_sum.88), channel_id=1, source_target_pairs={{0,0},{128,1},{16,2},{144,3},{32,4},{160,5},{48,6},{176,7},{64,8},... | collective-permute-start | bytes 98312 | tf_op jit(solution)/shard_map/ppermute | solution.py:179
  160.3 9.5 %collective-permute-start.5 = (bf16[576,512]{1,0:T(8,128)(2,1)S(1)}, bf16[576,512]{1,0:T(8,128)(2,1)S(1)}, u32[]{:S(2)}, u32[]{:S(2)}) collective-permute-start(bf16[576,512]{1,0:T(8,128)(2,1)S(1)} %bitcast.88), channel_id=1, source_target_pairs={{0,1},{1,0},{2,3},{3,2},{4,5},{5,4},{6,7},{7,6},{8,9},{9,8},{10,11... | collective-permute-start | bytes 1769480 | tf_op jit(solution)/shard_map/ppermute | solution.py:39
  166.1 18.7 %all-to-all-start.8 = ((bf16[4,256,512]{2,1,0:T(8,128)(2,1)}), bf16[4,256,512]{2,1,0:T(8,128)(2,1)S(1)}, u32[]{:S(2)}, u32[]{:S(2)}) async-start(bf16[4,256,512]{2,1,0:T(8,128)(2,1)} %broadcast_in_dim.87), calls=%async_computation.8 | async-start | bytes 2097152 | tf_op jit(solution)/shard_map/all_to_all | solution.py:34

commit v6 on v5

--- a/solution.py
+++ b/solution.py
@@ -7,6 +7,7 @@
 from jax.experimental.layout import Layout, with_layout_constraint
 from jax.sharding import Mesh
 from jax.sharding import PartitionSpec as P
+
 
 M = 16384
 ROWS = 512
@@ -45,12 +46,6 @@
     there = lax.dynamic_slice_in_dim(x, (1 - core) * half, half, 0)
     here = lax.dynamic_slice_in_dim(x, core * half, half, 0)
     return here + swap(there)
-
-
-def join_cores(x):
-    other = swap(x)
-    first = lax.axis_index("core") == 0
-    return jnp.concatenate([jnp.where(first, x, other), jnp.where(first, other, x)], axis=0)
 
 
 def exact_pair(x):
@@ -156,8 +151,8 @@
     part = sum(
         lax.dot_general(term, rows_here, (((0,), (0,)), ((), ())), preferred_element_type=F32)
         for term in exact_pair(less_one)
-    )
-    change = scatter_sum(part.astype(BF16), ("x", "y"), NX * NY).astype(BF16)
+    ).astype(BF16)
+    change = scatter_sum(part, ("x", "y"), NX * NY).astype(BF16)
     both = jnp.concatenate([piece_by_columns, change], axis=0)
     both = gather(both, "y", NY).reshape(NY, 2, -1, both.shape[1])
     rows_cols = both[:, 0].reshape(-1, both.shape[3])
@@ -177,7 +172,12 @@
     low = jnp.sum(jnp.where(on_diagonal, low.astype(F32), 0.0), axis=0, keepdims=True)
     low = jnp.pad(low, ((0, PAD - 1), (0, 0))).astype(BF16)
     change_there = lax.ppermute(change, AXES, to_rows)
-    gathered = gather(jnp.concatenate([high, low, change_there], axis=0), "z", NZ)
+    sent = jnp.concatenate([high, low, change_there], axis=0)
+    images = (rows_cols.astype(F32) + change_cols.astype(F32)).astype(BF16)
+    images = jnp.broadcast_to(images[None], (NX,) + images.shape)
+    sent, images = lax.optimization_barrier((sent, images))
+    gathered = gather(sent, "z", NZ)
+    images_cols = lax.all_to_all(images, "x", 0, 0, tiled=True).reshape(-1, images.shape[2])
     mine, other = gathered, swap(gathered)
     first = core == 0
     halves = [jnp.where(first, mine, other), jnp.where(first, other, mine)]
@@ -191,8 +191,6 @@
     change_here = [h[:, n + PAD :].reshape(-1, h.shape[2]) for h in halves]
     change_here = jnp.concatenate(change_here, axis=0)
     images_rows = rows_here.astype(F32) + change_here
-    images_cols = gather((rows_cols.astype(F32) + change_cols.astype(F32)).astype(BF16), "x", NX)
-
     solved = solve_rows(images_rows * BETA, scaled)
     return inverse + lax.dot_general(
         solved,
@@ -206,6 +204,7 @@
 def solution(mesh):
     devices = np.asarray(mesh.devices).reshape(NX, NY, NZ, NC)
     placed = (P(("x", "y"), ("z", "core")), P(("z", "core"), ("x", "y")), P())
+
     return jax.shard_map(
         on_device,
         mesh=Mesh(devices, AXES),

time: 190 us -> 182 us (0.958)
  blocking collectives: 66.3 us -> 40.2 us
  waiting for transfers between devices: 47.2 us -> 57.9 us
  starting transfers between devices: 48.4 us -> 55.2 us
    all_to_all x1 -> x0, blocking collectives: 17.7 us -> none  [spread(): return lax.all_to_all(x, axis, 0, 0, tiled=True)]
    all_to_all x1 -> x2, waiting for transfers between devices: 21.1 us -> 30.1 us  [spread(): return lax.all_to_all(x, axis, 0, 0, tiled=True)]
    all_to_all x2, blocking collectives: 45.2 us -> 36.8 us  [gather(): lax.all_to_all(jnp.broadcast_to(x[None], (parts,) + x.shape), axis, 0, 0,...]
    all_to_all x1 -> x2, starting transfers between devices: 9.67 us -> 16.4 us  [spread(): return lax.all_to_all(x, axis, 0, 0, tiled=True)]
    all_to_all x0 -> x1, waiting for transfers between devices: none -> 3.74 us  [on_device(): lax.all_to_all(images, 'x', 0, 0, tiled=True).reshape(-1, images.shape[2])]
    all_to_all x0 -> x1, starting transfers between devices: none -> 3.71 us  [on_device(): lax.all_to_all(images, 'x', 0, 0, tiled=True).reshape(-1, images.shape[2])]
    all_to_all x3 -> x2, starting transfers between devices: 12.9 us -> 9.16 us  [gather(): lax.all_to_all(jnp.broadcast_to(x[None], (parts,) + x.shape), axis, 0, 0,...]
    all_to_all x3 -> x2, waiting for transfers between devices: 21.1 us -> 20.5 us  [gather(): lax.all_to_all(jnp.broadcast_to(x[None], (parts,) + x.shape), axis, 0, 0,...]
  transfers between devices with their start and end apart: 9 -> 10, of which waited for: 8 -> 8; matrix products, arithmetic and copies ran while one was open for 6% -> 6% of each run, Pallas kernels for 0% -> 0%
where the time goes in v6:
time: 182 us; the launch traced here: 181 us
  waiting for transfers between devices  57.9 us (32%)
  starting transfers between devices  55.2 us (30%)
  blocking collectives  40.2 us (22%)
  matrix products  18.8 us (10%)
  other arithmetic  4.59 us (3%)
  local copies, waits for them, and re-layouts  3.01 us (2%)
    all_to_all x2, blocking collectives, gather(): lax.all_to_all(jnp.broadcast_to(x[None], (parts,) + x.shape), axis, 0, 0,...  36.8 us
    all_to_all x2, waiting for transfers between devices, spread(): return lax.all_to_all(x, axis, 0, 0, tiled=True)  30.1 us
    all_to_all x2, waiting for transfers between devices, gather(): lax.all_to_all(jnp.broadcast_to(x[None], (parts,) + x.shape), axis, 0, 0,...  20.5 us
    ppermute x3, starting transfers between devices, swap(): return lax.ppermute(x, 'core', [(0, 1), (1, 0)])  19.9 us
    all_to_all x2, starting transfers between devices, spread(): return lax.all_to_all(x, axis, 0, 0, tiled=True)  16.4 us
    dot_general x8, matrix products, dot(): return jnp.dot(a, b, precision=precision, preferred_element_type=F32)  9.17 us
    all_to_all x2, starting transfers between devices, gather(): lax.all_to_all(jnp.broadcast_to(x[None], (parts,) + x.shape), axis, 0, 0,...  9.16 us
    dot_general x1, matrix products, on_device(): lax.dot_general(solved, images_cols.astype(F32), (((1,), (1,)), ((), ()))...  4.53 us
  transfers between devices with their start and end apart: 10, of which 8 were waited for; matrix products, arithmetic and copies ran while one was open for 6% of the time, Pallas kernels for 0%

profile of v6, /device:TPU:1, one launch (start us, length us, event | category | flops | bytes accessed | tf_op | source)
XLA Modules:
  0.0 181.4 jit_solution(2445833201113698484)
XLA Ops:
  0.0 0.7 add_select_fusion
  0.7 0.2 convert_reduce_fusion
  0.9 0.6 reduce_max.27
  2.2 30.9 %conditional.1 = (bf16[256,512]{1,0:T(8,128)(2,1)S(1)}) conditional(s32[]{:T(128)} %convert_element_type.97, (s32[]{:T(128)}, s32[512]{0:T(512)}, bf16[256,512]{1,0:T(8,128)(2,1)}) %tuple.16, (s32[]{:T(128)}, s32[512]{0:T(512)S(1)}, s32[512]{0:T(512)S(1)}, s32[]{:T(128)}, s32[512]{0:T(512)}, /*index=5*/bf16[256,512]{1,0:T(8,128)(2,1)}, ...), branch_computations={%region_2.4_spmd, %region_4.5_spmd} | conditional | flops 252537344 | bytes 4790458 | solution.py:132
  2.2 0.8 multiply_add_fusion
  3.0 1.4 convolution_convert_fusion.1
  4.4 8.7 %collective-permute-start.1 = (bf16[96,256]{1,0:T(8,128)(2,1)S(1)}, bf16[96,256]{1,0:T(8,128)(2,1)S(1)}, u32[]{:S(2)}, u32[]{:S(2)}) collective-permute-start(bf16[96,256]{1,0:T(8,128)(2,1)S(1)} %constant_dynamic-slice_fusion), channel_id=1, source_target_pairs={{0,1},{1,0},{2,3},{3,2},{4,5},{5,4},{6,7},{7,6},{8,9},{9,8},{10,11... | collective-permute-start | bytes 147464 | tf_op jit(solution)/shard_map/cond/branch_1_fun/ppermute | solution.py:40
  13.2 0.9 collective-permute-done.1
  14.1 18.5 %all_to_all.44 = bf16[8,96,256]{2,1,0:T(8,128)(2,1)S(1)} all-to-all(bf16[8,96,256]{2,1,0:T(8,128)(2,1)S(1)} %broadcast_in_dim.43), channel_id=1, replica_groups=mesh['x'=4,'y'=8,'z'=8,'core'=2] {'z'}, dimensions={0} | all-to-all | bytes 786432 | tf_op jit(solution)/shard_map/cond/branch_1_fun/all_to_all | solution.py:35
  32.6 0.5 fusion.2
  33.1 3.4 %all_gather.3 = bf16[512,512]{1,0:T(8,128)(2,1)S(1)} all-gather(bf16[256,512]{1,0:T(8,128)(2,1)S(1)} %get-tuple-element.136), channel_id=1, replica_groups=mesh['x'=4,'y'=8,'z'=8,'core'=2] {'core'}, dimensions={0}, use_global_device_ids=true | all-gather | bytes 786432 | tf_op jit(solution)/shard_map/all_gather | solution.py:146
  36.5 0.8 fusion.15
  37.4 1.8 add_convert_fusion
  39.2 9.7 %all-to-all-start.3 = ((bf16[32,32,512]{2,1,0:T(8,128)(2,1)}), bf16[32,32,512]{2,1,0:T(8,128)(2,1)S(1)}, u32[]{:S(2)}, u32[]{:S(2)}) async-start(bf16[32,32,512]{2,1,0:T(8,128)(2,1)} %bitcast.6), calls=%async_computation.3 | async-start | bytes 2097152 | tf_op jit(solution)/shard_map/all_to_all | solution.py:27
  48.9 4.0 %collective-permute-start.2 = (bf16[32,512]{1,0:T(8,128)(2,1)S(1)}, bf16[32,512]{1,0:T(8,128)(2,1)S(1)}, u32[]{:S(2)}, u32[]{:S(2)}) collective-permute-start(bf16[32,512]{1,0:T(8,128)(2,1)S(1)} %constant_dynamic-slice_fusion.2), channel_id=1, source_target_pairs={{0,0},{1,128},{2,16},{3,144},{4,32},{5,160},{6,48},{7,176},{8,64},... | collective-permute-start | bytes 98312 | tf_op jit(solution)/shard_map/ppermute | solution.py:145
  52.9 21.1 %all-to-all-done.3 = bf16[32,32,512]{2,1,0:T(8,128)(2,1)S(1)} async-done(((bf16[32,32,512]{2,1,0:T(8,128)(2,1)}), bf16[32,32,512]{2,1,0:T(8,128)(2,1)S(1)}, u32[]{:S(2)}, u32[]{:S(2)}) %all-to-all-start.3) | async-done | bytes 1048608 | tf_op jit(solution)/shard_map/all_to_all | solution.py:27
  74.0 0.2 reduce_sum.88
  74.1 1.2 collective-permute-done.2
  75.3 0.8 broadcast_in_dim.57
  76.1 5.7 %all-to-all-start.4 = ((bf16[8,64,512]{2,1,0:T(8,128)(2,1)}), bf16[8,64,512]{2,1,0:T(8,128)(2,1)S(1)}, u32[]{:S(2)}, u32[]{:S(2)}) async-start(bf16[8,64,512]{2,1,0:T(8,128)(2,1)} %broadcast_in_dim.57), calls=%async_computation.4 | async-start | bytes 1048576 | tf_op jit(solution)/shard_map/all_to_all | solution.py:35
  81.9 15.1 %all-to-all-done.4 = bf16[8,64,512]{2,1,0:T(8,128)(2,1)S(1)} async-done(((bf16[8,64,512]{2,1,0:T(8,128)(2,1)}), bf16[8,64,512]{2,1,0:T(8,128)(2,1)S(1)}, u32[]{:S(2)}, u32[]{:S(2)}) %all-to-all-start.4) | async-done | bytes 524320 | tf_op jit(solution)/shard_map/all_to_all | solution.py:35
  97.0 0.3 convolution_bitcast_fusion.1
  97.3 0.3 fusion.13
  97.7 5.3 %collective-permute-start.3 = (f32[256,512]{1,0:T(8,128)S(1)}, f32[256,512]{1,0:T(8,128)S(1)}, u32[]{:S(2)}, u32[]{:S(2)}) collective-permute-start(f32[256,512]{1,0:T(8,128)S(1)} %constant_dynamic-slice_fusion.1), channel_id=1, source_target_pairs={{0,1},{1,0},{2,3},{3,2},{4,5},{5,4},{6,7},{7,6},{8,9},{9,8},{10,11... | collective-permute-start | bytes 1572872 | tf_op jit(solution)/shard_map/ppermute | solution.py:40
  102.9 1.5 collective-permute-done.3
  104.4 0.8 add_convert_fusion.2
  105.2 6.8 %all-to-all-start.5 = ((bf16[8,32,512]{2,1,0:T(8,128)(2,1)}), bf16[8,32,512]{2,1,0:T(8,128)(2,1)S(1)}, u32[]{:S(2)}, u32[]{:S(2)}) async-start(bf16[8,32,512]{2,1,0:T(8,128)(2,1)} %bitcast.12), calls=%async_computation.5 | async-start | bytes 524288 | tf_op jit(solution)/shard_map/all_to_all | solution.py:27
  112.0 2.1 %collective-permute-start.4 = (bf16[32,512]{1,0:T(8,128)(2,1)S(1)}, bf16[32,512]{1,0:T(8,128)(2,1)S(1)}, u32[]{:S(2)}, u32[]{:S(2)}) collective-permute-start(bf16[32,512]{1,0:T(8,128)(2,1)S(1)} %reduce_sum.88), channel_id=1, source_target_pairs={{0,0},{128,1},{16,2},{144,3},{32,4},{160,5},{48,6},{176,7},{64,8},... | collective-permute-start | bytes 98312 | tf_op jit(solution)/shard_map/ppermute | solution.py:174
  114.1 9.0 %all-to-all-done.5 = bf16[8,32,512]{2,1,0:T(8,128)(2,1)S(1)} async-done(((bf16[8,32,512]{2,1,0:T(8,128)(2,1)}), bf16[8,32,512]{2,1,0:T(8,128)(2,1)S(1)}, u32[]{:S(2)}, u32[]{:S(2)}) %all-to-all-start.5) | async-done | bytes 262176 | tf_op jit(solution)/shard_map/all_to_all | solution.py:27
  123.1 0.7 broadcast_in_dim.58
  123.9 3.4 %all-to-all-start.6 = ((f32[4,1,32,512]{3,2,1,0:T(8,128)}), f32[4,1,32,512]{3,2,1,0:T(8,128)S(1)}, u32[]{:S(2)}, u32[]{:S(2)}) async-start(f32[4,1,32,512]{3,2,1,0:T(8,128)} %broadcast_in_dim.58), calls=%async_computation.6 | async-start | bytes 524288 | tf_op jit(solution)/shard_map/all_to_all | solution.py:35
  127.4 5.4 %all-to-all-done.6 = f32[4,1,32,512]{3,2,1,0:T(8,128)S(1)} async-done(((f32[4,1,32,512]{3,2,1,0:T(8,128)}), f32[4,1,32,512]{3,2,1,0:T(8,128)S(1)}, u32[]{:S(2)}, u32[]{:S(2)}) %all-to-all-start.6) | async-done | bytes 262176 | tf_op jit(solution)/shard_map/all_to_all | solution.py:35
  132.9 1.1 broadcast_in_dim.61
  134.0 18.3 %all_to_all.45 = bf16[8,72,512]{2,1,0:T(8,128)(2,1)S(1)} all-to-all(bf16[8,72,512]{2,1,0:T(8,128)(2,1)S(1)} %broadcast_in_dim.62), channel_id=1, replica_groups=mesh['x'=4,'y'=8,'z'=8,'core'=2] {'z'}, dimensions={0} | all-to-all | bytes 1179648 | tf_op jit(solution)/shard_map/all_to_all | solution.py:35
  152.3 5.8 %collective-permute-start.5 = (bf16[576,512]{1,0:T(8,128)(2,1)S(1)}, bf16[576,512]{1,0:T(8,128)(2,1)S(1)}, u32[]{:S(2)}, u32[]{:S(2)}) collective-permute-start(bf16[576,512]{1,0:T(8,128)(2,1)S(1)} %bitcast.88), channel_id=1, source_target_pairs={{0,1},{1,0},{2,3},{3,2},{4,5},{5,4},{6,7},{7,6},{8,9},{9,8},{10,11... | collective-permute-start | bytes 1769480 | tf_op jit(solution)/shard_map/ppermute | solution.py:40
  158.2 3.7 %all-to-all-start.8 = ((bf16[4,256,512]{2,1,0:T(8,128)(2,1)}), bf16[4,256,512]{2,1,0:T(8,128)(2,1)S(1)}, u32[]{:S(2)}, u32[]{:S(2)}) async-start(bf16[4,256,512]{2,1,0:T(8,128)(2,1)} %broadcast_in_dim.61), calls=%async_computation.8 | async-start | bytes 2097152 | tf_op jit(solution)/shard_map/all_to_all | solution.py:180
  162.6 1.0 fusion.30
  163.7 1.0 fusion.61
  164.7 1.1 convolution_add_fusion.5
  165.8 1.0 convolution_add_fusion.4
  166.9 1.1 abs_reduce_fusion.1
  168.0 1.1 convolution_add_fusion.3
  169.0 1.0 convolution_add_fusion.2
  170.1 0.6 reduce_max.28
  170.7 0.6 while.14
  171.3 1.8 convolution_add_fusion.1
  173.1 3.7 %all-to-all-done.8 = bf16[4,256,512]{2,1,0:T(8,128)(2,1)S(1)} async-done(((bf16[4,256,512]{2,1,0:T(8,128)(2,1)}), bf16[4,256,512]{2,1,0:T(8,128)(2,1)S(1)}, u32[]{:S(2)}, u32[]{:S(2)}) %all-to-all-start.8) | async-done | bytes 1048608 | tf_op jit(solution)/shard_map/all_to_all | solution.py:180
  176.8 4.5 %convolution_add_fusion = f32[512,1024]{1,0:T(8,128)} fusion(f32[512,1024]{1,0:T(8,128)} %param.7, f32[512,512]{1,0:T(8,128)} %convolution_add_fusion.1, bf16[1024,512]{1,0:T(8,128)(2,1)S(1)} %bitcast.87), kind=kOutput, calls=%fused_computation.29 | convolution fusion | flops 1611137024 | bytes 6291456 | tf_op jit(solution)/shard_map/dot_general | solution.py:195
  (26 shorter events, 1.1 us)
Async XLA Ops:
  2.2 34.4 %copy-start = (f32[512,1024]{1,0:T(8,128)S(1)}, f32[512,1024]{1,0:T(8,128)}, u32[]{:S(2)}) copy-start(f32[512,1024]{1,0:T(8,128)} %param.7) | copy-start | bytes 6291460
  4.4 9.6 %collective-permute-start.1 = (bf16[96,256]{1,0:T(8,128)(2,1)S(1)}, bf16[96,256]{1,0:T(8,128)(2,1)S(1)}, u32[]{:S(2)}, u32[]{:S(2)}) collective-permute-start(bf16[96,256]{1,0:T(8,128)(2,1)S(1)} %constant_dynamic-slice_fusion), channel_id=1, source_target_pairs={{0,1},{1,0},{2,3},{3,2},{4,5},{5,4},{6,7},{7,6},{8,9},{9,8},{10,11... | collective-permute-start | bytes 147464 | tf_op jit(solution)/shard_map/cond/branch_1_fun/ppermute | solution.py:40
  39.2 34.8 %all-to-all-start.3 = ((bf16[32,32,512]{2,1,0:T(8,128)(2,1)}), bf16[32,32,512]{2,1,0:T(8,128)(2,1)S(1)}, u32[]{:S(2)}, u32[]{:S(2)}) async-start(bf16[32,32,512]{2,1,0:T(8,128)(2,1)} %bitcast.6), calls=%async_computation.3 | async-start | bytes 2097152 | tf_op jit(solution)/shard_map/all_to_all | solution.py:27
  48.9 26.4 %collective-permute-start.2 = (bf16[32,512]{1,0:T(8,128)(2,1)S(1)}, bf16[32,512]{1,0:T(8,128)(2,1)S(1)}, u32[]{:S(2)}, u32[]{:S(2)}) collective-permute-start(bf16[32,512]{1,0:T(8,128)(2,1)S(1)} %constant_dynamic-slice_fusion.2), channel_id=1, source_target_pairs={{0,0},{1,128},{2,16},{3,144},{4,32},{5,160},{6,48},{7,176},{8,64},... | collective-permute-start | bytes 98312 | tf_op jit(solution)/shard_map/ppermute | solution.py:145
  76.1 20.8 %all-to-all-start.4 = ((bf16[8,64,512]{2,1,0:T(8,128)(2,1)}), bf16[8,64,512]{2,1,0:T(8,128)(2,1)S(1)}, u32[]{:S(2)}, u32[]{:S(2)}) async-start(bf16[8,64,512]{2,1,0:T(8,128)(2,1)} %broadcast_in_dim.57), calls=%async_computation.4 | async-start | bytes 1048576 | tf_op jit(solution)/shard_map/all_to_all | solution.py:35
  97.7 6.8 %collective-permute-start.3 = (f32[256,512]{1,0:T(8,128)S(1)}, f32[256,512]{1,0:T(8,128)S(1)}, u32[]{:S(2)}, u32[]{:S(2)}) collective-permute-start(f32[256,512]{1,0:T(8,128)S(1)} %constant_dynamic-slice_fusion.1), channel_id=1, source_target_pairs={{0,1},{1,0},{2,3},{3,2},{4,5},{5,4},{6,7},{7,6},{8,9},{9,8},{10,11... | collective-permute-start | bytes 1572872 | tf_op jit(solution)/shard_map/ppermute | solution.py:40
  105.2 17.9 %all-to-all-start.5 = ((bf16[8,32,512]{2,1,0:T(8,128)(2,1)}), bf16[8,32,512]{2,1,0:T(8,128)(2,1)S(1)}, u32[]{:S(2)}, u32[]{:S(2)}) async-start(bf16[8,32,512]{2,1,0:T(8,128)(2,1)} %bitcast.12), calls=%async_computation.5 | async-start | bytes 524288 | tf_op jit(solution)/shard_map/all_to_all | solution.py:27
  112.0 20.9 %collective-permute-start.4 = (bf16[32,512]{1,0:T(8,128)(2,1)S(1)}, bf16[32,512]{1,0:T(8,128)(2,1)S(1)}, u32[]{:S(2)}, u32[]{:S(2)}) collective-permute-start(bf16[32,512]{1,0:T(8,128)(2,1)S(1)} %reduce_sum.88), channel_id=1, source_target_pairs={{0,0},{128,1},{16,2},{144,3},{32,4},{160,5},{48,6},{176,7},{64,8},... | collective-permute-start | bytes 98312 | tf_op jit(solution)/shard_map/ppermute | solution.py:174
  123.9 8.9 %all-to-all-start.6 = ((f32[4,1,32,512]{3,2,1,0:T(8,128)}), f32[4,1,32,512]{3,2,1,0:T(8,128)S(1)}, u32[]{:S(2)}, u32[]{:S(2)}) async-start(f32[4,1,32,512]{3,2,1,0:T(8,128)} %broadcast_in_dim.58), calls=%async_computation.6 | async-start | bytes 524288 | tf_op jit(solution)/shard_map/all_to_all | solution.py:35
  152.3 9.6 %collective-permute-start.5 = (bf16[576,512]{1,0:T(8,128)(2,1)S(1)}, bf16[576,512]{1,0:T(8,128)(2,1)S(1)}, u32[]{:S(2)}, u32[]{:S(2)}) collective-permute-start(bf16[576,512]{1,0:T(8,128)(2,1)S(1)} %bitcast.88), channel_id=1, source_target_pairs={{0,1},{1,0},{2,3},{3,2},{4,5},{5,4},{6,7},{7,6},{8,9},{9,8},{10,11... | collective-permute-start | bytes 1769480 | tf_op jit(solution)/shard_map/ppermute | solution.py:40
  158.2 18.7 %all-to-all-start.8 = ((bf16[4,256,512]{2,1,0:T(8,128)(2,1)}), bf16[4,256,512]{2,1,0:T(8,128)(2,1)S(1)}, u32[]{:S(2)}, u32[]{:S(2)}) async-start(bf16[4,256,512]{2,1,0:T(8,128)(2,1)} %broadcast_in_dim.61), calls=%async_computation.8 | async-start | bytes 2097152 | tf_op jit(solution)/shard_map/all_to_all | solution.py:180

commit v7 on v6

--- a/solution.py
+++ b/solution.py
@@ -4,7 +4,9 @@
 import jax.numpy as jnp
 import numpy as np
 from jax import lax
+from jax.experimental import pallas as pl
 from jax.experimental.layout import Layout, with_layout_constraint
+from jax.experimental.pallas import tpu as pltpu
 from jax.sharding import Mesh
 from jax.sharding import PartitionSpec as P
 
@@ -132,6 +134,46 @@
     return lax.cond(jnp.max(rank) < SLOTS, by_slots, by_sums, activations)
 
 
+def add_product(inverse, solved, images):
+    height, width = inverse.shape
+    rows = solved.shape[1]
+    block = width // 4
+
+    def kernel(inverse_ref, solved_ref, images_ref, out_ref, high_ref, low_ref):
+        @pl.when(pl.program_id(0) == 0)
+        def _():
+            high = solved_ref[...].astype(BF16)
+            high_ref[...] = high
+            low_ref[...] = (solved_ref[...] - high.astype(F32)).astype(BF16)
+
+        total = inverse_ref[...]
+        for term in (low_ref, high_ref):
+            total += lax.dot_general(
+                term[...], images_ref[...], (((1,), (1,)), ((), ())), preferred_element_type=F32
+            )
+        out_ref[...] = total
+
+    return pl.pallas_call(
+        kernel,
+        out_shape=jax.ShapeDtypeStruct(inverse.shape, F32),
+        grid=(width // block,),
+        in_specs=[
+            pl.BlockSpec((height, block), lambda i: (0, i)),
+            pl.BlockSpec((height, rows), lambda i: (0, 0)),
+            pl.BlockSpec((block, rows), lambda i: (i, 0)),
+        ],
+        out_specs=pl.BlockSpec((height, block), lambda i: (0, i)),
+        scratch_shapes=[pltpu.VMEM((height, rows), BF16), pltpu.VMEM((height, rows), BF16)],
+        compiler_params=pltpu.CompilerParams(vmem_limit_bytes=61 << 20),
+        cost_estimate=pl.CostEstimate(
+            flops=4 * height * width * rows,
+            bytes_accessed=8 * height * width + 4 * height * rows + 2 * width * rows,
+            transcendentals=0,
+        ),
+        name="add_product",
+    )(inverse, solved, images)
+
+
 def on_device(inverse, activations, forget):
     x, y = lax.axis_index("x"), lax.axis_index("y")
     z, core = lax.axis_index("z"), lax.axis_index("core")
@@ -162,15 +204,25 @@
         lax.dot_general(rows_cols, term, (((0,), (0,)), ((), ())), preferred_element_type=F32)
         for term in (rows_cols, change_cols)
     )
-    share = scatter_sum(fold_cores(share * BETA).astype(BF16), "z", NZ)
+    share = share * BETA
+    side = share.shape[0] // 2
+    beside = share[:side, side:]
+    parts = [
+        jnp.concatenate([share[:side, :side], beside[: side // 2]], axis=0),
+        jnp.concatenate([share[side:, side:], beside[side // 2 :]], axis=0),
+    ]
+    there = jnp.where(core == 0, parts[1], parts[0])
+    share = jnp.where(core == 0, parts[0], parts[1]) + swap(there)
+    share = scatter_sum(share.astype(BF16), "z", NZ)
     share = jnp.sum(gather(share[None], "x", NX), axis=0)
 
     n = share.shape[0]
-    own = (core * NZ + z) * n + lax.broadcasted_iota(jnp.int32, share.shape, 0)
+    own = z * n + lax.broadcasted_iota(jnp.int32, share.shape, 0)
     on_diagonal = own == lax.broadcasted_iota(jnp.int32, share.shape, 1)
     high, low = exact_pair(share)
     low = jnp.sum(jnp.where(on_diagonal, low.astype(F32), 0.0), axis=0, keepdims=True)
-    low = jnp.pad(low, ((0, PAD - 1), (0, 0))).astype(BF16)
+    low = jnp.pad(low, ((0, PAD - 1), (0, side))).astype(BF16)
+    high = jnp.concatenate([high[: n // 2], high[n // 2 :]], axis=1)
     change_there = lax.ppermute(change, AXES, to_rows)
     sent = jnp.concatenate([high, low, change_there], axis=0)
     images = (rows_cols.astype(F32) + change_cols.astype(F32)).astype(BF16)
@@ -182,23 +234,28 @@
     first = core == 0
     halves = [jnp.where(first, mine, other), jnp.where(first, other, mine)]
     halves = [h.reshape(NZ, -1, h.shape[1]).astype(F32) for h in halves]
-    scaled = jnp.concatenate([h[:, :n].reshape(-1, h.shape[2]) for h in halves], axis=0)
-    low = jnp.sum(halves[0][:, n] + halves[1][:, n], axis=0)
-    diagonal = lax.broadcasted_iota(jnp.int32, scaled.shape, 0) == lax.broadcasted_iota(
-        jnp.int32, scaled.shape, 1
-    )
-    scaled = scaled + jnp.where(diagonal, low[None], 0.0)
-    change_here = [h[:, n + PAD :].reshape(-1, h.shape[2]) for h in halves]
+    m = n // 2
+    blocks = [
+        jnp.concatenate([h[:, :m, :side], h[:, :m, side:]], axis=1).reshape(-1, side) for h in halves
+    ]
+    lows = [jnp.sum(h[:, m, :side], axis=0) for h in halves]
+    diagonal = lax.broadcasted_iota(jnp.int32, (side, side), 0) == lax.broadcasted_iota(
+        jnp.int32, (side, side), 1
+    )
+    corners = [b[:side] + jnp.where(diagonal, l[None], 0.0) for b, l in zip(blocks, lows)]
+    beside = jnp.concatenate([b[side:] for b in blocks], axis=0)
+    scaled = jnp.concatenate(
+        [
+            jnp.concatenate([corners[0], beside], axis=1),
+            jnp.concatenate([beside.T, corners[1]], axis=1),
+        ],
+        axis=0,
+    )
+    change_here = [h[:, m + PAD :].reshape(-1, h.shape[2]) for h in halves]
     change_here = jnp.concatenate(change_here, axis=0)
     images_rows = rows_here.astype(F32) + change_here
     solved = solve_rows(images_rows * BETA, scaled)
-    return inverse + lax.dot_general(
-        solved,
-        images_cols.astype(F32),
-        (((1,), (1,)), ((), ())),
-        precision=lax.Precision.HIGH,
-        preferred_element_type=F32,
-    )
+    return add_product(inverse, solved, images_cols)
 
 
 def solution(mesh):

time: 182 us -> 181 us (level)
  Pallas kernels: 0 us -> 5.48 us
  matrix products: 18.8 us -> 14.2 us
  waiting for transfers between devices: 57.9 us -> 55.9 us
    pallas_call x0 -> x1, Pallas kernels: none -> 5.48 us  [add_product(): pl.pallas_call(kernel, out_shape=jax.ShapeDtypeStruct(inverse.shape, F32)...]
    dot_general x1 -> x0, matrix products: 4.53 us -> none  [on_device(): lax.dot_general(solved, images_cols.astype(F32), (((1,), (1,)), ((), ()))...]
where the time goes in v7:
time: 181 us; the launch traced here: 180 us
  starting transfers between devices  56.1 us (31%)
  waiting for transfers between devices  55.9 us (31%)
  blocking collectives  39.1 us (22%)
  matrix products  14.2 us (8%)
  Pallas kernels  5.48 us (3%)
  other arithmetic  4.49 us (2%)
  local copies, waits for them, and re-layouts  3.02 us (2%)
    all_to_all x2, blocking collectives, gather(): lax.all_to_all(jnp.broadcast_to(x[None], (parts,) + x.shape), axis, 0, 0,...  35.7 us
    all_to_all x2, waiting for transfers between devices, spread(): return lax.all_to_all(x, axis, 0, 0, tiled=True)  28.4 us
    all_to_all x2, waiting for transfers between devices, gather(): lax.all_to_all(jnp.broadcast_to(x[None], (parts,) + x.shape), axis, 0, 0,...  20.2 us
    ppermute x3, starting transfers between devices, swap(): return lax.ppermute(x, 'core', [(0, 1), (1, 0)])  20 us
    all_to_all x2, starting transfers between devices, spread(): return lax.all_to_all(x, axis, 0, 0, tiled=True)  16.5 us
    all_to_all x2, starting transfers between devices, gather(): lax.all_to_all(jnp.broadcast_to(x[None], (parts,) + x.shape), axis, 0, 0,...  9.11 us
    dot_general x8, matrix products, dot(): return jnp.dot(a, b, precision=precision, preferred_element_type=F32)  9.08 us
    pallas_call x1, Pallas kernels, add_product(): pl.pallas_call(kernel, out_shape=jax.ShapeDtypeStruct(inverse.shape, F32)...  5.48 us
  transfers between devices with their start and end apart: 10, of which 8 were waited for; matrix products, arithmetic and copies ran while one was open for 6% of the time, Pallas kernels for 0%

profile of v7, /device:TPU:1, one launch (start us, length us, event | category | flops | bytes accessed | tf_op | source)
XLA Modules:
  0.0 179.9 jit_solution(16995387513345778771)
XLA Ops:
  0.0 0.7 add_select_fusion
  0.7 0.2 convert_reduce_fusion
  0.9 0.6 reduce_max.27
  2.2 30.9 %conditional.1 = (bf16[256,512]{1,0:T(8,128)(2,1)S(1)}) conditional(s32[]{:T(128)} %convert_element_type.96, (s32[]{:T(128)}, s32[512]{0:T(512)}, bf16[256,512]{1,0:T(8,128)(2,1)}) %tuple.16, (s32[]{:T(128)}, s32[512]{0:T(512)S(1)}, s32[512]{0:T(512)S(1)}, s32[]{:T(128)}, s32[512]{0:T(512)}, /*index=5*/bf16[256,512]{1,0:T(8,128)(2,1)}, ...), branch_computations={%region_2.4_spmd, %region_4.5_spmd} | conditional | flops 252537344 | bytes 4790458 | solution.py:134
  2.2 0.8 multiply_add_fusion
  3.1 1.4 convolution_convert_fusion.1
  4.5 8.7 %collective-permute-start.1 = (bf16[96,256]{1,0:T(8,128)(2,1)S(1)}, bf16[96,256]{1,0:T(8,128)(2,1)S(1)}, u32[]{:S(2)}, u32[]{:S(2)}) collective-permute-start(bf16[96,256]{1,0:T(8,128)(2,1)S(1)} %constant_dynamic-slice_fusion), channel_id=1, source_target_pairs={{0,1},{1,0},{2,3},{3,2},{4,5},{5,4},{6,7},{7,6},{8,9},{9,8},{10,11... | collective-permute-start | bytes 147464 | tf_op jit(solution)/shard_map/cond/branch_1_fun/ppermute | solution.py:42
  13.2 0.9 collective-permute-done.1
  14.1 18.5 %all_to_all.44 = bf16[8,96,256]{2,1,0:T(8,128)(2,1)S(1)} all-to-all(bf16[8,96,256]{2,1,0:T(8,128)(2,1)S(1)} %broadcast_in_dim.49), channel_id=1, replica_groups=mesh['x'=4,'y'=8,'z'=8,'core'=2] {'z'}, dimensions={0} | all-to-all | bytes 786432 | tf_op jit(solution)/shard_map/cond/branch_1_fun/all_to_all | solution.py:37
  32.6 0.5 fusion.2
  33.1 3.4 %all_gather.3 = bf16[512,512]{1,0:T(8,128)(2,1)S(1)} all-gather(bf16[256,512]{1,0:T(8,128)(2,1)S(1)} %get-tuple-element.146), channel_id=1, replica_groups=mesh['x'=4,'y'=8,'z'=8,'core'=2] {'core'}, dimensions={0}, use_global_device_ids=true | all-gather | bytes 786432 | tf_op jit(solution)/shard_map/all_gather | solution.py:188
  36.6 0.8 fusion.15
  37.4 1.8 %add_convert_fusion = bf16[1024,512]{1,0:T(8,128)(2,1)} fusion(f32[1024,512]{1,0:T(8,128)S(1)} %fusion.15, bf16[512,512]{1,0:T(8,128)(2,1)S(1)} %all_gather.3, f32[512,1024]{1,0:T(8,128)S(1)} %copy-done, s32[1024]{0:T(1024)S(1)} %iota_add_fusion, s32[512]{0:T(512)S(1)} %iota_add_fusion.1), kind=kOutput, calls=%fused_computation.27 | convolution fusion | flops 541065216 | bytes 5773312 | tf_op jit(solution)/shard_map/dot_general | solution.py:194
  39.2 9.7 %all-to-all-start.3 = ((bf16[32,32,512]{2,1,0:T(8,128)(2,1)}), bf16[32,32,512]{2,1,0:T(8,128)(2,1)S(1)}, u32[]{:S(2)}, u32[]{:S(2)}) async-start(bf16[32,32,512]{2,1,0:T(8,128)(2,1)} %bitcast.6), calls=%async_computation.3 | async-start | bytes 2097152 | tf_op jit(solution)/shard_map/all_to_all | solution.py:29
  48.9 3.9 %collective-permute-start.2 = (bf16[32,512]{1,0:T(8,128)(2,1)S(1)}, bf16[32,512]{1,0:T(8,128)(2,1)S(1)}, u32[]{:S(2)}, u32[]{:S(2)}) collective-permute-start(bf16[32,512]{1,0:T(8,128)(2,1)S(1)} %constant_dynamic-slice_fusion.1), channel_id=1, source_target_pairs={{0,0},{1,128},{2,16},{3,144},{4,32},{5,160},{6,48},{7,176},{8,64},... | collective-permute-start | bytes 98312 | tf_op jit(solution)/shard_map/ppermute | solution.py:187
  52.9 21.1 %all-to-all-done.3 = bf16[32,32,512]{2,1,0:T(8,128)(2,1)S(1)} async-done(((bf16[32,32,512]{2,1,0:T(8,128)(2,1)}), bf16[32,32,512]{2,1,0:T(8,128)(2,1)S(1)}, u32[]{:S(2)}, u32[]{:S(2)}) %all-to-all-start.3) | async-done | bytes 1048608 | tf_op jit(solution)/shard_map/all_to_all | solution.py:29
  74.1 1.1 collective-permute-done.2
  75.3 0.8 broadcast_in_dim.67
  76.1 5.7 %all-to-all-start.4 = ((bf16[8,64,512]{2,1,0:T(8,128)(2,1)}), bf16[8,64,512]{2,1,0:T(8,128)(2,1)S(1)}, u32[]{:S(2)}, u32[]{:S(2)}) async-start(bf16[8,64,512]{2,1,0:T(8,128)(2,1)} %broadcast_in_dim.67), calls=%async_computation.4 | async-start | bytes 1048576 | tf_op jit(solution)/shard_map/all_to_all | solution.py:37
  81.9 15.1 %all-to-all-done.4 = bf16[8,64,512]{2,1,0:T(8,128)(2,1)S(1)} async-done(((bf16[8,64,512]{2,1,0:T(8,128)(2,1)}), bf16[8,64,512]{2,1,0:T(8,128)(2,1)S(1)}, u32[]{:S(2)}, u32[]{:S(2)}) %all-to-all-start.4) | async-done | bytes 524320 | tf_op jit(solution)/shard_map/all_to_all | solution.py:37
  97.0 0.3 convolution_bitcast_fusion.1
  97.3 0.3 fusion.13
  97.7 5.3 %collective-permute-start.3 = (f32[384,256]{1,0:T(8,128)S(1)}, f32[384,256]{1,0:T(8,128)S(1)}, u32[]{:S(2)}, u32[]{:S(2)}) collective-permute-start(f32[384,256]{1,0:T(8,128)S(1)} %fusion.32), channel_id=1, source_target_pairs={{0,1},{1,0},{2,3},{3,2},{4,5},{5,4},{6,7},{7,6},{8,9},{9,8},{10,11... | collective-permute-start | bytes 1179656 | tf_op jit(solution)/shard_map/ppermute | solution.py:42
  103.0 1.3 collective-permute-done.3
  104.3 0.7 add_convert_fusion.2
  105.1 6.8 %all-to-all-start.5 = ((bf16[8,48,256]{2,1,0:T(8,128)(2,1)}), bf16[8,48,256]{2,1,0:T(8,128)(2,1)S(1)}, u32[]{:S(2)}, u32[]{:S(2)}) async-start(bf16[8,48,256]{2,1,0:T(8,128)(2,1)} %bitcast.12), calls=%async_computation.5 | async-start | bytes 393216 | tf_op jit(solution)/shard_map/all_to_all | solution.py:29
  111.9 2.1 %collective-permute-start.4 = (bf16[32,512]{1,0:T(8,128)(2,1)S(1)}, bf16[32,512]{1,0:T(8,128)(2,1)S(1)}, u32[]{:S(2)}, u32[]{:S(2)}) collective-permute-start(bf16[32,512]{1,0:T(8,128)(2,1)S(1)} %reduce_sum.97), channel_id=1, source_target_pairs={{0,0},{128,1},{16,2},{144,3},{32,4},{160,5},{48,6},{176,7},{64,8},... | collective-permute-start | bytes 98312 | tf_op jit(solution)/shard_map/ppermute | solution.py:226
  114.0 7.3 %all-to-all-done.5 = bf16[8,48,256]{2,1,0:T(8,128)(2,1)S(1)} async-done(((bf16[8,48,256]{2,1,0:T(8,128)(2,1)}), bf16[8,48,256]{2,1,0:T(8,128)(2,1)S(1)}, u32[]{:S(2)}, u32[]{:S(2)}) %all-to-all-start.5) | async-done | bytes 196640 | tf_op jit(solution)/shard_map/all_to_all | solution.py:29
  121.3 0.7 broadcast_in_dim.88
  122.0 3.4 %all-to-all-start.6 = ((f32[4,1,48,256]{3,2,1,0:T(8,128)}), f32[4,1,48,256]{3,2,1,0:T(8,128)S(1)}, u32[]{:S(2)}, u32[]{:S(2)}) async-start(f32[4,1,48,256]{3,2,1,0:T(8,128)} %broadcast_in_dim.88), calls=%async_computation.6 | async-start | bytes 393216 | tf_op jit(solution)/shard_map/all_to_all | solution.py:37
  125.5 5.1 %all-to-all-done.6 = f32[4,1,48,256]{3,2,1,0:T(8,128)S(1)} async-done(((f32[4,1,48,256]{3,2,1,0:T(8,128)}), f32[4,1,48,256]{3,2,1,0:T(8,128)S(1)}, u32[]{:S(2)}, u32[]{:S(2)}) %all-to-all-start.6) | async-done | bytes 196640 | tf_op jit(solution)/shard_map/all_to_all | solution.py:37
  130.7 1.1 broadcast_in_dim.91
  131.8 17.2 %all_to_all.45 = bf16[8,64,512]{2,1,0:T(8,128)(2,1)S(1)} all-to-all(bf16[8,64,512]{2,1,0:T(8,128)(2,1)S(1)} %broadcast_in_dim.92), channel_id=1, replica_groups=mesh['x'=4,'y'=8,'z'=8,'core'=2] {'z'}, dimensions={0} | all-to-all | bytes 1048576 | tf_op jit(solution)/shard_map/all_to_all | solution.py:37
  149.0 6.0 %collective-permute-start.5 = (bf16[512,512]{1,0:T(8,128)(2,1)S(1)}, bf16[512,512]{1,0:T(8,128)(2,1)S(1)}, u32[]{:S(2)}, u32[]{:S(2)}) collective-permute-start(bf16[512,512]{1,0:T(8,128)(2,1)S(1)} %bitcast.92), channel_id=1, source_target_pairs={{0,1},{1,0},{2,3},{3,2},{4,5},{5,4},{6,7},{7,6},{8,9},{9,8},{10,11... | collective-permute-start | bytes 1572872 | tf_op jit(solution)/shard_map/ppermute | solution.py:42
  155.0 4.4 %all-to-all-start.8 = ((bf16[4,256,512]{2,1,0:T(8,128)(2,1)}), bf16[4,256,512]{2,1,0:T(8,128)(2,1)}, u32[]{:S(2)}, u32[]{:S(2)}) async-start(bf16[4,256,512]{2,1,0:T(8,128)(2,1)} %broadcast_in_dim.91), calls=%async_computation.8 | async-start | bytes 2097152 | tf_op jit(solution)/shard_map/all_to_all | solution.py:232
  159.4 0.2 bitcast_convert_fusion.1
  160.1 1.0 fusion.31
  161.1 1.0 fusion.58
  162.2 1.1 convolution_add_fusion.4
  163.3 1.0 convolution_add_fusion.3
  164.3 1.1 abs_reduce_fusion.1
  165.4 1.0 convolution_add_fusion.2
  166.4 0.6 reduce_max.28
  167.0 1.0 convolution_add_fusion.1
  168.1 0.6 while.14
  168.7 1.8 %convolution_add_fusion.solved_ref = f32[512,512]{1,0:T(8,128)} fusion(f32[512,512]{1,0:T(8,128)S(1)} %get-tuple-element.64, f32[512,512]{1,0:T(8,128)S(1)} %get-tuple-element.65), kind=kOutput, calls=%fused_computation.29 | convolution fusion | flops 537133056 | bytes 3145728 | tf_op jit(solution)/shard_map/dot_general | solution.py:73
  170.5 3.9 %all-to-all-done.8 = bf16[4,256,512]{2,1,0:T(8,128)(2,1)} async-done(((bf16[4,256,512]{2,1,0:T(8,128)(2,1)}), bf16[4,256,512]{2,1,0:T(8,128)(2,1)}, u32[]{:S(2)}, u32[]{:S(2)}) %all-to-all-start.8) | async-done | bytes 1048608 | tf_op jit(solution)/shard_map/all_to_all | solution.py:232
  174.5 5.5 %add_product.1 = f32[512,1024]{1,0:T(8,128)} custom-call(f32[512,1024]{1,0:T(8,128)} %inverse_ref.1, f32[512,512]{1,0:T(8,128)} %convolution_add_fusion.solved_ref, bf16[1024,512]{1,0:T(8,128)(2,1)} %bitcast.24.images_ref), custom_call_target="tpu_custom_call" | custom-call | flops 1073741824 | bytes 6291456 | tf_op jit(solution)/shard_map/add_product/pallas_call | solution.py:156
  (36 shorter events, 1.1 us)
Async XLA Ops:
  2.2 34.4 %copy-start = (f32[512,1024]{1,0:T(8,128)S(1)}, f32[512,1024]{1,0:T(8,128)}, u32[]{:S(2)}) copy-start(f32[512,1024]{1,0:T(8,128)} %inverse_ref.1) | copy-start | bytes 6291460
  4.5 9.6 %collective-permute-start.1 = (bf16[96,256]{1,0:T(8,128)(2,1)S(1)}, bf16[96,256]{1,0:T(8,128)(2,1)S(1)}, u32[]{:S(2)}, u32[]{:S(2)}) collective-permute-start(bf16[96,256]{1,0:T(8,128)(2,1)S(1)} %constant_dynamic-slice_fusion), channel_id=1, source_target_pairs={{0,1},{1,0},{2,3},{3,2},{4,5},{5,4},{6,7},{7,6},{8,9},{9,8},{10,11... | collective-permute-start | bytes 147464 | tf_op jit(solution)/shard_map/cond/branch_1_fun/ppermute | solution.py:42
  39.2 34.8 %all-to-all-start.3 = ((bf16[32,32,512]{2,1,0:T(8,128)(2,1)}), bf16[32,32,512]{2,1,0:T(8,128)(2,1)S(1)}, u32[]{:S(2)}, u32[]{:S(2)}) async-start(bf16[32,32,512]{2,1,0:T(8,128)(2,1)} %bitcast.6), calls=%async_computation.3 | async-start | bytes 2097152 | tf_op jit(solution)/shard_map/all_to_all | solution.py:29
  48.9 26.4 %collective-permute-start.2 = (bf16[32,512]{1,0:T(8,128)(2,1)S(1)}, bf16[32,512]{1,0:T(8,128)(2,1)S(1)}, u32[]{:S(2)}, u32[]{:S(2)}) collective-permute-start(bf16[32,512]{1,0:T(8,128)(2,1)S(1)} %constant_dynamic-slice_fusion.1), channel_id=1, source_target_pairs={{0,0},{1,128},{2,16},{3,144},{4,32},{5,160},{6,48},{7,176},{8,64},... | collective-permute-start | bytes 98312 | tf_op jit(solution)/shard_map/ppermute | solution.py:187
  76.1 20.8 %all-to-all-start.4 = ((bf16[8,64,512]{2,1,0:T(8,128)(2,1)}), bf16[8,64,512]{2,1,0:T(8,128)(2,1)S(1)}, u32[]{:S(2)}, u32[]{:S(2)}) async-start(bf16[8,64,512]{2,1,0:T(8,128)(2,1)} %broadcast_in_dim.67), calls=%async_computation.4 | async-start | bytes 1048576 | tf_op jit(solution)/shard_map/all_to_all | solution.py:37
  97.7 6.6 %collective-permute-start.3 = (f32[384,256]{1,0:T(8,128)S(1)}, f32[384,256]{1,0:T(8,128)S(1)}, u32[]{:S(2)}, u32[]{:S(2)}) collective-permute-start(f32[384,256]{1,0:T(8,128)S(1)} %fusion.32), channel_id=1, source_target_pairs={{0,1},{1,0},{2,3},{3,2},{4,5},{5,4},{6,7},{7,6},{8,9},{9,8},{10,11... | collective-permute-start | bytes 1179656 | tf_op jit(solution)/shard_map/ppermute | solution.py:42
  105.1 16.2 %all-to-all-start.5 = ((bf16[8,48,256]{2,1,0:T(8,128)(2,1)}), bf16[8,48,256]{2,1,0:T(8,128)(2,1)S(1)}, u32[]{:S(2)}, u32[]{:S(2)}) async-start(bf16[8,48,256]{2,1,0:T(8,128)(2,1)} %bitcast.12), calls=%async_computation.5 | async-start | bytes 393216 | tf_op jit(solution)/shard_map/all_to_all | solution.py:29
  111.9 18.8 %collective-permute-start.4 = (bf16[32,512]{1,0:T(8,128)(2,1)S(1)}, bf16[32,512]{1,0:T(8,128)(2,1)S(1)}, u32[]{:S(2)}, u32[]{:S(2)}) collective-permute-start(bf16[32,512]{1,0:T(8,128)(2,1)S(1)} %reduce_sum.97), channel_id=1, source_target_pairs={{0,0},{128,1},{16,2},{144,3},{32,4},{160,5},{48,6},{176,7},{64,8},... | collective-permute-start | bytes 98312 | tf_op jit(solution)/shard_map/ppermute | solution.py:226
  122.0 8.5 %all-to-all-start.6 = ((f32[4,1,48,256]{3,2,1,0:T(8,128)}), f32[4,1,48,256]{3,2,1,0:T(8,128)S(1)}, u32[]{:S(2)}, u32[]{:S(2)}) async-start(f32[4,1,48,256]{3,2,1,0:T(8,128)} %broadcast_in_dim.88), calls=%async_computation.6 | async-start | bytes 393216 | tf_op jit(solution)/shard_map/all_to_all | solution.py:37
  149.0 10.4 %collective-permute-start.5 = (bf16[512,512]{1,0:T(8,128)(2,1)S(1)}, bf16[512,512]{1,0:T(8,128)(2,1)S(1)}, u32[]{:S(2)}, u32[]{:S(2)}) collective-permute-start(bf16[512,512]{1,0:T(8,128)(2,1)S(1)} %bitcast.92), channel_id=1, source_target_pairs={{0,1},{1,0},{2,3},{3,2},{4,5},{5,4},{6,7},{7,6},{8,9},{9,8},{10,11... | collective-permute-start | bytes 1572872 | tf_op jit(solution)/shard_map/ppermute | solution.py:42
  155.0 19.5 %all-to-all-start.8 = ((bf16[4,256,512]{2,1,0:T(8,128)(2,1)}), bf16[4,256,512]{2,1,0:T(8,128)(2,1)}, u32[]{:S(2)}, u32[]{:S(2)}) async-start(bf16[4,256,512]{2,1,0:T(8,128)(2,1)} %broadcast_in_dim.91), calls=%async_computation.8 | async-start | bytes 2097152 | tf_op jit(solution)/shard_map/all_to_all | solution.py:232

commit v8 on v6

--- a/solution.py
+++ b/solution.py
@@ -152,7 +152,8 @@
         lax.dot_general(term, rows_here, (((0,), (0,)), ((), ())), preferred_element_type=F32)
         for term in exact_pair(less_one)
     ).astype(BF16)
-    change = scatter_sum(part, ("x", "y"), NX * NY).astype(BF16)
+    summed = scatter_sum(part, "x", NX).astype(BF16)
+    change = scatter_sum(summed, "y", NY).astype(BF16)
     both = jnp.concatenate([piece_by_columns, change], axis=0)
     both = gather(both, "y", NY).reshape(NY, 2, -1, both.shape[1])
     rows_cols = both[:, 0].reshape(-1, both.shape[3])
@@ -162,15 +163,26 @@
         lax.dot_general(rows_cols, term, (((0,), (0,)), ((), ())), preferred_element_type=F32)
         for term in (rows_cols, change_cols)
     )
-    share = scatter_sum(fold_cores(share * BETA).astype(BF16), "z", NZ)
+
+    share = share * BETA
+    side = share.shape[0] // 2
+    beside = share[:side, side:]
+    parts = [
+        jnp.concatenate([share[:side, :side], beside[: side // 2]], axis=0),
+        jnp.concatenate([share[side:, side:], beside[side // 2 :]], axis=0),
+    ]
+    there = jnp.where(core == 0, parts[1], parts[0])
+    share = jnp.where(core == 0, parts[0], parts[1]) + swap(there)
+    share = scatter_sum(share.astype(BF16), "z", NZ)
     share = jnp.sum(gather(share[None], "x", NX), axis=0)
 
     n = share.shape[0]
-    own = (core * NZ + z) * n + lax.broadcasted_iota(jnp.int32, share.shape, 0)
+    own = z * n + lax.broadcasted_iota(jnp.int32, share.shape, 0)
     on_diagonal = own == lax.broadcasted_iota(jnp.int32, share.shape, 1)
     high, low = exact_pair(share)
     low = jnp.sum(jnp.where(on_diagonal, low.astype(F32), 0.0), axis=0, keepdims=True)
-    low = jnp.pad(low, ((0, PAD - 1), (0, 0))).astype(BF16)
+    low = jnp.pad(low, ((0, PAD - 1), (0, side))).astype(BF16)
+    high = jnp.concatenate([high[: n // 2], high[n // 2 :]], axis=1)
     change_there = lax.ppermute(change, AXES, to_rows)
     sent = jnp.concatenate([high, low, change_there], axis=0)
     images = (rows_cols.astype(F32) + change_cols.astype(F32)).astype(BF16)
@@ -182,13 +194,24 @@
     first = core == 0
     halves = [jnp.where(first, mine, other), jnp.where(first, other, mine)]
     halves = [h.reshape(NZ, -1, h.shape[1]).astype(F32) for h in halves]
-    scaled = jnp.concatenate([h[:, :n].reshape(-1, h.shape[2]) for h in halves], axis=0)
-    low = jnp.sum(halves[0][:, n] + halves[1][:, n], axis=0)
-    diagonal = lax.broadcasted_iota(jnp.int32, scaled.shape, 0) == lax.broadcasted_iota(
-        jnp.int32, scaled.shape, 1
-    )
-    scaled = scaled + jnp.where(diagonal, low[None], 0.0)
-    change_here = [h[:, n + PAD :].reshape(-1, h.shape[2]) for h in halves]
+    m = n // 2
+    blocks = [
+        jnp.concatenate([h[:, :m, :side], h[:, :m, side:]], axis=1).reshape(-1, side) for h in halves
+    ]
+    lows = [jnp.sum(h[:, m, :side], axis=0) for h in halves]
+    diagonal = lax.broadcasted_iota(jnp.int32, (side, side), 0) == lax.broadcasted_iota(
+        jnp.int32, (side, side), 1
+    )
+    corners = [b[:side] + jnp.where(diagonal, l[None], 0.0) for b, l in zip(blocks, lows)]
+    beside = jnp.concatenate([b[side:] for b in blocks], axis=0)
+    scaled = jnp.concatenate(
+        [
+            jnp.concatenate([corners[0], beside], axis=1),
+            jnp.concatenate([beside.T, corners[1]], axis=1),
+        ],
+        axis=0,
+    )
+    change_here = [h[:, m + PAD :].reshape(-1, h.shape[2]) for h in halves]
     change_here = jnp.concatenate(change_here, axis=0)
     images_rows = rows_here.astype(F32) + change_here
     solved = solve_rows(images_rows * BETA, scaled)

time: 182 us -> 179 us (0.984)
  waiting for transfers between devices: 57.9 us -> 37 us
  blocking collectives: 40.2 us -> 56.8 us
  starting transfers between devices: 55.2 us -> 57.8 us
  matrix products: 18.8 us -> 16.8 us
    all_to_all x0 -> x1, blocking collectives: none -> 18 us  [spread(): return lax.all_to_all(x, axis, 0, 0, tiled=True)]
    all_to_all x2, waiting for transfers between devices: 30.1 us -> 12.7 us  [spread(): return lax.all_to_all(x, axis, 0, 0, tiled=True)]
    all_to_all x2, starting transfers between devices: 16.4 us -> 10.2 us  [spread(): return lax.all_to_all(x, axis, 0, 0, tiled=True)]
    all_to_all x2, starting transfers between devices: 9.16 us -> 13.7 us  [gather(): lax.all_to_all(jnp.broadcast_to(x[None], (parts,) + x.shape), axis, 0, 0,...]
    all_to_all x2, waiting for transfers between devices: 20.5 us -> 17.2 us  [gather(): lax.all_to_all(jnp.broadcast_to(x[None], (parts,) + x.shape), axis, 0, 0,...]
    ppermute x3, starting transfers between devices: 19.9 us -> 23 us  [swap(): return lax.ppermute(x, 'core', [(0, 1), (1, 0)])]
  transfers between devices with their start and end apart: 10 -> 10, of which waited for: 8 -> 7; matrix products, arithmetic and copies ran while one was open for 6% -> 6% of each run, Pallas kernels for 0% -> 0%
where the time goes in v8:
time: 179 us; the launch traced here: 178 us
  starting transfers between devices  57.8 us (32%)
  blocking collectives  56.8 us (32%)
  waiting for transfers between devices  37 us (21%)
  matrix products  16.8 us (9%)
  other arithmetic  5.28 us (3%)
  local copies, waits for them, and re-layouts  3.01 us (2%)
    all_to_all x2, blocking collectives, gather(): lax.all_to_all(jnp.broadcast_to(x[None], (parts,) + x.shape), axis, 0, 0,...  35.3 us
    ppermute x3, starting transfers between devices, swap(): return lax.ppermute(x, 'core', [(0, 1), (1, 0)])  23 us
    all_to_all x1, blocking collectives, spread(): return lax.all_to_all(x, axis, 0, 0, tiled=True)  18 us
    all_to_all x2, waiting for transfers between devices, gather(): lax.all_to_all(jnp.broadcast_to(x[None], (parts,) + x.shape), axis, 0, 0,...  17.2 us
    all_to_all x2, starting transfers between devices, gather(): lax.all_to_all(jnp.broadcast_to(x[None], (parts,) + x.shape), axis, 0, 0,...  13.7 us
    all_to_all x2, waiting for transfers between devices, spread(): return lax.all_to_all(x, axis, 0, 0, tiled=True)  12.7 us
    all_to_all x2, starting transfers between devices, spread(): return lax.all_to_all(x, axis, 0, 0, tiled=True)  10.2 us
    dot_general x8, matrix products, dot(): return jnp.dot(a, b, precision=precision, preferred_element_type=F32)  8.05 us
  transfers between devices with their start and end apart: 10, of which 7 were waited for; matrix products, arithmetic and copies ran while one was open for 6% of the time, Pallas kernels for 0%

profile of v8, /device:TPU:1, one launch (start us, length us, event | category | flops | bytes accessed | tf_op | source)
XLA Modules:
  0.0 178.4 jit_solution(656013277614739268)
XLA Ops:
  0.0 0.7 add_select_fusion
  0.7 0.2 convert_reduce_fusion
  0.9 0.6 reduce_max.27
  2.2 30.9 %conditional.1 = (bf16[256,512]{1,0:T(8,128)(2,1)S(1)}) conditional(s32[]{:T(128)} %convert_element_type.99, (s32[]{:T(128)}, s32[512]{0:T(512)}, bf16[256,512]{1,0:T(8,128)(2,1)}) %tuple.16, (s32[]{:T(128)}, s32[512]{0:T(512)S(1)}, s32[512]{0:T(512)S(1)}, s32[]{:T(128)}, s32[512]{0:T(512)}, /*index=5*/bf16[256,512]{1,0:T(8,128)(2,1)}, ...), branch_computations={%region_2.4_spmd, %region_4.5_spmd} | conditional | flops 252537344 | bytes 4790458 | solution.py:132
  2.2 0.8 multiply_add_fusion
  3.1 1.4 convolution_convert_fusion.1
  4.5 8.7 %collective-permute-start.1 = (bf16[96,256]{1,0:T(8,128)(2,1)S(1)}, bf16[96,256]{1,0:T(8,128)(2,1)S(1)}, u32[]{:S(2)}, u32[]{:S(2)}) collective-permute-start(bf16[96,256]{1,0:T(8,128)(2,1)S(1)} %constant_dynamic-slice_fusion), channel_id=1, source_target_pairs={{0,1},{1,0},{2,3},{3,2},{4,5},{5,4},{6,7},{7,6},{8,9},{9,8},{10,11... | collective-permute-start | bytes 147464 | tf_op jit(solution)/shard_map/cond/branch_1_fun/ppermute | solution.py:40
  13.2 0.9 collective-permute-done.1
  14.1 18.5 %all_to_all.49 = bf16[8,96,256]{2,1,0:T(8,128)(2,1)S(1)} all-to-all(bf16[8,96,256]{2,1,0:T(8,128)(2,1)S(1)} %broadcast_in_dim.49), channel_id=1, replica_groups=mesh['x'=4,'y'=8,'z'=8,'core'=2] {'z'}, dimensions={0} | all-to-all | bytes 786432 | tf_op jit(solution)/shard_map/cond/branch_1_fun/all_to_all | solution.py:35
  32.6 0.5 fusion.2
  33.1 3.4 %all_gather.3 = bf16[512,512]{1,0:T(8,128)(2,1)S(1)} all-gather(bf16[256,512]{1,0:T(8,128)(2,1)S(1)} %get-tuple-element.146), channel_id=1, replica_groups=mesh['x'=4,'y'=8,'z'=8,'core'=2] {'core'}, dimensions={0}, use_global_device_ids=true | all-gather | bytes 786432 | tf_op jit(solution)/shard_map/all_gather | solution.py:146
  36.6 0.8 fusion.15
  37.4 0.8 add_convert_fusion
  38.2 18.0 %all_to_all.50 = bf16[4,256,512]{2,1,0:T(8,128)(2,1)S(1)} all-to-all(bf16[4,256,512]{2,1,0:T(8,128)(2,1)S(1)} %bitcast.102), channel_id=1, replica_groups=mesh['x'=4,'y'=8,'z'=8,'core'=2] {'x'}, dimensions={0} | all-to-all | bytes 2097152 | tf_op jit(solution)/shard_map/all_to_all | solution.py:27
  56.3 0.9 reduce_sum.109
  57.2 6.9 %all-to-all-start.4 = ((bf16[8,32,512]{2,1,0:T(8,128)(2,1)}), bf16[8,32,512]{2,1,0:T(8,128)(2,1)S(1)}, u32[]{:S(2)}, u32[]{:S(2)}) async-start(bf16[8,32,512]{2,1,0:T(8,128)(2,1)} %bitcast.7), calls=%async_computation.4 | async-start | bytes 524288 | tf_op jit(solution)/shard_map/all_to_all | solution.py:27
  64.1 4.1 %collective-permute-start.2 = (bf16[32,512]{1,0:T(8,128)(2,1)S(1)}, bf16[32,512]{1,0:T(8,128)(2,1)S(1)}, u32[]{:S(2)}, u32[]{:S(2)}) collective-permute-start(bf16[32,512]{1,0:T(8,128)(2,1)S(1)} %constant_dynamic-slice_fusion.1), channel_id=1, source_target_pairs={{0,0},{1,128},{2,16},{3,144},{4,32},{5,160},{6,48},{7,176},{8,64},... | collective-permute-start | bytes 98312 | tf_op jit(solution)/shard_map/ppermute | solution.py:145
  68.2 5.0 %all-to-all-done.4 = bf16[8,32,512]{2,1,0:T(8,128)(2,1)S(1)} async-done(((bf16[8,32,512]{2,1,0:T(8,128)(2,1)}), bf16[8,32,512]{2,1,0:T(8,128)(2,1)S(1)}, u32[]{:S(2)}, u32[]{:S(2)}) %all-to-all-start.4) | async-done | bytes 262176 | tf_op jit(solution)/shard_map/all_to_all | solution.py:27
  73.3 0.8 broadcast_in_dim.67
  74.1 9.5 %all-to-all-start.5 = ((bf16[8,64,512]{2,1,0:T(8,128)(2,1)}), bf16[8,64,512]{2,1,0:T(8,128)(2,1)S(1)}, u32[]{:S(2)}, u32[]{:S(2)}) async-start(bf16[8,64,512]{2,1,0:T(8,128)(2,1)} %broadcast_in_dim.67), calls=%async_computation.5 | async-start | bytes 1048576 | tf_op jit(solution)/shard_map/all_to_all | solution.py:35
  83.7 12.1 %all-to-all-done.5 = bf16[8,64,512]{2,1,0:T(8,128)(2,1)S(1)} async-done(((bf16[8,64,512]{2,1,0:T(8,128)(2,1)}), bf16[8,64,512]{2,1,0:T(8,128)(2,1)S(1)}, u32[]{:S(2)}, u32[]{:S(2)}) %all-to-all-start.5) | async-done | bytes 524320 | tf_op jit(solution)/shard_map/all_to_all | solution.py:35
  95.8 0.3 convolution_bitcast_fusion.1
  96.1 0.3 fusion.13
  96.5 8.3 %collective-permute-start.3 = (f32[384,256]{1,0:T(8,128)S(1)}, f32[384,256]{1,0:T(8,128)S(1)}, u32[]{:S(2)}, u32[]{:S(2)}) collective-permute-start(f32[384,256]{1,0:T(8,128)S(1)} %fusion.32), channel_id=1, source_target_pairs={{0,1},{1,0},{2,3},{3,2},{4,5},{5,4},{6,7},{7,6},{8,9},{9,8},{10,11... | collective-permute-start | bytes 1179656 | tf_op jit(solution)/shard_map/ppermute | solution.py:40
  104.9 1.3 collective-permute-done.3
  106.2 0.7 add_convert_fusion.2
  106.9 3.4 %all-to-all-start.6 = ((bf16[8,48,256]{2,1,0:T(8,128)(2,1)}), bf16[8,48,256]{2,1,0:T(8,128)(2,1)S(1)}, u32[]{:S(2)}, u32[]{:S(2)}) async-start(bf16[8,48,256]{2,1,0:T(8,128)(2,1)} %bitcast.13), calls=%async_computation.6 | async-start | bytes 393216 | tf_op jit(solution)/shard_map/all_to_all | solution.py:27
  110.4 2.3 %collective-permute-start.4 = (bf16[32,512]{1,0:T(8,128)(2,1)S(1)}, bf16[32,512]{1,0:T(8,128)(2,1)S(1)}, u32[]{:S(2)}, u32[]{:S(2)}) collective-permute-start(bf16[32,512]{1,0:T(8,128)(2,1)S(1)} %reduce_sum.110), channel_id=1, source_target_pairs={{0,0},{128,1},{16,2},{144,3},{32,4},{160,5},{48,6},{176,7},{64,8},... | collective-permute-start | bytes 98312 | tf_op jit(solution)/shard_map/ppermute | solution.py:186
  112.6 7.7 %all-to-all-done.6 = bf16[8,48,256]{2,1,0:T(8,128)(2,1)S(1)} async-done(((bf16[8,48,256]{2,1,0:T(8,128)(2,1)}), bf16[8,48,256]{2,1,0:T(8,128)(2,1)S(1)}, u32[]{:S(2)}, u32[]{:S(2)}) %all-to-all-start.6) | async-done | bytes 196640 | tf_op jit(solution)/shard_map/all_to_all | solution.py:27
  120.3 0.7 broadcast_in_dim.88
  121.0 4.1 %all-to-all-start.7 = ((f32[4,1,48,256]{3,2,1,0:T(8,128)}), f32[4,1,48,256]{3,2,1,0:T(8,128)S(1)}, u32[]{:S(2)}, u32[]{:S(2)}) async-start(f32[4,1,48,256]{3,2,1,0:T(8,128)} %broadcast_in_dim.88), calls=%async_computation.7 | async-start | bytes 393216 | tf_op jit(solution)/shard_map/all_to_all | solution.py:35
  125.2 5.1 %all-to-all-done.7 = f32[4,1,48,256]{3,2,1,0:T(8,128)S(1)} async-done(((f32[4,1,48,256]{3,2,1,0:T(8,128)}), f32[4,1,48,256]{3,2,1,0:T(8,128)S(1)}, u32[]{:S(2)}, u32[]{:S(2)}) %all-to-all-start.7) | async-done | bytes 196640 | tf_op jit(solution)/shard_map/all_to_all | solution.py:35
  130.5 1.1 broadcast_in_dim.91
  131.6 16.8 %all_to_all.51 = bf16[8,64,512]{2,1,0:T(8,128)(2,1)S(1)} all-to-all(bf16[8,64,512]{2,1,0:T(8,128)(2,1)S(1)} %broadcast_in_dim.92), channel_id=1, replica_groups=mesh['x'=4,'y'=8,'z'=8,'core'=2] {'z'}, dimensions={0} | all-to-all | bytes 1048576 | tf_op jit(solution)/shard_map/all_to_all | solution.py:35
  148.4 6.0 %collective-permute-start.5 = (bf16[512,512]{1,0:T(8,128)(2,1)S(1)}, bf16[512,512]{1,0:T(8,128)(2,1)S(1)}, u32[]{:S(2)}, u32[]{:S(2)}) collective-permute-start(bf16[512,512]{1,0:T(8,128)(2,1)S(1)} %bitcast.95), channel_id=1, source_target_pairs={{0,1},{1,0},{2,3},{3,2},{4,5},{5,4},{6,7},{7,6},{8,9},{9,8},{10,11... | collective-permute-start | bytes 1572872 | tf_op jit(solution)/shard_map/ppermute | solution.py:40
  154.3 4.4 %all-to-all-start.9 = ((bf16[4,256,512]{2,1,0:T(8,128)(2,1)}), bf16[4,256,512]{2,1,0:T(8,128)(2,1)}, u32[]{:S(2)}, u32[]{:S(2)}) async-start(bf16[4,256,512]{2,1,0:T(8,128)(2,1)} %broadcast_in_dim.91), calls=%async_computation.9 | async-start | bytes 2097152 | tf_op jit(solution)/shard_map/all_to_all | solution.py:192
  159.5 1.0 fusion.31
  160.5 1.0 fusion.58
  161.6 1.1 convolution_add_fusion.5
  162.6 1.0 convolution_add_fusion.4
  163.7 1.1 abs_reduce_fusion.1
  164.7 1.0 convolution_add_fusion.3
  165.8 0.6 reduce_max.28
  166.4 1.0 convolution_add_fusion.2
  167.4 0.6 while.14
  168.1 0.8 convolution_add_fusion.1
  168.9 5.0 %all-to-all-done.9 = bf16[4,256,512]{2,1,0:T(8,128)(2,1)} async-done(((bf16[4,256,512]{2,1,0:T(8,128)(2,1)}), bf16[4,256,512]{2,1,0:T(8,128)(2,1)}, u32[]{:S(2)}, u32[]{:S(2)}) %all-to-all-start.9) | async-done | bytes 1048608 | tf_op jit(solution)/shard_map/all_to_all | solution.py:192
  173.8 4.5 %convolution_add_fusion = f32[512,1024]{1,0:T(8,128)} fusion(f32[512,1024]{1,0:T(8,128)} %param.7, f32[512,512]{1,0:T(8,128)S(1)} %convolution_add_fusion.1, bf16[1024,512]{1,0:T(8,128)(2,1)} %bitcast.25), kind=kOutput, calls=%fused_computation.29 | convolution fusion | flops 1611137024 | bytes 6291456 | tf_op jit(solution)/shard_map/dot_general | solution.py:218
  (38 shorter events, 1.1 us)
Async XLA Ops:
  2.2 34.4 %copy-start = (f32[512,1024]{1,0:T(8,128)S(1)}, f32[512,1024]{1,0:T(8,128)}, u32[]{:S(2)}) copy-start(f32[512,1024]{1,0:T(8,128)} %param.7) | copy-start | bytes 6291460
  4.5 9.6 %collective-permute-start.1 = (bf16[96,256]{1,0:T(8,128)(2,1)S(1)}, bf16[96,256]{1,0:T(8,128)(2,1)S(1)}, u32[]{:S(2)}, u32[]{:S(2)}) collective-permute-start(bf16[96,256]{1,0:T(8,128)(2,1)S(1)} %constant_dynamic-slice_fusion), channel_id=1, source_target_pairs={{0,1},{1,0},{2,3},{3,2},{4,5},{5,4},{6,7},{7,6},{8,9},{9,8},{10,11... | collective-permute-start | bytes 147464 | tf_op jit(solution)/shard_map/cond/branch_1_fun/ppermute | solution.py:40
  57.2 16.0 %all-to-all-start.4 = ((bf16[8,32,512]{2,1,0:T(8,128)(2,1)}), bf16[8,32,512]{2,1,0:T(8,128)(2,1)S(1)}, u32[]{:S(2)}, u32[]{:S(2)}) async-start(bf16[8,32,512]{2,1,0:T(8,128)(2,1)} %bitcast.7), calls=%async_computation.4 | async-start | bytes 524288 | tf_op jit(solution)/shard_map/all_to_all | solution.py:27
  64.1 9.2 %collective-permute-start.2 = (bf16[32,512]{1,0:T(8,128)(2,1)S(1)}, bf16[32,512]{1,0:T(8,128)(2,1)S(1)}, u32[]{:S(2)}, u32[]{:S(2)}) collective-permute-start(bf16[32,512]{1,0:T(8,128)(2,1)S(1)} %constant_dynamic-slice_fusion.1), channel_id=1, source_target_pairs={{0,0},{1,128},{2,16},{3,144},{4,32},{5,160},{6,48},{7,176},{8,64},... | collective-permute-start | bytes 98312 | tf_op jit(solution)/shard_map/ppermute | solution.py:145
  74.1 21.6 %all-to-all-start.5 = ((bf16[8,64,512]{2,1,0:T(8,128)(2,1)}), bf16[8,64,512]{2,1,0:T(8,128)(2,1)S(1)}, u32[]{:S(2)}, u32[]{:S(2)}) async-start(bf16[8,64,512]{2,1,0:T(8,128)(2,1)} %broadcast_in_dim.67), calls=%async_computation.5 | async-start | bytes 1048576 | tf_op jit(solution)/shard_map/all_to_all | solution.py:35
  96.5 9.7 %collective-permute-start.3 = (f32[384,256]{1,0:T(8,128)S(1)}, f32[384,256]{1,0:T(8,128)S(1)}, u32[]{:S(2)}, u32[]{:S(2)}) collective-permute-start(f32[384,256]{1,0:T(8,128)S(1)} %fusion.32), channel_id=1, source_target_pairs={{0,1},{1,0},{2,3},{3,2},{4,5},{5,4},{6,7},{7,6},{8,9},{9,8},{10,11... | collective-permute-start | bytes 1179656 | tf_op jit(solution)/shard_map/ppermute | solution.py:40
  106.9 13.3 %all-to-all-start.6 = ((bf16[8,48,256]{2,1,0:T(8,128)(2,1)}), bf16[8,48,256]{2,1,0:T(8,128)(2,1)S(1)}, u32[]{:S(2)}, u32[]{:S(2)}) async-start(bf16[8,48,256]{2,1,0:T(8,128)(2,1)} %bitcast.13), calls=%async_computation.6 | async-start | bytes 393216 | tf_op jit(solution)/shard_map/all_to_all | solution.py:27
  110.4 20.1 %collective-permute-start.4 = (bf16[32,512]{1,0:T(8,128)(2,1)S(1)}, bf16[32,512]{1,0:T(8,128)(2,1)S(1)}, u32[]{:S(2)}, u32[]{:S(2)}) collective-permute-start(bf16[32,512]{1,0:T(8,128)(2,1)S(1)} %reduce_sum.110), channel_id=1, source_target_pairs={{0,0},{128,1},{16,2},{144,3},{32,4},{160,5},{48,6},{176,7},{64,8},... | collective-permute-start | bytes 98312 | tf_op jit(solution)/shard_map/ppermute | solution.py:186
  121.0 9.3 %all-to-all-start.7 = ((f32[4,1,48,256]{3,2,1,0:T(8,128)}), f32[4,1,48,256]{3,2,1,0:T(8,128)S(1)}, u32[]{:S(2)}, u32[]{:S(2)}) async-start(f32[4,1,48,256]{3,2,1,0:T(8,128)} %broadcast_in_dim.88), calls=%async_computation.7 | async-start | bytes 393216 | tf_op jit(solution)/shard_map/all_to_all | solution.py:35
  148.4 10.4 %collective-permute-start.5 = (bf16[512,512]{1,0:T(8,128)(2,1)S(1)}, bf16[512,512]{1,0:T(8,128)(2,1)S(1)}, u32[]{:S(2)}, u32[]{:S(2)}) collective-permute-start(bf16[512,512]{1,0:T(8,128)(2,1)S(1)} %bitcast.95), channel_id=1, source_target_pairs={{0,1},{1,0},{2,3},{3,2},{4,5},{5,4},{6,7},{7,6},{8,9},{9,8},{10,11... | collective-permute-start | bytes 1572872 | tf_op jit(solution)/shard_map/ppermute | solution.py:40
  154.3 19.5 %all-to-all-start.9 = ((bf16[4,256,512]{2,1,0:T(8,128)(2,1)}), bf16[4,256,512]{2,1,0:T(8,128)(2,1)}, u32[]{:S(2)}, u32[]{:S(2)}) async-start(bf16[4,256,512]{2,1,0:T(8,128)(2,1)} %broadcast_in_dim.91), calls=%async_computation.9 | async-start | bytes 2097152 | tf_op jit(solution)/shard_map/all_to_all | solution.py:192
